TPU v7x, 32 devices: a whole 2x2x4 slice. The times are simulated.
32 devices in a mesh: stn: 4 (over y, x), freq: 8 (over z, core).
Axes of the slice: x: 2, y: 2, z: 4, core: 2. Of those that a mesh axis runs over, the one named last changes fastest.
Arguments:
- voltages: bfloat16 [512, 2, 8, 2, 5376], P(('stn', 'freq')), may hold values from -6 to 6
- filter_taps: float32 [12, 256], replicated, may hold values from -1.75 to 1.75
- beam_weights: bfloat16 [8, 2, 512, 1024], P('freq', None, 'stn'), may hold values from -0.25 to 0.25
- station_map: int32 [512], P('stn'), may hold values from 0 to 511, each once
- active_counts: int32 [8], P('freq'), may hold values from 256 to 512
Outputs:
- beams: bfloat16 [1024, 2, 8, 5120], P('stn', None, 'freq')
Inputs may be any that keep to these rules, and one draw needn't show every extreme that they name: `station_map`: each station id appears in exactly one slot. `active_counts`: stations whose id is below the entry are active in that coarse channel.
All inputs are finite; a program needn't handle non-finite values.
Results may differ from a plain program's by a relative error of at most 0.0062.
Values may be sent and summed in bfloat16 or wider, within the bound.
No kernel may reach another device: no remote copies, remote signals or barrier semaphores. Data moves between devices by JAX's collectives and lax.ppermute only.
A program may use at most 192 MiB of HBM per device.

v0:
```python
import functools

import jax
import jax.numpy as jnp
import numpy as np
from jax import lax
from jax.experimental import pallas as pl
from jax.experimental.layout import Layout, with_layout_constraint
from jax.experimental.pallas import tpu as pltpu
from jax.sharding import PartitionSpec as P


LANES = 128


def dft_table(fine):
    index = jnp.arange(fine, dtype=jnp.int32)
    phase = index[:, None] * index[None, :] % fine
    angle = phase.astype(jnp.float32) * (2.0 * jnp.pi / fine)
    factor = fine ** (-0.5)
    cosine = jnp.cos(angle) * factor
    sine = jnp.sin(angle) * factor
    upper = jnp.concatenate([cosine, -sine], axis=1)
    lower = jnp.concatenate([sine, cosine], axis=1)
    return jnp.concatenate([upper, lower], axis=0).astype(jnp.bfloat16)


def build_weights(masked):
    real_part = masked[:, 0]
    imag_part = masked[:, 1]
    real_row = jnp.concatenate([real_part, -imag_part], axis=1)
    imag_row = jnp.concatenate([imag_part, real_part], axis=1)
    return jnp.stack([real_row, imag_row], axis=2)


def plain(voltages, filter_taps, beam_weights, station_map, active_counts):
    slots, polars, chans, _, samples = voltages.shape
    taps, fine = filter_taps.shape
    blocks = samples // fine
    frames_out = blocks - taps + 1
    frames = voltages.reshape(slots, polars, chans, 2, blocks, fine)
    polyphase = jnp.zeros((slots, polars, chans, 2, frames_out, fine), jnp.float32)
    for tap in range(taps):
        polyphase = polyphase + filter_taps[tap] * frames[
            :, :, :, :, tap : tap + frames_out, :
        ].astype(jnp.float32)
    polyphase = polyphase.astype(jnp.bfloat16)
    inputs = polyphase.transpose(0, 1, 2, 4, 3, 5).reshape(
        slots * polars * chans * frames_out, 2 * fine
    )
    spectra = jnp.dot(inputs, dft_table(fine), preferred_element_type=jnp.float32).astype(
        jnp.bfloat16
    )
    spectra = spectra.reshape(slots, polars, chans, frames_out, 2, fine)
    arranged = spectra.transpose(2, 4, 0, 1, 3, 5).reshape(
        chans, 2, slots, polars * frames_out * fine
    )
    turned = lax.all_to_all(arranged, "freq", split_axis=0, concat_axis=2, tiled=True)
    own_chans, _, _, row_count = turned.shape
    mask = (station_map[None, :] < active_counts[:, None]).astype(jnp.bfloat16)
    masked = beam_weights * mask[:, None, :, None]
    all_weights = lax.all_to_all(masked, "stn", split_axis=3, concat_axis=2, tiled=True)
    piece = lax.all_gather(turned, "stn", axis=2, tiled=True)
    width = piece.shape[2]
    wbig = build_weights(all_weights)
    data = piece.reshape(own_chans, 2 * width, row_count)
    summed = jnp.einsum("ckob,ckr->bocr", wbig, data, preferred_element_type=jnp.float32)
    return summed.astype(jnp.bfloat16)


def cos_sin(fine):
    index = np.arange(fine)
    angle = 2.0 * np.pi * ((index[:, None] * index[None, :]) % fine) / fine
    both = np.concatenate([np.cos(angle), np.sin(angle)], axis=1) * fine ** (-0.5)
    return jnp.asarray(both.astype(np.float32)).astype(jnp.bfloat16)


def spectra_body(dims, info, volt, taps_ref, table, *refs):
    slots, taps, frames_out, per_pair, pitch, split = dims
    outs, wide, rows = refs[:-2], refs[-2], refs[-1]
    blocks = frames_out + taps - 1
    core = info[1]
    fine = 2 * LANES
    for s in range(slots):
        wide[pl.ds(s * pitch, per_pair), :] = volt[s, 0, 0].astype(jnp.float32)
    for turn in range(2):
        base = jnp.bitwise_xor(core, turn) * (per_pair // 2)
        for q in range(2):
            for half in range(2):
                lane = half * LANES
                coef = [taps_ref[t : t + 1, lane : lane + LANES] for t in range(taps)]
                data = [
                    wide[pl.ds(base + 2 * (2 * i + half) + q, slots, stride=pitch), :]
                    for i in range(blocks)
                ]
                for m in range(frames_out):
                    total = coef[0] * data[m]
                    for t in range(1, taps):
                        total = total + coef[t] * data[m + t]
                    col = q * fine + lane
                    rows[m * slots : (m + 1) * slots, col : col + LANES] = total.astype(
                        jnp.bfloat16
                    )
        first = jnp.dot(rows[:, :fine], table[...], preferred_element_type=jnp.float32)
        second = jnp.dot(rows[:, fine:], table[...], preferred_element_type=jnp.float32)
        real = (first[:, :fine] + second[:, fine:]).astype(jnp.bfloat16)
        imag = (second[:, :fine] - first[:, fine:]).astype(jnp.bfloat16)

        def put(out):
            for m in range(frames_out):
                span = slice(m * fine, (m + 1) * fine)
                out[0, :, span] = real[m * slots : (m + 1) * slots]
                out[1, :, span] = imag[m * slots : (m + 1) * slots]

        if not split:
            put(outs[turn])
        else:
            for p in range(len(outs) // 2):
                pl.when(pl.program_id(0) == p)(functools.partial(put, outs[2 * p + turn]))


def spectra_pair(info, view, filter_taps, table, split):
    slots, polars, _, per_pair, _ = view.shape
    taps, fine = filter_taps.shape
    frames_out = per_pair // 8 - taps + 1
    width = frames_out * fine
    pitch = per_pair + 1
    if split:
        shapes = [jax.ShapeDtypeStruct((2, slots, width), jnp.bfloat16)] * (2 * polars)
        out_specs = [pl.BlockSpec((2, slots, width), lambda p, info: (0, 0, 0))] * len(shapes)
    else:
        shapes = [jax.ShapeDtypeStruct((2, slots, polars * width), jnp.bfloat16)] * 2
        out_specs = [pl.BlockSpec((2, slots, width), lambda p, info: (0, 0, p))] * 2
    return pl.pallas_call(
        functools.partial(
            spectra_body, (slots, taps, frames_out, per_pair, pitch, split)
        ),
        grid_spec=pltpu.PrefetchScalarGridSpec(
            num_scalar_prefetch=1,
            grid=(polars,),
            in_specs=[
                pl.BlockSpec(
                    (slots, 1, 1, per_pair, LANES), lambda p, info: (0, p, info[0], 0, 0)
                ),
                pl.BlockSpec((taps, fine), lambda p, info: (0, 0)),
                pl.BlockSpec((fine, 2 * fine), lambda p, info: (0, 0)),
            ],
            out_specs=out_specs,
            scratch_shapes=[
                pltpu.VMEM((slots * pitch, LANES), jnp.float32),
                pltpu.VMEM((frames_out * slots, 2 * fine), jnp.bfloat16),
            ],
        ),
        out_shape=shapes,
        compiler_params=pltpu.CompilerParams(dimension_semantics=("arbitrary",)),
        cost_estimate=pl.CostEstimate(
            flops=8 * 10**8, bytes_accessed=4 * 10**6, transcendentals=0
        ),
        name="spectra",
    )(info, view, filter_taps, table)


def mask_body(info, ids, count, weights, *outs):
    slots = weights.shape[2]
    width = outs[0].shape[3]
    place = jnp.bitwise_xor(pl.program_id(0), info[1]) * slots
    row = lax.broadcasted_iota(jnp.int32, (slots, LANES), 0)
    mine = jnp.zeros((slots, LANES), jnp.int32)
    for s in range(slots):
        mine = jnp.where(row == s, ids[place + s], mine)
    live = (mine < count[0]).astype(jnp.float32)[:, :1]
    for d, out in enumerate(outs):
        start = pl.multiple_of(jnp.bitwise_xor(info[0], d) * width, width)
        for q in range(2):
            value = weights[q, 0, :, pl.ds(start, width)].astype(jnp.float32)
            out[q, 0] = (value * live).astype(jnp.bfloat16)


def mask_weights(info, ids, count, weights, stn):
    _, freq, slots, beams = weights.shape
    width = beams // stn
    shape = jax.ShapeDtypeStruct((2, freq, slots, width), jnp.bfloat16)
    return pl.pallas_call(
        mask_body,
        grid_spec=pltpu.PrefetchScalarGridSpec(
            num_scalar_prefetch=3,
            grid=(freq,),
            in_specs=[
                pl.BlockSpec(
                    (2, 1, slots, beams),
                    lambda j, info, ids, count: (0, jnp.bitwise_xor(j, info[1]), 0, 0),
                )
            ],
            out_specs=[
                pl.BlockSpec((2, 1, slots, width), lambda j, info, ids, count: (0, j, 0, 0))
            ]
            * stn,
        ),
        out_shape=[shape] * stn,
        compiler_params=pltpu.CompilerParams(dimension_semantics=("arbitrary",)),
        name="mask",
    )(info, ids, count, weights)


def turn_body(*refs):
    parts, out = refs[:-1], refs[-1]
    rows = parts[0].shape[1]
    for g, part in enumerate(parts):
        real = part[0].astype(jnp.float32).T
        imag = part[1].astype(jnp.float32).T
        lead = slice(2 * g * rows, (2 * g + 1) * rows)
        tail = slice((2 * g + 1) * rows, (2 * g + 2) * rows)
        out[0, :, lead] = real.astype(jnp.bfloat16)
        out[0, :, tail] = (-imag).astype(jnp.bfloat16)
        out[1, :, lead] = imag.astype(jnp.bfloat16)
        out[1, :, tail] = real.astype(jnp.bfloat16)


def turn_weights(parts):
    _, rows, width = parts[0].shape
    return pl.pallas_call(
        turn_body,
        out_shape=jax.ShapeDtypeStruct((2, width, 2 * len(parts) * rows), jnp.bfloat16),
        name="turn",
    )(*parts)


def beam_body(places, tile, pitch, aliased, weights, *refs):
    count = len(places)
    pieces = refs[:count]
    out, data, wide = refs[count + aliased :]
    slots = pieces[0].shape[1]
    span = data.shape[0] // (2 * (max(g for g, _ in places) + 1))
    for (g, j), piece in zip(places, pieces):
        for q in range(2):
            row = (2 * g + q) * span + j * slots
            data[row : row + slots, :] = piece[q]
    beams = weights.shape[1]
    for q in range(2):
        part = jnp.dot(weights[q], data[...], preferred_element_type=jnp.float32)
        for j in range(tile // LANES):
            wide[pl.ds(2 * j + q, beams, stride=pitch), :] = part[
                :, j * LANES : (j + 1) * LANES
            ]
    high = 2 * tile // LANES
    for b in range(beams):
        out[b] = wide[pl.ds(b * pitch, high), :].astype(jnp.bfloat16)


def beam_sum(weights, pieces, total, first, steps, tile, before):
    _, beams, depth = weights.shape
    slots = pieces[0][2].shape[1]
    high = 2 * tile // LANES
    pitch = high + 1
    specs = [pl.BlockSpec((2, beams, depth), lambda n: (0, 0, 0))]
    for _, _, piece in pieces:
        shift = first if piece.shape[2] == total else 0
        specs.append(
            pl.BlockSpec((2, slots, tile), functools.partial(lambda d, n: (0, 0, n + d), shift))
        )
    extra = [] if before is None else [before]
    specs += [pl.BlockSpec(memory_space=pl.ANY)] * len(extra)
    return pl.pallas_call(
        functools.partial(
            beam_body, [(g, j) for g, j, _ in pieces], tile, pitch, len(extra)
        ),
        grid=(steps,),
        in_specs=specs,
        out_specs=pl.BlockSpec((beams, high, LANES), lambda n: (0, n + first, 0)),
        out_shape=jax.ShapeDtypeStruct((beams, 2 * total // LANES, LANES), jnp.bfloat16),
        input_output_aliases={len(pieces) + 1: 0} if extra else {},
        scratch_shapes=[
            pltpu.VMEM((depth, tile), jnp.bfloat16),
            pltpu.VMEM((beams * pitch, LANES), jnp.float32),
        ],
        compiler_params=pltpu.CompilerParams(dimension_semantics=("arbitrary",)),
        cost_estimate=pl.CostEstimate(
            flops=4 * beams * depth * tile * steps,
            bytes_accessed=2 * (depth + 2 * beams) * tile * steps,
            transcendentals=0,
        ),
        name="beams",
    )(weights, *[piece for _, _, piece in pieces], *extra)


def swap(array, axis, step, size):
    return lax.ppermute(array, axis, [(i, i ^ step) for i in range(size)])


def fast(stn, freq, voltages, filter_taps, beam_weights, station_map, active_counts):
    slots, polars, chans, _, samples = voltages.shape
    taps, fine = filter_taps.shape
    s_me = lax.axis_index("stn")
    f_me = lax.axis_index("freq")

    info = jnp.stack([s_me, f_me]).astype(jnp.int32)
    grouped = beam_weights[0].reshape(2, freq, slots, beam_weights.shape[3])
    wparts = mask_weights(info, station_map, active_counts, grouped, stn)
    wparts = [wparts[0]] + [swap(wparts[d], "stn", d, stn) for d in range(1, stn)]
    weights = turn_weights([w.reshape(2, freq * slots, -1) for w in wparts])

    view = with_layout_constraint(
        voltages.reshape(slots, polars, chans, 2, samples // LANES, LANES),
        Layout((0, 1, 2, 4, 3, 5)),
    )
    view = view.transpose(0, 1, 2, 4, 3, 5).reshape(
        slots, polars, chans // 2, 4 * samples // LANES, LANES
    )
    table = cos_sin(fine)
    planes = freq // 2
    total = polars * (samples - (taps - 1) * fine)
    held = {}
    for jz in range(planes):
        split = jz == planes - 1
        place = jnp.stack([(f_me >> 1) ^ jz, f_me & 1]).astype(jnp.int32)
        made = spectra_pair(place, view, filter_taps, table, split)
        for i, piece in enumerate(made):
            j, p = 2 * jz + i % 2, i // 2
            held[j, p] = piece if j == 0 else swap(piece, "freq", j, freq)

    bits = [1 << i for i in range(stn.bit_length() - 1)]
    have = {}
    for (j, p), piece in held.items():
        have[j, p] = {0: piece}
        for bit in bits if j % 2 == 0 else bits[::-1]:
            have[j, p].update({g ^ bit: swap(a, "stn", bit, stn) for g, a in have[j, p].items()})

    tile = 4 * LANES
    steps = total // polars // tile
    out = None
    for p in range(polars):
        pieces = [
            (g, j, piece)
            for (j, part), group in have.items()
            for g, piece in group.items()
            if j < freq - 2 or part == p
        ]
        out = beam_sum(weights, pieces, total, p * steps, steps, tile, out)
    high = out.shape[1] // 2
    return out.reshape(out.shape[0], high, 2, LANES).transpose(0, 2, 1, 3).reshape(
        out.shape[0], 2, 1, high * LANES
    )


def solution(mesh):
    placed = (
        P(("stn", "freq"), None, None, None, None),
        P(),
        P("freq", None, "stn", None),
        P("stn"),
        P("freq"),
    )
    stn, freq = mesh.shape["stn"], mesh.shape["freq"]

    def per_device(voltages, filter_taps, beam_weights, station_map, active_counts):
        args = (voltages, filter_taps, beam_weights, station_map, active_counts)
        if voltages.shape[0] % 16 or active_counts.shape[0] != 1:
            return plain(*args)
        return fast(stn, freq, *args)

    return jax.shard_map(
        per_device,
        mesh=mesh,
        in_specs=placed,
        out_specs=P("stn", None, "freq", None),
        check_vma=False,
    )
```

profile of v0, /device:TPU:0, one launch (start us, length us, event | category | flops | bytes accessed | tf_op | source)
XLA Modules:
  0.0 169.4 jit_solution(7322566595566261555)
XLA Ops:
  1.3 5.5 %mask.1 = (bf16[2,8,16,256]{3,2,1,0:T(8,128)(2,1)}, bf16[2,8,16,256]{3,2,1,0:T(8,128)(2,1)}, bf16[2,8,16,256]{3,2,1,0:T(8,128)(2,1)}, bf16[2,8,16,256]{3,2,1,0:T(8,128)(2,1)}) custom-call(s32[2]{0:T(128)} %pad_add_fusion.info, s32[128]{0:T(128)} %ids.1, s32[1]{0:T(128)S(6)} %copy.10.count, bf16[2,8,16,1024]{3,2,1,0:T(8,128)(2,1)} %bitcast.26), custom_call_target="tpu_custom_call" | custom-call | tf_op jit(solution)/shard_map/mask/pallas_call | solution.py:183
  6.8 3.0 %collective-permute-start = (bf16[2,8,16,256]{3,2,1,0:T(8,128)(2,1)}, bf16[2,8,16,256]{3,2,1,0:T(8,128)(2,1)S(1)}, u32[]{:S(2)}, u32[]{:S(2)}) collective-permute-start(bf16[2,8,16,256]{3,2,1,0:T(8,128)(2,1)} %get-tuple-element.20), channel_id=1, source_target_pairs={{0,8},{8,0},{16,24},{24,16},{1,9},{9,1},{17,25},{25,17},{2,10},{10... | collective-permute-start | bytes 393224 | tf_op jit(solution)/shard_map/ppermute | solution.py:287
  9.8 1.5 collective-permute-start.1
  12.0 4.8 %spectra.7 = (bf16[2,16,2560]{2,1,0:T(8,128)(2,1)}, bf16[2,16,2560]{2,1,0:T(8,128)(2,1)}, bf16[2,16,2560]{2,1,0:T(8,128)(2,1)}, bf16[2,16,2560]{2,1,0:T(8,128)(2,1)}) custom-call(s32[2]{0:T(128)} %get-tuple-element.36.info, bf16[16,2,4,168,128]{4,3,2,1,0:T(8,128)(2,1)} %bitcast.22, f32[12,256]{1,0:T(8,128)} %taps_ref.7, bf16[256,512]{1,0:T(8,128)(2,1)} %constant.20.table), custom_call_target="tpu_custom_call" | custom-call | flops 800000000 | bytes 4000000 | tf_op jit(solution)/shard_map/spectra/pallas_call | solution.py:134
  16.8 4.1 %collective-permute-start.26 = (bf16[2,16,2560]{2,1,0:T(8,128)(2,1)}, bf16[2,16,2560]{2,1,0:T(8,128)(2,1)S(1)}, u32[]{:S(2)}, u32[]{:S(2)}) collective-permute-start(bf16[2,16,2560]{2,1,0:T(8,128)(2,1)} %get-tuple-element.29), channel_id=1, source_target_pairs={{0,6},{1,7},{2,4},{3,5},{4,2},{5,3},{6,0},{7,1},{8,14},{9,15},{10,... | collective-permute-start | bytes 491528 | tf_op jit(solution)/shard_map/ppermute | solution.py:287
  20.9 2.1 %collective-permute-start.34 = (bf16[2,16,2560]{2,1,0:T(8,128)(2,1)}, bf16[2,16,2560]{2,1,0:T(8,128)(2,1)S(1)}, u32[]{:S(2)}, u32[]{:S(2)}) collective-permute-start(bf16[2,16,2560]{2,1,0:T(8,128)(2,1)} %get-tuple-element.31), channel_id=1, source_target_pairs={{0,6},{1,7},{2,4},{3,5},{4,2},{5,3},{6,0},{7,1},{8,14},{9,15},{10,... | collective-permute-start | bytes 491528 | tf_op jit(solution)/shard_map/ppermute | solution.py:287
  23.7 4.4 %spectra.4 = (bf16[2,16,5120]{2,1,0:T(8,128)(2,1)}, bf16[2,16,5120]{2,1,0:T(8,128)(2,1)}) custom-call(s32[2]{0:T(128)} %get-tuple-element.33.info, bf16[16,2,4,168,128]{4,3,2,1,0:T(8,128)(2,1)} %bitcast.23, f32[12,256]{1,0:T(8,128)} %taps_ref.7, bf16[256,512]{1,0:T(8,128)(2,1)} %constant.20.table), custom_call_target="tpu_custom_call" | custom-call | flops 800000000 | bytes 4000000 | tf_op jit(solution)/shard_map/spectra/pallas_call | solution.py:134
  28.1 1.6 collective-permute-start.4
  33.1 4.5 %spectra.6 = (bf16[2,16,5120]{2,1,0:T(8,128)(2,1)}, bf16[2,16,5120]{2,1,0:T(8,128)(2,1)}) custom-call(s32[2]{0:T(128)} %get-tuple-element.35.info, bf16[16,2,4,168,128]{4,3,2,1,0:T(8,128)(2,1)} %bitcast.24, f32[12,256]{1,0:T(8,128)} %taps_ref.7, bf16[256,512]{1,0:T(8,128)(2,1)} %constant.20.table), custom_call_target="tpu_custom_call" | custom-call | flops 800000000 | bytes 4000000 | tf_op jit(solution)/shard_map/spectra/pallas_call | solution.py:134
  37.6 10.5 %collective-permute-start.18 = (bf16[2,16,5120]{2,1,0:T(8,128)(2,1)}, bf16[2,16,5120]{2,1,0:T(8,128)(2,1)S(1)}, u32[]{:S(2)}, u32[]{:S(2)}) collective-permute-start(bf16[2,16,5120]{2,1,0:T(8,128)(2,1)} %get-tuple-element.27), channel_id=1, source_target_pairs={{0,4},{1,5},{2,6},{3,7},{4,0},{5,1},{6,2},{7,3},{8,12},{9,13},{10,... | collective-permute-start | bytes 983048 | tf_op jit(solution)/shard_map/ppermute | solution.py:287
  49.6 1.5 collective-permute-start.27
  51.1 1.5 collective-permute-start.31
  53.1 17.6 %collective-permute-done.18.refs_16_ = bf16[2,16,5120]{2,1,0:T(8,128)(2,1)S(1)} collective-permute-done((bf16[2,16,5120]{2,1,0:T(8,128)(2,1)}, bf16[2,16,5120]{2,1,0:T(8,128)(2,1)S(1)}, u32[]{:S(2)}, u32[]{:S(2)}) %collective-permute-start.18) | collective-permute-done | bytes 327712 | tf_op jit(solution)/shard_map/ppermute | solution.py:287
  70.7 1.5 collective-permute-start.35
  72.2 4.4 %spectra.5 = (bf16[2,16,5120]{2,1,0:T(8,128)(2,1)}, bf16[2,16,5120]{2,1,0:T(8,128)(2,1)}) custom-call(s32[2]{0:T(128)} %get-tuple-element.34.info, bf16[16,2,4,168,128]{4,3,2,1,0:T(8,128)(2,1)} %bitcast.25, f32[12,256]{1,0:T(8,128)} %taps_ref.7, bf16[256,512]{1,0:T(8,128)(2,1)} %constant.20.table), custom_call_target="tpu_custom_call" | custom-call | flops 800000000 | bytes 4000000 | tf_op jit(solution)/shard_map/spectra/pallas_call | solution.py:134
  79.9 1.5 collective-permute-start.40
  81.4 1.5 collective-permute-start.39
  83.5 3.5 %collective-permute-done.40.refs_30_ = bf16[2,16,2560]{2,1,0:T(8,128)(2,1)S(1)} collective-permute-done((bf16[2,16,2560]{2,1,0:T(8,128)(2,1)S(1)}, bf16[2,16,2560]{2,1,0:T(8,128)(2,1)S(1)}, u32[]{:S(2)}, u32[]{:S(2)}) %collective-permute-start.40) | collective-permute-done | bytes 163872 | tf_op jit(solution)/shard_map/ppermute | solution.py:287
  87.0 1.5 collective-permute-start.37
  88.5 1.5 collective-permute-start.41
  90.6 3.1 %collective-permute-done.14.refs_12_ = bf16[2,16,5120]{2,1,0:T(8,128)(2,1)S(1)} collective-permute-done((bf16[2,16,5120]{2,1,0:T(8,128)(2,1)}, bf16[2,16,5120]{2,1,0:T(8,128)(2,1)S(1)}, u32[]{:S(2)}, u32[]{:S(2)}) %collective-permute-start.14) | collective-permute-done | bytes 327712 | tf_op jit(solution)/shard_map/ppermute | solution.py:287
  93.7 1.5 collective-permute-start.5
  95.9 1.5 collective-permute-done.41.refs_31_
  97.4 1.5 collective-permute-start.19
  99.6 1.7 %collective-permute-done.7.refs_5_ = bf16[2,16,5120]{2,1,0:T(8,128)(2,1)S(1)} collective-permute-done((bf16[2,16,5120]{2,1,0:T(8,128)(2,1)S(1)}, bf16[2,16,5120]{2,1,0:T(8,128)(2,1)S(1)}, u32[]{:S(2)}, u32[]{:S(2)}) %collective-permute-start.7) | collective-permute-done | bytes 327712 | tf_op jit(solution)/shard_map/ppermute | solution.py:287
  101.3 1.5 collective-permute-start.23
  102.8 5.5 %collective-permute-done.5.refs_3_ = bf16[2,16,5120]{2,1,0:T(8,128)(2,1)S(1)} collective-permute-done((bf16[2,16,5120]{2,1,0:T(8,128)(2,1)S(1)}, bf16[2,16,5120]{2,1,0:T(8,128)(2,1)S(1)}, u32[]{:S(2)}, u32[]{:S(2)}) %collective-permute-start.5) | collective-permute-done | bytes 327712 | tf_op jit(solution)/shard_map/ppermute | solution.py:287
  108.3 1.5 collective-permute-start.12
  109.8 5.5 %collective-permute-done.20.refs_18_ = bf16[2,16,5120]{2,1,0:T(8,128)(2,1)S(1)} collective-permute-done((bf16[2,16,5120]{2,1,0:T(8,128)(2,1)S(1)}, bf16[2,16,5120]{2,1,0:T(8,128)(2,1)S(1)}, u32[]{:S(2)}, u32[]{:S(2)}) %collective-permute-start.20) | collective-permute-done | bytes 327712 | tf_op jit(solution)/shard_map/ppermute | solution.py:287
  115.3 1.5 collective-permute-start.11
  117.4 1.5 collective-permute-start.15
  118.9 3.6 %collective-permute-done.23.refs_21_ = bf16[2,16,5120]{2,1,0:T(8,128)(2,1)} collective-permute-done((bf16[2,16,5120]{2,1,0:T(8,128)(2,1)S(1)}, bf16[2,16,5120]{2,1,0:T(8,128)(2,1)}, u32[]{:S(2)}, u32[]{:S(2)}) %collective-permute-start.23) | collective-permute-done | bytes 327712 | tf_op jit(solution)/shard_map/ppermute | solution.py:287
  122.4 1.5 collective-permute-start.9
  123.9 5.4 %collective-permute-done.12.refs_10_ = bf16[2,16,5120]{2,1,0:T(8,128)(2,1)S(1)} collective-permute-done((bf16[2,16,5120]{2,1,0:T(8,128)(2,1)S(1)}, bf16[2,16,5120]{2,1,0:T(8,128)(2,1)S(1)}, u32[]{:S(2)}, u32[]{:S(2)}) %collective-permute-start.12) | collective-permute-done | bytes 327712 | tf_op jit(solution)/shard_map/ppermute | solution.py:287
  129.4 1.5 collective-permute-start.21
  130.9 1.5 collective-permute-start.25
  132.9 1.5 collective-permute-start.13
  134.4 2.0 %collective-permute-done.15.refs_13_ = bf16[2,16,5120]{2,1,0:T(8,128)(2,1)} collective-permute-done((bf16[2,16,5120]{2,1,0:T(8,128)(2,1)S(1)}, bf16[2,16,5120]{2,1,0:T(8,128)(2,1)}, u32[]{:S(2)}, u32[]{:S(2)}) %collective-permute-start.15) | collective-permute-done | bytes 327712 | tf_op jit(solution)/shard_map/ppermute | solution.py:287
  136.5 1.5 collective-permute-start.17
  138.0 2.3 %turn.1.weights = bf16[2,256,1024]{2,1,0:T(8,128)(2,1)} custom-call(bf16[2,128,256]{2,1,0:T(8,128)(2,1)} %bitcast.27, bf16[2,128,256]{2,1,0:T(8,128)(2,1)} %bitcast.28, bf16[2,128,256]{2,1,0:T(8,128)(2,1)} %bitcast.29, bf16[2,128,256]{2,1,0:T(8,128)(2,1)} %bitcast.30), custom_call_target="tpu_custom_call" | custom-call | tf_op jit(solution)/shard_map/turn/pallas_call | solution.py:221
  140.3 1.5 collective-permute-start.28
  141.9 1.6 collective-permute-done.21.refs_19_
  145.0 2.1 %collective-permute-done.25.refs_23_ = bf16[2,16,5120]{2,1,0:T(8,128)(2,1)} collective-permute-done((bf16[2,16,5120]{2,1,0:T(8,128)(2,1)}, bf16[2,16,5120]{2,1,0:T(8,128)(2,1)}, u32[]{:S(2)}, u32[]{:S(2)}) %collective-permute-start.25) | collective-permute-done | bytes 327712 | tf_op jit(solution)/shard_map/ppermute | solution.py:287
  147.1 1.5 collective-permute-start.29
  148.6 1.9 %collective-permute-done.13.refs_11_ = bf16[2,16,5120]{2,1,0:T(8,128)(2,1)} collective-permute-done((bf16[2,16,5120]{2,1,0:T(8,128)(2,1)}, bf16[2,16,5120]{2,1,0:T(8,128)(2,1)}, u32[]{:S(2)}, u32[]{:S(2)}) %collective-permute-start.13) | collective-permute-done | bytes 327712 | tf_op jit(solution)/shard_map/ppermute | solution.py:287
  152.0 2.1 %collective-permute-done.17.refs_15_ = bf16[2,16,5120]{2,1,0:T(8,128)(2,1)} collective-permute-done((bf16[2,16,5120]{2,1,0:T(8,128)(2,1)}, bf16[2,16,5120]{2,1,0:T(8,128)(2,1)}, u32[]{:S(2)}, u32[]{:S(2)}) %collective-permute-start.17) | collective-permute-done | bytes 327712 | tf_op jit(solution)/shard_map/ppermute | solution.py:287
  154.2 7.6 %beams.2.refs_32_ = bf16[256,80,128]{2,1,0:T(8,128)(2,1)} custom-call(bf16[2,256,1024]{2,1,0:T(8,128)(2,1)} %turn.1.weights, bf16[2,16,5120]{2,1,0:T(8,128)(2,1)} %get-tuple-element.23.refs_0_, bf16[2,16,5120]{2,1,0:T(8,128)(2,1)} %copy-done.1, bf16[2,16,5120]{2,1,0:T(8,128)(2,1)} %copy-done, bf16[2,16,5120]{2,1,0:T(8,128)(2,1)} %copy-done.9, ...), custom_call_target="tpu_custom_call" | custom-call | flops 2684354560 | bytes 7864320 | tf_op jit(solution)/shard_map/beams/pallas_call | solution.py:263
  161.8 7.6 %beams.3 = bf16[256,80,128]{2,1,0:T(8,128)(2,1)} custom-call(bf16[2,256,1024]{2,1,0:T(8,128)(2,1)} %turn.1.weights, bf16[2,16,5120]{2,1,0:T(8,128)(2,1)} %get-tuple-element.23.refs_0_, bf16[2,16,5120]{2,1,0:T(8,128)(2,1)} %copy-done.1, bf16[2,16,5120]{2,1,0:T(8,128)(2,1)} %copy-done, ...), custom_call_target="tpu_custom_call", output_to_operand_aliasing={{}: (33, {})} | custom-call | flops 2684354560 | bytes 7864320 | tf_op jit(solution)/shard_map/beams/pallas_call | solution.py:263
  (103 shorter events, 17.3 us)
Async XLA Ops:
  6.8 14.1 %collective-permute-start = (bf16[2,8,16,256]{3,2,1,0:T(8,128)(2,1)}, bf16[2,8,16,256]{3,2,1,0:T(8,128)(2,1)S(1)}, u32[]{:S(2)}, u32[]{:S(2)}) collective-permute-start(bf16[2,8,16,256]{3,2,1,0:T(8,128)(2,1)} %get-tuple-element.20), channel_id=1, source_target_pairs={{0,8},{8,0},{16,24},{24,16},{1,9},{9,1},{17,25},{25,17},{2,10},{10... | collective-permute-start | bytes 393224 | tf_op jit(solution)/shard_map/ppermute | solution.py:287
  9.8 18.3 %collective-permute-start.1 = (bf16[2,8,16,256]{3,2,1,0:T(8,128)(2,1)}, bf16[2,8,16,256]{3,2,1,0:T(8,128)(2,1)S(1)}, u32[]{:S(2)}, u32[]{:S(2)}) collective-permute-start(bf16[2,8,16,256]{3,2,1,0:T(8,128)(2,1)} %get-tuple-element.21), channel_id=1, source_target_pairs={{0,16},{8,24},{16,0},{24,8},{1,17},{9,25},{17,1},{25,9},{2,18},{10... | collective-permute-start | bytes 393224 | tf_op jit(solution)/shard_map/ppermute | solution.py:287
  11.3 18.4 %collective-permute-start.2 = (bf16[2,8,16,256]{3,2,1,0:T(8,128)(2,1)}, bf16[2,8,16,256]{3,2,1,0:T(8,128)(2,1)S(1)}, u32[]{:S(2)}, u32[]{:S(2)}) collective-permute-start(bf16[2,8,16,256]{3,2,1,0:T(8,128)(2,1)} %get-tuple-element.22), channel_id=1, source_target_pairs={{0,24},{8,16},{16,8},{24,0},{1,25},{9,17},{17,9},{25,1},{2,26},{10... | collective-permute-start | bytes 393224 | tf_op jit(solution)/shard_map/ppermute | solution.py:287
  16.8 14.4 %collective-permute-start.26 = (bf16[2,16,2560]{2,1,0:T(8,128)(2,1)}, bf16[2,16,2560]{2,1,0:T(8,128)(2,1)S(1)}, u32[]{:S(2)}, u32[]{:S(2)}) collective-permute-start(bf16[2,16,2560]{2,1,0:T(8,128)(2,1)} %get-tuple-element.29), channel_id=1, source_target_pairs={{0,6},{1,7},{2,4},{3,5},{4,2},{5,3},{6,0},{7,1},{8,14},{9,15},{10,... | collective-permute-start | bytes 491528 | tf_op jit(solution)/shard_map/ppermute | solution.py:287
  20.9 11.3 %collective-permute-start.30 = (bf16[2,16,2560]{2,1,0:T(8,128)(2,1)}, bf16[2,16,2560]{2,1,0:T(8,128)(2,1)S(1)}, u32[]{:S(2)}, u32[]{:S(2)}) collective-permute-start(bf16[2,16,2560]{2,1,0:T(8,128)(2,1)} %get-tuple-element.30), channel_id=1, source_target_pairs={{0,7},{1,6},{2,5},{3,4},{4,3},{5,2},{6,1},{7,0},{8,15},{9,14},{10,... | collective-permute-start | bytes 491528 | tf_op jit(solution)/shard_map/ppermute | solution.py:287
  20.9 16.7 %collective-permute-start.34 = (bf16[2,16,2560]{2,1,0:T(8,128)(2,1)}, bf16[2,16,2560]{2,1,0:T(8,128)(2,1)S(1)}, u32[]{:S(2)}, u32[]{:S(2)}) collective-permute-start(bf16[2,16,2560]{2,1,0:T(8,128)(2,1)} %get-tuple-element.31), channel_id=1, source_target_pairs={{0,6},{1,7},{2,4},{3,5},{4,2},{5,3},{6,0},{7,1},{8,14},{9,15},{10,... | collective-permute-start | bytes 491528 | tf_op jit(solution)/shard_map/ppermute | solution.py:287
  28.1 23.0 %collective-permute-start.4 = (bf16[2,16,5120]{2,1,0:T(8,128)(2,1)}, bf16[2,16,5120]{2,1,0:T(8,128)(2,1)S(1)}, u32[]{:S(2)}, u32[]{:S(2)}) collective-permute-start(bf16[2,16,5120]{2,1,0:T(8,128)(2,1)} %get-tuple-element.23.refs_0_), channel_id=1, source_target_pairs={{0,16},{8,24},{16,0},{24,8},{1,17},{9,25},{17,1},{25,9},{2,18},{10... | collective-permute-start | bytes 983048 | tf_op jit(solution)/shard_map/ppermute | solution.py:287
  29.7 22.9 %collective-permute-start.3 = (bf16[2,16,5120]{2,1,0:T(8,128)(2,1)}, bf16[2,16,5120]{2,1,0:T(8,128)(2,1)S(1)}, u32[]{:S(2)}, u32[]{:S(2)}) collective-permute-start(bf16[2,16,5120]{2,1,0:T(8,128)(2,1)} %get-tuple-element.23.refs_0_), channel_id=1, source_target_pairs={{0,8},{8,0},{16,24},{24,16},{1,9},{9,1},{17,25},{25,17},{2,10},{10... | collective-permute-start | bytes 983048 | tf_op jit(solution)/shard_map/ppermute | solution.py:287
  31.2 109.1 %copy-start.14 = (bf16[2,16,2560]{2,1,0:T(8,128)(2,1)}, bf16[2,16,2560]{2,1,0:T(8,128)(2,1)S(1)}, u32[]{:S(2)}) copy-start(bf16[2,16,2560]{2,1,0:T(8,128)(2,1)S(1)} %collective-permute-done.26.refs_24_) | copy-start | bytes 491524
  31.2 18.4 %collective-permute-start.6 = (bf16[2,16,5120]{2,1,0:T(8,128)(2,1)}, bf16[2,16,5120]{2,1,0:T(8,128)(2,1)S(1)}, u32[]{:S(2)}, u32[]{:S(2)}) collective-permute-start(bf16[2,16,5120]{2,1,0:T(8,128)(2,1)} %get-tuple-element.24), channel_id=1, source_target_pairs={{0,1},{1,0},{2,3},{3,2},{4,5},{5,4},{6,7},{7,6},{8,9},{9,8},{10,11... | collective-permute-start | bytes 983048 | tf_op jit(solution)/shard_map/ppermute | solution.py:287
  32.2 15.9 %collective-permute-start.38 = (bf16[2,16,2560]{2,1,0:T(8,128)(2,1)S(1)}, bf16[2,16,2560]{2,1,0:T(8,128)(2,1)S(1)}, u32[]{:S(2)}, u32[]{:S(2)}) collective-permute-start(bf16[2,16,2560]{2,1,0:T(8,128)(2,1)S(1)} %copy-done.27), channel_id=1, source_target_pairs={{0,7},{1,6},{2,5},{3,4},{4,3},{5,2},{6,1},{7,0},{8,15},{9,14},{10,... | collective-permute-start | bytes 491528 | tf_op jit(solution)/shard_map/ppermute | solution.py:287
  37.6 33.1 %collective-permute-start.18 = (bf16[2,16,5120]{2,1,0:T(8,128)(2,1)}, bf16[2,16,5120]{2,1,0:T(8,128)(2,1)S(1)}, u32[]{:S(2)}, u32[]{:S(2)}) collective-permute-start(bf16[2,16,5120]{2,1,0:T(8,128)(2,1)} %get-tuple-element.27), channel_id=1, source_target_pairs={{0,4},{1,5},{2,6},{3,7},{4,0},{5,1},{6,2},{7,3},{8,12},{9,13},{10,... | collective-permute-start | bytes 983048 | tf_op jit(solution)/shard_map/ppermute | solution.py:287
  48.1 29.8 %collective-permute-start.22 = (bf16[2,16,5120]{2,1,0:T(8,128)(2,1)}, bf16[2,16,5120]{2,1,0:T(8,128)(2,1)S(1)}, u32[]{:S(2)}, u32[]{:S(2)}) collective-permute-start(bf16[2,16,5120]{2,1,0:T(8,128)(2,1)} %get-tuple-element.28), channel_id=1, source_target_pairs={{0,5},{1,4},{2,7},{3,6},{4,1},{5,0},{6,3},{7,2},{8,13},{9,12},{10,... | collective-permute-start | bytes 983048 | tf_op jit(solution)/shard_map/ppermute | solution.py:287
  49.6 104.5 %copy-start.2 = (bf16[2,16,5120]{2,1,0:T(8,128)(2,1)}, bf16[2,16,5120]{2,1,0:T(8,128)(2,1)S(1)}, u32[]{:S(2)}) copy-start(bf16[2,16,5120]{2,1,0:T(8,128)(2,1)S(1)} %collective-permute-done.6.refs_4_) | copy-start | bytes 983044
  49.6 28.3 %collective-permute-start.27 = (bf16[2,16,2560]{2,1,0:T(8,128)(2,1)S(1)}, bf16[2,16,2560]{2,1,0:T(8,128)(2,1)S(1)}, u32[]{:S(2)}, u32[]{:S(2)}) collective-permute-start(bf16[2,16,2560]{2,1,0:T(8,128)(2,1)S(1)} %collective-permute-done.26.refs_24_), channel_id=1, source_target_pairs={{0,8},{8,0},{16,24},{24,16},{1,9},{9,1},{17,25},{25,17},{2,10},{10... | collective-permute-start | bytes 491528 | tf_op jit(solution)/shard_map/ppermute | solution.py:287
  51.1 103.0 %copy-start = (bf16[2,16,5120]{2,1,0:T(8,128)(2,1)}, bf16[2,16,5120]{2,1,0:T(8,128)(2,1)S(1)}, u32[]{:S(2)}) copy-start(bf16[2,16,5120]{2,1,0:T(8,128)(2,1)S(1)} %collective-permute-done.4.refs_2_) | copy-start | bytes 983044
  51.1 28.8 %collective-permute-start.31 = (bf16[2,16,2560]{2,1,0:T(8,128)(2,1)S(1)}, bf16[2,16,2560]{2,1,0:T(8,128)(2,1)S(1)}, u32[]{:S(2)}, u32[]{:S(2)}) collective-permute-start(bf16[2,16,2560]{2,1,0:T(8,128)(2,1)S(1)} %collective-permute-done.30.refs_28_), channel_id=1, source_target_pairs={{0,16},{8,24},{16,0},{24,8},{1,17},{9,25},{17,1},{25,9},{2,18},{10... | collective-permute-start | bytes 491528 | tf_op jit(solution)/shard_map/ppermute | solution.py:287
  52.6 101.5 %copy-start.1 = (bf16[2,16,5120]{2,1,0:T(8,128)(2,1)}, bf16[2,16,5120]{2,1,0:T(8,128)(2,1)S(1)}, u32[]{:S(2)}) copy-start(bf16[2,16,5120]{2,1,0:T(8,128)(2,1)S(1)} %collective-permute-done.3.refs_1_) | copy-start | bytes 983044
  52.6 28.8 %collective-permute-start.36 = (bf16[2,16,2560]{2,1,0:T(8,128)(2,1)S(1)}, bf16[2,16,2560]{2,1,0:T(8,128)(2,1)S(1)}, u32[]{:S(2)}, u32[]{:S(2)}) collective-permute-start(bf16[2,16,2560]{2,1,0:T(8,128)(2,1)S(1)} %collective-permute-done.34.refs_24_), channel_id=1, source_target_pairs={{0,16},{8,24},{16,0},{24,8},{1,17},{9,25},{17,1},{25,9},{2,18},{10... | collective-permute-start | bytes 491528 | tf_op jit(solution)/shard_map/ppermute | solution.py:287
  70.7 83.4 %copy-start.3 = (bf16[2,16,5120]{2,1,0:T(8,128)(2,1)}, bf16[2,16,5120]{2,1,0:T(8,128)(2,1)S(1)}, u32[]{:S(2)}) copy-start(bf16[2,16,5120]{2,1,0:T(8,128)(2,1)S(1)} %collective-permute-done.18.refs_16_) | copy-start | bytes 983044
  70.7 12.2 %collective-permute-start.35 = (bf16[2,16,2560]{2,1,0:T(8,128)(2,1)S(1)}, bf16[2,16,2560]{2,1,0:T(8,128)(2,1)}, u32[]{:S(2)}, u32[]{:S(2)}) collective-permute-start(bf16[2,16,2560]{2,1,0:T(8,128)(2,1)S(1)} %collective-permute-done.34.refs_24_), channel_id=1, source_target_pairs={{0,8},{8,0},{16,24},{24,16},{1,9},{9,1},{17,25},{25,17},{2,10},{10... | collective-permute-start | bytes 491528 | tf_op jit(solution)/shard_map/ppermute | solution.py:287
  77.9 76.2 %copy-start.4 = (bf16[2,16,5120]{2,1,0:T(8,128)(2,1)}, bf16[2,16,5120]{2,1,0:T(8,128)(2,1)S(1)}, u32[]{:S(2)}) copy-start(bf16[2,16,5120]{2,1,0:T(8,128)(2,1)S(1)} %collective-permute-done.22.refs_20_) | copy-start | bytes 983044
  77.9 12.1 %collective-permute-start.10 = (bf16[2,16,5120]{2,1,0:T(8,128)(2,1)}, bf16[2,16,5120]{2,1,0:T(8,128)(2,1)S(1)}, u32[]{:S(2)}, u32[]{:S(2)}) collective-permute-start(bf16[2,16,5120]{2,1,0:T(8,128)(2,1)} %get-tuple-element.25), channel_id=1, source_target_pairs={{0,2},{1,3},{2,0},{3,1},{4,6},{5,7},{6,4},{7,5},{8,10},{9,11},{10,... | collective-permute-start | bytes 983048 | tf_op jit(solution)/shard_map/ppermute | solution.py:287
  78.7 15.0 %collective-permute-start.14 = (bf16[2,16,5120]{2,1,0:T(8,128)(2,1)}, bf16[2,16,5120]{2,1,0:T(8,128)(2,1)S(1)}, u32[]{:S(2)}, u32[]{:S(2)}) collective-permute-start(bf16[2,16,5120]{2,1,0:T(8,128)(2,1)} %get-tuple-element.26), channel_id=1, source_target_pairs={{0,3},{1,2},{2,1},{3,0},{4,7},{5,6},{6,5},{7,4},{8,11},{9,10},{10,... | collective-permute-start | bytes 983048 | tf_op jit(solution)/shard_map/ppermute | solution.py:287
  79.9 7.1 %collective-permute-start.40 = (bf16[2,16,2560]{2,1,0:T(8,128)(2,1)S(1)}, bf16[2,16,2560]{2,1,0:T(8,128)(2,1)S(1)}, u32[]{:S(2)}, u32[]{:S(2)}) collective-permute-start(bf16[2,16,2560]{2,1,0:T(8,128)(2,1)S(1)} %collective-permute-done.38.refs_28_), channel_id=1, source_target_pairs={{0,8},{8,0},{16,24},{24,16},{1,9},{9,1},{17,25},{25,17},{2,10},{10... | collective-permute-start | bytes 491528 | tf_op jit(solution)/shard_map/ppermute | solution.py:287
  81.4 7.1 %collective-permute-start.39 = (bf16[2,16,2560]{2,1,0:T(8,128)(2,1)S(1)}, bf16[2,16,2560]{2,1,0:T(8,128)(2,1)S(1)}, u32[]{:S(2)}, u32[]{:S(2)}) collective-permute-start(bf16[2,16,2560]{2,1,0:T(8,128)(2,1)S(1)} %collective-permute-done.38.refs_28_), channel_id=1, source_target_pairs={{0,16},{8,24},{16,0},{24,8},{1,17},{9,25},{17,1},{25,9},{2,18},{10... | collective-permute-start | bytes 491528 | tf_op jit(solution)/shard_map/ppermute | solution.py:287
  82.9 16.0 %collective-permute-start.8 = (bf16[2,16,5120]{2,1,0:T(8,128)(2,1)S(1)}, bf16[2,16,5120]{2,1,0:T(8,128)(2,1)S(1)}, u32[]{:S(2)}, u32[]{:S(2)}) collective-permute-start(bf16[2,16,5120]{2,1,0:T(8,128)(2,1)S(1)} %collective-permute-done.6.refs_4_), channel_id=1, source_target_pairs={{0,8},{8,0},{16,24},{24,16},{1,9},{9,1},{17,25},{25,17},{2,10},{10... | collective-permute-start | bytes 983048 | tf_op jit(solution)/shard_map/ppermute | solution.py:287
  87.0 8.2 %collective-permute-start.37 = (bf16[2,16,2560]{2,1,0:T(8,128)(2,1)}, bf16[2,16,2560]{2,1,0:T(8,128)(2,1)}, u32[]{:S(2)}, u32[]{:S(2)}) collective-permute-start(bf16[2,16,2560]{2,1,0:T(8,128)(2,1)} %collective-permute-done.35.refs_25_), channel_id=1, source_target_pairs={{0,16},{8,24},{16,0},{24,8},{1,17},{9,25},{17,1},{25,9},{2,18},{10... | collective-permute-start | bytes 491528 | tf_op jit(solution)/shard_map/ppermute | solution.py:287
  88.5 8.9 %collective-permute-start.41 = (bf16[2,16,2560]{2,1,0:T(8,128)(2,1)S(1)}, bf16[2,16,2560]{2,1,0:T(8,128)(2,1)S(1)}, u32[]{:S(2)}, u32[]{:S(2)}) collective-permute-start(bf16[2,16,2560]{2,1,0:T(8,128)(2,1)S(1)} %collective-permute-done.39.refs_29_), channel_id=1, source_target_pairs={{0,8},{8,0},{16,24},{24,16},{1,9},{9,1},{17,25},{25,17},{2,10},{10... | collective-permute-start | bytes 491528 | tf_op jit(solution)/shard_map/ppermute | solution.py:287
  90.0 11.3 %collective-permute-start.7 = (bf16[2,16,5120]{2,1,0:T(8,128)(2,1)S(1)}, bf16[2,16,5120]{2,1,0:T(8,128)(2,1)S(1)}, u32[]{:S(2)}, u32[]{:S(2)}) collective-permute-start(bf16[2,16,5120]{2,1,0:T(8,128)(2,1)S(1)} %collective-permute-done.6.refs_4_), channel_id=1, source_target_pairs={{0,16},{8,24},{16,0},{24,8},{1,17},{9,25},{17,1},{25,9},{2,18},{10... | collective-permute-start | bytes 983048 | tf_op jit(solution)/shard_map/ppermute | solution.py:287
  93.7 14.6 %collective-permute-start.5 = (bf16[2,16,5120]{2,1,0:T(8,128)(2,1)S(1)}, bf16[2,16,5120]{2,1,0:T(8,128)(2,1)S(1)}, u32[]{:S(2)}, u32[]{:S(2)}) collective-permute-start(bf16[2,16,5120]{2,1,0:T(8,128)(2,1)S(1)} %collective-permute-done.3.refs_1_), channel_id=1, source_target_pairs={{0,16},{8,24},{16,0},{24,8},{1,17},{9,25},{17,1},{25,9},{2,18},{10... | collective-permute-start | bytes 983048 | tf_op jit(solution)/shard_map/ppermute | solution.py:287
  95.2 20.1 %collective-permute-start.20 = (bf16[2,16,5120]{2,1,0:T(8,128)(2,1)S(1)}, bf16[2,16,5120]{2,1,0:T(8,128)(2,1)S(1)}, u32[]{:S(2)}, u32[]{:S(2)}) collective-permute-start(bf16[2,16,5120]{2,1,0:T(8,128)(2,1)S(1)} %collective-permute-done.18.refs_16_), channel_id=1, source_target_pairs={{0,16},{8,24},{16,0},{24,8},{1,17},{9,25},{17,1},{25,9},{2,18},{10... | collective-permute-start | bytes 983048 | tf_op jit(solution)/shard_map/ppermute | solution.py:287
  97.4 19.4 %collective-permute-start.19 = (bf16[2,16,5120]{2,1,0:T(8,128)(2,1)S(1)}, bf16[2,16,5120]{2,1,0:T(8,128)(2,1)}, u32[]{:S(2)}, u32[]{:S(2)}) collective-permute-start(bf16[2,16,5120]{2,1,0:T(8,128)(2,1)S(1)} %collective-permute-done.18.refs_16_), channel_id=1, source_target_pairs={{0,8},{8,0},{16,24},{24,16},{1,9},{9,1},{17,25},{25,17},{2,10},{10... | collective-permute-start | bytes 983048 | tf_op jit(solution)/shard_map/ppermute | solution.py:287
  98.9 18.4 %collective-permute-start.24 = (bf16[2,16,5120]{2,1,0:T(8,128)(2,1)S(1)}, bf16[2,16,5120]{2,1,0:T(8,128)(2,1)S(1)}, u32[]{:S(2)}, u32[]{:S(2)}) collective-permute-start(bf16[2,16,5120]{2,1,0:T(8,128)(2,1)S(1)} %collective-permute-done.22.refs_20_), channel_id=1, source_target_pairs={{0,8},{8,0},{16,24},{24,16},{1,9},{9,1},{17,25},{25,17},{2,10},{10... | collective-permute-start | bytes 983048 | tf_op jit(solution)/shard_map/ppermute | solution.py:287
  101.3 21.2 %collective-permute-start.23 = (bf16[2,16,5120]{2,1,0:T(8,128)(2,1)S(1)}, bf16[2,16,5120]{2,1,0:T(8,128)(2,1)}, u32[]{:S(2)}, u32[]{:S(2)}) collective-permute-start(bf16[2,16,5120]{2,1,0:T(8,128)(2,1)S(1)} %collective-permute-done.22.refs_20_), channel_id=1, source_target_pairs={{0,16},{8,24},{16,0},{24,8},{1,17},{9,25},{17,1},{25,9},{2,18},{10... | collective-permute-start | bytes 983048 | tf_op jit(solution)/shard_map/ppermute | solution.py:287
  108.3 21.1 %collective-permute-start.12 = (bf16[2,16,5120]{2,1,0:T(8,128)(2,1)S(1)}, bf16[2,16,5120]{2,1,0:T(8,128)(2,1)S(1)}, u32[]{:S(2)}, u32[]{:S(2)}) collective-permute-start(bf16[2,16,5120]{2,1,0:T(8,128)(2,1)S(1)} %collective-permute-done.10.refs_8_), channel_id=1, source_target_pairs={{0,16},{8,24},{16,0},{24,8},{1,17},{9,25},{17,1},{25,9},{2,18},{10... | collective-permute-start | bytes 983048 | tf_op jit(solution)/shard_map/ppermute | solution.py:287
  115.3 15.6 %collective-permute-start.11 = (bf16[2,16,5120]{2,1,0:T(8,128)(2,1)S(1)}, bf16[2,16,5120]{2,1,0:T(8,128)(2,1)}, u32[]{:S(2)}, u32[]{:S(2)}) collective-permute-start(bf16[2,16,5120]{2,1,0:T(8,128)(2,1)S(1)} %collective-permute-done.10.refs_8_), channel_id=1, source_target_pairs={{0,8},{8,0},{16,24},{24,16},{1,9},{9,1},{17,25},{25,17},{2,10},{10... | collective-permute-start | bytes 983048 | tf_op jit(solution)/shard_map/ppermute | solution.py:287
  116.8 16.1 %collective-permute-start.16 = (bf16[2,16,5120]{2,1,0:T(8,128)(2,1)S(1)}, bf16[2,16,5120]{2,1,0:T(8,128)(2,1)S(1)}, u32[]{:S(2)}, u32[]{:S(2)}) collective-permute-start(bf16[2,16,5120]{2,1,0:T(8,128)(2,1)S(1)} %collective-permute-done.14.refs_12_), channel_id=1, source_target_pairs={{0,8},{8,0},{16,24},{24,16},{1,9},{9,1},{17,25},{25,17},{2,10},{10... | collective-permute-start | bytes 983048 | tf_op jit(solution)/shard_map/ppermute | solution.py:287
  117.4 19.1 %collective-permute-start.15 = (bf16[2,16,5120]{2,1,0:T(8,128)(2,1)S(1)}, bf16[2,16,5120]{2,1,0:T(8,128)(2,1)}, u32[]{:S(2)}, u32[]{:S(2)}) collective-permute-start(bf16[2,16,5120]{2,1,0:T(8,128)(2,1)S(1)} %collective-permute-done.14.refs_12_), channel_id=1, source_target_pairs={{0,16},{8,24},{16,0},{24,8},{1,17},{9,25},{17,1},{25,9},{2,18},{10... | collective-permute-start | bytes 983048 | tf_op jit(solution)/shard_map/ppermute | solution.py:287
  122.4 17.9 %collective-permute-start.9 = (bf16[2,16,5120]{2,1,0:T(8,128)(2,1)S(1)}, bf16[2,16,5120]{2,1,0:T(8,128)(2,1)}, u32[]{:S(2)}, u32[]{:S(2)}) collective-permute-start(bf16[2,16,5120]{2,1,0:T(8,128)(2,1)S(1)} %collective-permute-done.7.refs_5_), channel_id=1, source_target_pairs={{0,8},{8,0},{16,24},{24,16},{1,9},{9,1},{17,25},{25,17},{2,10},{10... | collective-permute-start | bytes 983048 | tf_op jit(solution)/shard_map/ppermute | solution.py:287
  129.4 14.1 %collective-permute-start.21 = (bf16[2,16,5120]{2,1,0:T(8,128)(2,1)}, bf16[2,16,5120]{2,1,0:T(8,128)(2,1)}, u32[]{:S(2)}, u32[]{:S(2)}) collective-permute-start(bf16[2,16,5120]{2,1,0:T(8,128)(2,1)} %collective-permute-done.19.refs_17_), channel_id=1, source_target_pairs={{0,16},{8,24},{16,0},{24,8},{1,17},{9,25},{17,1},{25,9},{2,18},{10... | collective-permute-start | bytes 983048 | tf_op jit(solution)/shard_map/ppermute | solution.py:287
  130.9 16.2 %collective-permute-start.25 = (bf16[2,16,5120]{2,1,0:T(8,128)(2,1)}, bf16[2,16,5120]{2,1,0:T(8,128)(2,1)}, u32[]{:S(2)}, u32[]{:S(2)}) collective-permute-start(bf16[2,16,5120]{2,1,0:T(8,128)(2,1)} %collective-permute-done.23.refs_21_), channel_id=1, source_target_pairs={{0,8},{8,0},{16,24},{24,16},{1,9},{9,1},{17,25},{25,17},{2,10},{10... | collective-permute-start | bytes 983048 | tf_op jit(solution)/shard_map/ppermute | solution.py:287
  132.9 17.6 %collective-permute-start.13 = (bf16[2,16,5120]{2,1,0:T(8,128)(2,1)}, bf16[2,16,5120]{2,1,0:T(8,128)(2,1)}, u32[]{:S(2)}, u32[]{:S(2)}) collective-permute-start(bf16[2,16,5120]{2,1,0:T(8,128)(2,1)} %collective-permute-done.11.refs_9_), channel_id=1, source_target_pairs={{0,16},{8,24},{16,0},{24,8},{1,17},{9,25},{17,1},{25,9},{2,18},{10... | collective-permute-start | bytes 983048 | tf_op jit(solution)/shard_map/ppermute | solution.py:287
  136.5 17.6 %collective-permute-start.17 = (bf16[2,16,5120]{2,1,0:T(8,128)(2,1)}, bf16[2,16,5120]{2,1,0:T(8,128)(2,1)}, u32[]{:S(2)}, u32[]{:S(2)}) collective-permute-start(bf16[2,16,5120]{2,1,0:T(8,128)(2,1)} %collective-permute-done.15.refs_13_), channel_id=1, source_target_pairs={{0,8},{8,0},{16,24},{24,16},{1,9},{9,1},{17,25},{25,17},{2,10},{10... | collective-permute-start | bytes 983048 | tf_op jit(solution)/shard_map/ppermute | solution.py:287
  140.3 21.4 %collective-permute-start.28 = (bf16[2,16,2560]{2,1,0:T(8,128)(2,1)S(1)}, bf16[2,16,2560]{2,1,0:T(8,128)(2,1)}, u32[]{:S(2)}, u32[]{:S(2)}) collective-permute-start(bf16[2,16,2560]{2,1,0:T(8,128)(2,1)S(1)} %collective-permute-done.26.refs_24_), channel_id=1, source_target_pairs={{0,16},{8,24},{16,0},{24,8},{1,17},{9,25},{17,1},{25,9},{2,18},{10... | collective-permute-start | bytes 491528 | tf_op jit(solution)/shard_map/ppermute | solution.py:287
  143.5 18.3 %collective-permute-start.32 = (bf16[2,16,2560]{2,1,0:T(8,128)(2,1)}, bf16[2,16,2560]{2,1,0:T(8,128)(2,1)}, u32[]{:S(2)}, u32[]{:S(2)}) collective-permute-start(bf16[2,16,2560]{2,1,0:T(8,128)(2,1)} %copy-done.15), channel_id=1, source_target_pairs={{0,8},{8,0},{16,24},{24,16},{1,9},{9,1},{17,25},{25,17},{2,10},{10... | collective-permute-start | bytes 491528 | tf_op jit(solution)/shard_map/ppermute | solution.py:287
  147.1 14.7 %collective-permute-start.29 = (bf16[2,16,2560]{2,1,0:T(8,128)(2,1)}, bf16[2,16,2560]{2,1,0:T(8,128)(2,1)}, u32[]{:S(2)}, u32[]{:S(2)}) collective-permute-start(bf16[2,16,2560]{2,1,0:T(8,128)(2,1)} %copy-done.18), channel_id=1, source_target_pairs={{0,16},{8,24},{16,0},{24,8},{1,17},{9,25},{17,1},{25,9},{2,18},{10... | collective-permute-start | bytes 491528 | tf_op jit(solution)/shard_map/ppermute | solution.py:287
  150.5 11.3 %collective-permute-start.33 = (bf16[2,16,2560]{2,1,0:T(8,128)(2,1)}, bf16[2,16,2560]{2,1,0:T(8,128)(2,1)}, u32[]{:S(2)}, u32[]{:S(2)}) collective-permute-start(bf16[2,16,2560]{2,1,0:T(8,128)(2,1)} %copy-done.19), channel_id=1, source_target_pairs={{0,8},{8,0},{16,24},{24,16},{1,9},{9,1},{17,25},{25,17},{2,10},{10... | collective-permute-start | bytes 491528 | tf_op jit(solution)/shard_map/ppermute | solution.py:287
  (22 other events, 576.4 us)
where the time goes:
time: 171 us; the launch traced here: 169 us
  starting transfers between devices  65.5 us (38%)
  waiting for transfers between devices  59 us (35%)
  Pallas kernels  41.2 us (24%)
  other arithmetic  1.97 us (1%)
    ppermute x42, starting transfers between devices, swap(): return lax.ppermute(array, axis, [(i, i ^ step) for i in range(size)])  65.5 us
    ppermute x42, waiting for transfers between devices, swap(): return lax.ppermute(array, axis, [(i, i ^ step) for i in range(size)])  59 us
    pallas_call x4, Pallas kernels, spectra_pair(): pl.pallas_call(functools.partial(spectra_body, (slots, taps, frames_out,...  18.2 us
    pallas_call x2, Pallas kernels, beam_sum(): pl.pallas_call(functools.partial(beam_body, [(g, j) for g, j, _ in pieces...  15.2 us
    pallas_call x1, Pallas kernels, mask_weights(): pl.pallas_call(mask_body, grid_spec=pltpu.PrefetchScalarGridSpec(num_scal...  5.5 us
  transfers between devices with their start and end apart: 42, of which 16 were waited for; matrix products, arithmetic and copies ran while one was open for 1% of the time, Pallas kernels for 17%

commit v1 on v0

--- a/solution.py
+++ b/solution.py
@@ -79,7 +79,7 @@
     slots, taps, frames_out, per_pair, pitch, split = dims
     outs, wide, rows = refs[:-2], refs[-2], refs[-1]
     blocks = frames_out + taps - 1
-    core = info[1]
+    core = info[1] & 1
     fine = 2 * LANES
     for s in range(slots):
         wide[pl.ds(s * pitch, per_pair), :] = volt[s, 0, 0].astype(jnp.float32)
@@ -119,7 +119,7 @@
                 pl.when(pl.program_id(0) == p)(functools.partial(put, outs[2 * p + turn]))
 
 
-def spectra_pair(info, view, filter_taps, table, split):
+def spectra_pair(info, plane, view, filter_taps, table, split):
     slots, polars, _, per_pair, _ = view.shape
     taps, fine = filter_taps.shape
     frames_out = per_pair // 8 - taps + 1
@@ -132,15 +132,13 @@
         shapes = [jax.ShapeDtypeStruct((2, slots, polars * width), jnp.bfloat16)] * 2
         out_specs = [pl.BlockSpec((2, slots, width), lambda p, info: (0, 0, p))] * 2
     return pl.pallas_call(
-        functools.partial(
-            spectra_body, (slots, taps, frames_out, per_pair, pitch, split)
-        ),
+        functools.partial(spectra_body, (slots, taps, frames_out, per_pair, pitch, split)),
         grid_spec=pltpu.PrefetchScalarGridSpec(
             num_scalar_prefetch=1,
             grid=(polars,),
             in_specs=[
                 pl.BlockSpec(
-                    (slots, 1, 1, per_pair, LANES), lambda p, info: (0, p, info[0], 0, 0)
+                    (slots, 1, 1, per_pair, LANES), lambda p, info: (0, p, (info[1] >> 1) ^ plane, 0, 0)
                 ),
                 pl.BlockSpec((taps, fine), lambda p, info: (0, 0)),
                 pl.BlockSpec((fine, 2 * fine), lambda p, info: (0, 0)),
@@ -160,84 +158,91 @@
     )(info, view, filter_taps, table)
 
 
-def mask_body(info, ids, count, weights, *outs):
-    slots = weights.shape[2]
+def mask_body(info, count, ids, weights, *refs):
+    outs, live = refs[:-1], refs[-1]
+    _, freq, slots, _ = weights.shape
     width = outs[0].shape[3]
-    place = jnp.bitwise_xor(pl.program_id(0), info[1]) * slots
-    row = lax.broadcasted_iota(jnp.int32, (slots, LANES), 0)
-    mine = jnp.zeros((slots, LANES), jnp.int32)
-    for s in range(slots):
-        mine = jnp.where(row == s, ids[place + s], mine)
-    live = (mine < count[0]).astype(jnp.float32)[:, :1]
-    for d, out in enumerate(outs):
-        start = pl.multiple_of(jnp.bitwise_xor(info[0], d) * width, width)
-        for q in range(2):
-            value = weights[q, 0, :, pl.ds(start, width)].astype(jnp.float32)
-            out[q, 0] = (value * live).astype(jnp.bfloat16)
+    known = jnp.broadcast_to(ids[...], (LANES, ids.shape[1])).astype(jnp.float32).T
+    live[...] = (known < count[0].astype(jnp.float32)).astype(jnp.float32)
+    for j in range(freq):
+        place = jnp.bitwise_xor(info[1], j)
+        keep = live[pl.ds(pl.multiple_of(place * slots, slots), slots), :][:, :1]
+        for d, out in enumerate(outs):
+            start = pl.multiple_of(jnp.bitwise_xor(info[0], d) * width, width)
+            for q in range(2):
+                value = weights[q, place, :, pl.ds(start, width)].astype(jnp.float32)
+                out[q, j] = (value * keep).astype(jnp.bfloat16)
 
 
 def mask_weights(info, ids, count, weights, stn):
     _, freq, slots, beams = weights.shape
-    width = beams // stn
-    shape = jax.ShapeDtypeStruct((2, freq, slots, width), jnp.bfloat16)
+    shape = jax.ShapeDtypeStruct((2, freq, slots, beams // stn), jnp.bfloat16)
+    smem = pl.BlockSpec(memory_space=pltpu.SMEM)
+    vmem = pl.BlockSpec(memory_space=pltpu.VMEM)
     return pl.pallas_call(
         mask_body,
-        grid_spec=pltpu.PrefetchScalarGridSpec(
-            num_scalar_prefetch=3,
-            grid=(freq,),
-            in_specs=[
-                pl.BlockSpec(
-                    (2, 1, slots, beams),
-                    lambda j, info, ids, count: (0, jnp.bitwise_xor(j, info[1]), 0, 0),
-                )
-            ],
-            out_specs=[
-                pl.BlockSpec((2, 1, slots, width), lambda j, info, ids, count: (0, j, 0, 0))
-            ]
-            * stn,
-        ),
+        in_specs=[smem, smem, vmem, vmem],
+        out_specs=[vmem] * stn,
         out_shape=[shape] * stn,
-        compiler_params=pltpu.CompilerParams(dimension_semantics=("arbitrary",)),
+        scratch_shapes=[pltpu.VMEM((freq * slots, LANES), jnp.float32)],
         name="mask",
-    )(info, ids, count, weights)
-
-
-def turn_body(*refs):
-    parts, out = refs[:-1], refs[-1]
+    )(info, count, ids.reshape(1, freq * slots), weights)
+
+
+def turn_body(cut, *refs):
+    parts, outs = refs[:-2], refs[-2:]
     rows = parts[0].shape[1]
     for g, part in enumerate(parts):
-        real = part[0].astype(jnp.float32).T
-        imag = part[1].astype(jnp.float32).T
-        lead = slice(2 * g * rows, (2 * g + 1) * rows)
-        tail = slice((2 * g + 1) * rows, (2 * g + 2) * rows)
-        out[0, :, lead] = real.astype(jnp.bfloat16)
-        out[0, :, tail] = (-imag).astype(jnp.bfloat16)
-        out[1, :, lead] = imag.astype(jnp.bfloat16)
-        out[1, :, tail] = real.astype(jnp.bfloat16)
-
-
-def turn_weights(parts):
+        real = part[0].astype(jnp.float32).T.astype(jnp.bfloat16)
+        imag = part[1].astype(jnp.float32).T.astype(jnp.bfloat16)
+        for out, low, high in ((outs[0], 0, cut), (outs[1], cut, rows)):
+            size = high - low
+            lead = slice(2 * g * size, (2 * g + 1) * size)
+            tail = slice((2 * g + 1) * size, (2 * g + 2) * size)
+            out[0, :, lead] = real[:, low:high]
+            out[0, :, tail] = -imag[:, low:high]
+            out[1, :, lead] = imag[:, low:high]
+            out[1, :, tail] = real[:, low:high]
+
+
+def turn_weights(parts, cut):
     _, rows, width = parts[0].shape
     return pl.pallas_call(
-        turn_body,
-        out_shape=jax.ShapeDtypeStruct((2, width, 2 * len(parts) * rows), jnp.bfloat16),
+        functools.partial(turn_body, cut),
+        out_shape=[
+            jax.ShapeDtypeStruct((2, width, 2 * len(parts) * size), jnp.bfloat16)
+            for size in (cut, rows - cut)
+        ],
         name="turn",
     )(*parts)
 
 
-def beam_body(places, tile, pitch, aliased, weights, *refs):
-    count = len(places)
-    pieces = refs[:count]
-    out, data, wide = refs[count + aliased :]
+def gather_rows(places, pieces, data):
     slots = pieces[0].shape[1]
     span = data.shape[0] // (2 * (max(g for g, _ in places) + 1))
+    low = min(j for _, j in places)
     for (g, j), piece in zip(places, pieces):
         for q in range(2):
-            row = (2 * g + q) * span + j * slots
+            row = (2 * g + q) * span + (j - low) * slots
             data[row : row + slots, :] = piece[q]
+
+
+def early_body(places, weights, *refs):
+    pieces, out, data = refs[: len(places)], refs[-2], refs[-1]
+    gather_rows(places, pieces, data)
+    for q in range(2):
+        out[q] = jnp.dot(weights[q], data[...], preferred_element_type=jnp.float32)
+
+
+def late_body(places, tile, pitch, weights, partial, *refs):
+    pieces = refs[: len(places)]
+    out, data, wide = refs[len(places) :]
+    gather_rows(places, pieces, data)
     beams = weights.shape[1]
     for q in range(2):
-        part = jnp.dot(weights[q], data[...], preferred_element_type=jnp.float32)
+        part = partial[q] + jnp.dot(
+            weights[q], data[...], preferred_element_type=jnp.float32
+        )
         for j in range(tile // LANES):
             wide[pl.ds(2 * j + q, beams, stride=pitch), :] = part[
                 :, j * LANES : (j + 1) * LANES
@@ -247,40 +252,58 @@
         out[b] = wide[pl.ds(b * pitch, high), :].astype(jnp.bfloat16)
 
 
-def beam_sum(weights, pieces, total, first, steps, tile, before):
+def beam_specs(weights, pieces, tile):
     _, beams, depth = weights.shape
-    slots = pieces[0][2].shape[1]
+    _, slots, total = pieces[0][2].shape
+    specs = [pl.BlockSpec((2, beams, depth), lambda n: (0, 0, 0))]
+    parts = [pl.BlockSpec((2, slots, tile), lambda n: (0, 0, n))] * len(pieces)
+    sum_spec = pl.BlockSpec((2, beams, tile), lambda n: (0, 0, n))
+    cost = pl.CostEstimate(
+        flops=4 * beams * depth * total,
+        bytes_accessed=2 * (depth + 4 * beams) * total,
+        transcendentals=0,
+    )
+    places = [(g, j) for g, j, _ in pieces]
+    return beams, depth, total, specs, parts, sum_spec, cost, places
+
+
+def beam_early(weights, pieces, tile):
+    beams, depth, total, specs, parts, sum_spec, cost, places = beam_specs(
+        weights, pieces, tile
+    )
+    return pl.pallas_call(
+        functools.partial(early_body, places),
+        grid=(total // tile,),
+        in_specs=specs + parts,
+        out_specs=sum_spec,
+        out_shape=jax.ShapeDtypeStruct((2, beams, total), jnp.float32),
+        scratch_shapes=[pltpu.VMEM((depth, tile), jnp.bfloat16)],
+        compiler_params=pltpu.CompilerParams(dimension_semantics=("arbitrary",)),
+        cost_estimate=cost,
+        name="early",
+    )(weights, *[piece for _, _, piece in pieces])
+
+
+def beam_late(weights, partial, pieces, tile):
+    beams, depth, total, specs, parts, sum_spec, cost, places = beam_specs(
+        weights, pieces, tile
+    )
     high = 2 * tile // LANES
     pitch = high + 1
-    specs = [pl.BlockSpec((2, beams, depth), lambda n: (0, 0, 0))]
-    for _, _, piece in pieces:
-        shift = first if piece.shape[2] == total else 0
-        specs.append(
-            pl.BlockSpec((2, slots, tile), functools.partial(lambda d, n: (0, 0, n + d), shift))
-        )
-    extra = [] if before is None else [before]
-    specs += [pl.BlockSpec(memory_space=pl.ANY)] * len(extra)
-    return pl.pallas_call(
-        functools.partial(
-            beam_body, [(g, j) for g, j, _ in pieces], tile, pitch, len(extra)
-        ),
-        grid=(steps,),
-        in_specs=specs,
-        out_specs=pl.BlockSpec((beams, high, LANES), lambda n: (0, n + first, 0)),
+    return pl.pallas_call(
+        functools.partial(late_body, places, tile, pitch),
+        grid=(total // tile,),
+        in_specs=specs + [sum_spec] + parts,
+        out_specs=pl.BlockSpec((beams, high, LANES), lambda n: (0, n, 0)),
         out_shape=jax.ShapeDtypeStruct((beams, 2 * total // LANES, LANES), jnp.bfloat16),
-        input_output_aliases={len(pieces) + 1: 0} if extra else {},
         scratch_shapes=[
             pltpu.VMEM((depth, tile), jnp.bfloat16),
             pltpu.VMEM((beams * pitch, LANES), jnp.float32),
         ],
         compiler_params=pltpu.CompilerParams(dimension_semantics=("arbitrary",)),
-        cost_estimate=pl.CostEstimate(
-            flops=4 * beams * depth * tile * steps,
-            bytes_accessed=2 * (depth + 2 * beams) * tile * steps,
-            transcendentals=0,
-        ),
-        name="beams",
-    )(weights, *[piece for _, _, piece in pieces], *extra)
+        cost_estimate=cost,
+        name="late",
+    )(weights, partial, *[piece for _, _, piece in pieces])
 
 
 def swap(array, axis, step, size):
@@ -289,7 +312,7 @@
 
 def fast(stn, freq, voltages, filter_taps, beam_weights, station_map, active_counts):
     slots, polars, chans, _, samples = voltages.shape
-    taps, fine = filter_taps.shape
+    _, fine = filter_taps.shape
     s_me = lax.axis_index("stn")
     f_me = lax.axis_index("freq")
 
@@ -297,7 +320,9 @@
     grouped = beam_weights[0].reshape(2, freq, slots, beam_weights.shape[3])
     wparts = mask_weights(info, station_map, active_counts, grouped, stn)
     wparts = [wparts[0]] + [swap(wparts[d], "stn", d, stn) for d in range(1, stn)]
-    weights = turn_weights([w.reshape(2, freq * slots, -1) for w in wparts])
+    w_early, w_late = turn_weights(
+        [w.reshape(2, freq * slots, -1) for w in wparts], (freq - 2) * slots
+    )
 
     view = with_layout_constraint(
         voltages.reshape(slots, polars, chans, 2, samples // LANES, LANES),
@@ -308,12 +333,10 @@
     )
     table = cos_sin(fine)
     planes = freq // 2
-    total = polars * (samples - (taps - 1) * fine)
     held = {}
     for jz in range(planes):
-        split = jz == planes - 1
-        place = jnp.stack([(f_me >> 1) ^ jz, f_me & 1]).astype(jnp.int32)
-        made = spectra_pair(place, view, filter_taps, table, split)
+        split = False
+        made = spectra_pair(info, jz, view, filter_taps, table, split)
         for i, piece in enumerate(made):
             j, p = 2 * jz + i % 2, i // 2
             held[j, p] = piece if j == 0 else swap(piece, "freq", j, freq)
@@ -325,17 +348,11 @@
         for bit in bits if j % 2 == 0 else bits[::-1]:
             have[j, p].update({g ^ bit: swap(a, "stn", bit, stn) for g, a in have[j, p].items()})
 
-    tile = 4 * LANES
-    steps = total // polars // tile
-    out = None
-    for p in range(polars):
-        pieces = [
-            (g, j, piece)
-            for (j, part), group in have.items()
-            for g, piece in group.items()
-            if j < freq - 2 or part == p
-        ]
-        out = beam_sum(weights, pieces, total, p * steps, steps, tile, out)
+    every = [
+        (g, j, piece) for (j, _), group in have.items() for g, piece in group.items()
+    ]
+    partial = beam_early(w_early, [e for e in every if e[1] < freq - 2], 4 * LANES)
+    out = beam_late(w_late, partial, [e for e in every if e[1] >= freq - 2], 4 * LANES)
     high = out.shape[1] // 2
     return out.reshape(out.shape[0], high, 2, LANES).transpose(0, 2, 1, 3).reshape(
         out.shape[0], 2, 1, high * LANES

time: 171 us -> 167 us (0.977)
  starting transfers between devices: 65.5 us -> 31.9 us
  waiting for transfers between devices: 59 us -> 84.2 us
  Pallas kernels: 41.2 us -> 47.1 us
    ppermute x42 -> x34, starting transfers between devices: 65.5 us -> 31.9 us  [swap(): return lax.ppermute(array, axis, [(i, i ^ step) for i in range(size)])]
    ppermute x42 -> x34, waiting for transfers between devices: 59 us -> 84.2 us  [swap(): return lax.ppermute(array, axis, [(i, i ^ step) for i in range(size)])]
    pallas_call x4, Pallas kernels: 23.1 us -> 29.2 us  [the longest x1 12.6 us: beam_early(): pl.pallas_call(functools.partial(early_body, places), grid=(total // tile...]
  transfers between devices with their start and end apart: 42 -> 34, of which waited for: 16 -> 14; matrix products, arithmetic and copies ran while one was open for 1% -> 0% of each run, Pallas kernels for 17% -> 19%
where the time goes in v1:
time: 167 us; the launch traced here: 165 us
  waiting for transfers between devices  84.2 us (50%)
  Pallas kernels  47.1 us (28%)
  starting transfers between devices  31.9 us (19%)
    ppermute x34, waiting for transfers between devices, swap(): return lax.ppermute(array, axis, [(i, i ^ step) for i in range(size)])  84.2 us
    ppermute x34, starting transfers between devices, swap(): return lax.ppermute(array, axis, [(i, i ^ step) for i in range(size)])  31.9 us
    pallas_call x4, Pallas kernels, spectra_pair(): pl.pallas_call(functools.partial(spectra_body, (slots, taps, frames_out,...  17.9 us
    pallas_call x1, Pallas kernels, beam_early(): pl.pallas_call(functools.partial(early_body, places), grid=(total // tile...  12.6 us
    pallas_call x1, Pallas kernels, beam_late(): pl.pallas_call(functools.partial(late_body, places, tile, pitch), grid=(t...  11.5 us
  transfers between devices with their start and end apart: 34, of which 14 were waited for; matrix products, arithmetic and copies ran while one was open for 0% of the time, Pallas kernels for 19%

profile of v1, /device:TPU:0, one launch (start us, length us, event | category | flops | bytes accessed | tf_op | source)
XLA Modules:
  0.0 164.8 jit_solution(8390437654066168704)
XLA Ops:
  0.0 0.6 pad_add_fusion.info
  0.6 4.4 %spectra.4 = (bf16[2,16,5120]{2,1,0:T(8,128)(2,1)}, bf16[2,16,5120]{2,1,0:T(8,128)(2,1)}) custom-call(s32[2]{0:T(128)} %pad_add_fusion.info, bf16[16,2,4,168,128]{4,3,2,1,0:T(8,128)(2,1)} %bitcast.18, f32[12,256]{1,0:T(8,128)} %taps_ref.7, bf16[256,512]{1,0:T(8,128)(2,1)} %constant.14.table), custom_call_target="tpu_custom_call" | custom-call | flops 800000000 | bytes 4000000 | tf_op jit(solution)/shard_map/spectra/pallas_call | solution.py:134
  5.0 3.0 %collective-permute-start.3 = (bf16[2,16,5120]{2,1,0:T(8,128)(2,1)}, bf16[2,16,5120]{2,1,0:T(8,128)(2,1)S(1)}, u32[]{:S(2)}, u32[]{:S(2)}) collective-permute-start(bf16[2,16,5120]{2,1,0:T(8,128)(2,1)} %get-tuple-element.25.refs_0_), channel_id=1, source_target_pairs={{0,8},{8,0},{16,24},{24,16},{1,9},{9,1},{17,25},{25,17},{2,10},{10... | collective-permute-start | bytes 983048 | tf_op jit(solution)/shard_map/ppermute | solution.py:310
  8.0 1.5 collective-permute-start.4
  10.2 2.1 %mask.1 = (bf16[2,8,16,256]{3,2,1,0:T(8,128)(2,1)}, bf16[2,8,16,256]{3,2,1,0:T(8,128)(2,1)}, bf16[2,8,16,256]{3,2,1,0:T(8,128)(2,1)}, bf16[2,8,16,256]{3,2,1,0:T(8,128)(2,1)}) custom-call(s32[2]{0:T(128)} %pad_add_fusion.info, s32[1]{0:T(128)S(6)} %copy.8.count, s32[1,128]{1,0:T(1,128)} %bitcast.27, bf16[2,8,16,1024]{3,2,1,0:T(8,128)(2,1)} %bitcast.22), custom_call_target="tpu_custom_call" | custom-call | tf_op jit(solution)/shard_map/mask/pallas_call | solution.py:182
  12.3 0.5 collective-permute-start
  12.8 2.9 %collective-permute-start.2 = (bf16[2,8,16,256]{3,2,1,0:T(8,128)(2,1)}, bf16[2,8,16,256]{3,2,1,0:T(8,128)(2,1)S(1)}, u32[]{:S(2)}, u32[]{:S(2)}) collective-permute-start(bf16[2,8,16,256]{3,2,1,0:T(8,128)(2,1)} %get-tuple-element.22), channel_id=1, source_target_pairs={{0,24},{8,16},{16,8},{24,0},{1,25},{9,17},{17,9},{25,1},{2,26},{10... | collective-permute-start | bytes 393224 | tf_op jit(solution)/shard_map/ppermute | solution.py:310
  15.8 4.5 %spectra.5 = (bf16[2,16,5120]{2,1,0:T(8,128)(2,1)}, bf16[2,16,5120]{2,1,0:T(8,128)(2,1)}) custom-call(s32[2]{0:T(128)} %pad_add_fusion.info, bf16[16,2,4,168,128]{4,3,2,1,0:T(8,128)(2,1)} %bitcast.19, f32[12,256]{1,0:T(8,128)} %taps_ref.7, bf16[256,512]{1,0:T(8,128)(2,1)} %constant.14.table), custom_call_target="tpu_custom_call" | custom-call | flops 800000000 | bytes 4000000 | tf_op jit(solution)/shard_map/spectra/pallas_call | solution.py:134
  20.2 4.6 %spectra.6 = (bf16[2,16,5120]{2,1,0:T(8,128)(2,1)}, bf16[2,16,5120]{2,1,0:T(8,128)(2,1)}) custom-call(s32[2]{0:T(128)} %pad_add_fusion.info, bf16[16,2,4,168,128]{4,3,2,1,0:T(8,128)(2,1)} %bitcast.20, f32[12,256]{1,0:T(8,128)} %taps_ref.7, bf16[256,512]{1,0:T(8,128)(2,1)} %constant.14.table), custom_call_target="tpu_custom_call" | custom-call | flops 800000000 | bytes 4000000 | tf_op jit(solution)/shard_map/spectra/pallas_call | solution.py:134
  24.9 1.6 collective-permute-start.10
  26.8 2.6 %collective-permute-start.18 = (bf16[2,16,5120]{2,1,0:T(8,128)(2,1)}, bf16[2,16,5120]{2,1,0:T(8,128)(2,1)S(1)}, u32[]{:S(2)}, u32[]{:S(2)}) collective-permute-start(bf16[2,16,5120]{2,1,0:T(8,128)(2,1)} %get-tuple-element.29), channel_id=1, source_target_pairs={{0,4},{1,5},{2,6},{3,7},{4,0},{5,1},{6,2},{7,3},{8,12},{9,13},{10,... | collective-permute-start | bytes 983048 | tf_op jit(solution)/shard_map/ppermute | solution.py:310
  29.5 4.4 %spectra.7 = (bf16[2,16,5120]{2,1,0:T(8,128)(2,1)}, bf16[2,16,5120]{2,1,0:T(8,128)(2,1)}) custom-call(s32[2]{0:T(128)} %pad_add_fusion.info, bf16[16,2,4,168,128]{4,3,2,1,0:T(8,128)(2,1)} %bitcast.21, f32[12,256]{1,0:T(8,128)} %taps_ref.7, bf16[256,512]{1,0:T(8,128)(2,1)} %constant.14.table), custom_call_target="tpu_custom_call" | custom-call | flops 800000000 | bytes 4000000 | tf_op jit(solution)/shard_map/spectra/pallas_call | solution.py:134
  33.9 3.6 %collective-permute-start.26 = (bf16[2,16,5120]{2,1,0:T(8,128)(2,1)}, bf16[2,16,5120]{2,1,0:T(8,128)(2,1)S(1)}, u32[]{:S(2)}, u32[]{:S(2)}) collective-permute-start(bf16[2,16,5120]{2,1,0:T(8,128)(2,1)} %get-tuple-element.31), channel_id=1, source_target_pairs={{0,6},{1,7},{2,4},{3,5},{4,2},{5,3},{6,0},{7,1},{8,14},{9,15},{10,... | collective-permute-start | bytes 983048 | tf_op jit(solution)/shard_map/ppermute | solution.py:310
  37.6 11.6 %collective-permute-done.10.refs_8_ = bf16[2,16,5120]{2,1,0:T(8,128)(2,1)S(1)} collective-permute-done((bf16[2,16,5120]{2,1,0:T(8,128)(2,1)}, bf16[2,16,5120]{2,1,0:T(8,128)(2,1)S(1)}, u32[]{:S(2)}, u32[]{:S(2)}) %collective-permute-start.10) | collective-permute-done | bytes 327712 | tf_op jit(solution)/shard_map/ppermute | solution.py:310
  49.2 5.9 %collective-permute-done.14.refs_12_ = bf16[2,16,5120]{2,1,0:T(8,128)(2,1)S(1)} collective-permute-done((bf16[2,16,5120]{2,1,0:T(8,128)(2,1)S(1)}, bf16[2,16,5120]{2,1,0:T(8,128)(2,1)S(1)}, u32[]{:S(2)}, u32[]{:S(2)}) %collective-permute-start.14) | collective-permute-done | bytes 327712 | tf_op jit(solution)/shard_map/ppermute | solution.py:310
  55.1 0.5 collective-permute-start.5
  55.6 1.5 collective-permute-start.7
  57.2 15.3 %collective-permute-done.22.refs_20_ = bf16[2,16,5120]{2,1,0:T(8,128)(2,1)S(1)} collective-permute-done((bf16[2,16,5120]{2,1,0:T(8,128)(2,1)}, bf16[2,16,5120]{2,1,0:T(8,128)(2,1)S(1)}, u32[]{:S(2)}, u32[]{:S(2)}) %collective-permute-start.22) | collective-permute-done | bytes 327712 | tf_op jit(solution)/shard_map/ppermute | solution.py:310
  72.5 0.5 collective-permute-start.8
  73.0 1.5 collective-permute-start.11
  74.5 0.5 collective-permute-start.12
  75.0 1.5 collective-permute-start.15
  76.6 0.5 collective-permute-start.16
  77.1 5.9 %collective-permute-done.8.refs_6_ = bf16[2,16,5120]{2,1,0:T(8,128)(2,1)S(1)} collective-permute-done((bf16[2,16,5120]{2,1,0:T(8,128)(2,1)S(1)}, bf16[2,16,5120]{2,1,0:T(8,128)(2,1)S(1)}, u32[]{:S(2)}, u32[]{:S(2)}) %collective-permute-start.8) | collective-permute-done | bytes 327712 | tf_op jit(solution)/shard_map/ppermute | solution.py:310
  83.0 0.5 collective-permute-start.19
  83.6 6.6 %collective-permute-done.11.refs_9_ = bf16[2,16,5120]{2,1,0:T(8,128)(2,1)} collective-permute-done((bf16[2,16,5120]{2,1,0:T(8,128)(2,1)S(1)}, bf16[2,16,5120]{2,1,0:T(8,128)(2,1)}, u32[]{:S(2)}, u32[]{:S(2)}) %collective-permute-start.11) | collective-permute-done | bytes 327712 | tf_op jit(solution)/shard_map/ppermute | solution.py:310
  90.2 0.5 collective-permute-start.20
  90.7 1.5 collective-permute-start.23
  92.2 0.5 collective-permute-start.24
  92.7 4.3 %collective-permute-done.16.refs_14_ = bf16[2,16,5120]{2,1,0:T(8,128)(2,1)S(1)} collective-permute-done((bf16[2,16,5120]{2,1,0:T(8,128)(2,1)S(1)}, bf16[2,16,5120]{2,1,0:T(8,128)(2,1)S(1)}, u32[]{:S(2)}, u32[]{:S(2)}) %collective-permute-start.16) | collective-permute-done | bytes 327712 | tf_op jit(solution)/shard_map/ppermute | solution.py:310
  97.1 0.5 collective-permute-start.27
  97.6 6.6 %collective-permute-done.19.refs_17_ = bf16[2,16,5120]{2,1,0:T(8,128)(2,1)} collective-permute-done((bf16[2,16,5120]{2,1,0:T(8,128)(2,1)S(1)}, bf16[2,16,5120]{2,1,0:T(8,128)(2,1)}, u32[]{:S(2)}, u32[]{:S(2)}) %collective-permute-start.19) | collective-permute-done | bytes 327712 | tf_op jit(solution)/shard_map/ppermute | solution.py:310
  104.7 0.6 collective-permute-start.9
  105.3 1.8 %collective-permute-done.23.refs_21_ = bf16[2,16,5120]{2,1,0:T(8,128)(2,1)} collective-permute-done((bf16[2,16,5120]{2,1,0:T(8,128)(2,1)S(1)}, bf16[2,16,5120]{2,1,0:T(8,128)(2,1)}, u32[]{:S(2)}, u32[]{:S(2)}) %collective-permute-start.23) | collective-permute-done | bytes 327712 | tf_op jit(solution)/shard_map/ppermute | solution.py:310
  107.1 0.5 collective-permute-start.13
  107.6 3.5 %collective-permute-done.24.refs_22_ = bf16[2,16,5120]{2,1,0:T(8,128)(2,1)S(1)} collective-permute-done((bf16[2,16,5120]{2,1,0:T(8,128)(2,1)S(1)}, bf16[2,16,5120]{2,1,0:T(8,128)(2,1)S(1)}, u32[]{:S(2)}, u32[]{:S(2)}) %collective-permute-start.24) | collective-permute-done | bytes 327712 | tf_op jit(solution)/shard_map/ppermute | solution.py:310
  111.1 0.5 collective-permute-start.17
  111.7 6.5 %collective-permute-done.27.refs_1_ = bf16[2,16,5120]{2,1,0:T(8,128)(2,1)S(1)} collective-permute-done((bf16[2,16,5120]{2,1,0:T(8,128)(2,1)S(1)}, bf16[2,16,5120]{2,1,0:T(8,128)(2,1)S(1)}, u32[]{:S(2)}, u32[]{:S(2)}) %collective-permute-start.27) | collective-permute-done | bytes 327712 | tf_op jit(solution)/shard_map/ppermute | solution.py:310
  118.7 0.6 collective-permute-start.25
  119.4 3.0 %turn.1 = (bf16[2,256,768]{2,1,0:T(8,128)(2,1)}, bf16[2,256,256]{2,1,0:T(8,128)(2,1)}) custom-call(bf16[2,128,256]{2,1,0:T(8,128)(2,1)} %bitcast.23, bf16[2,128,256]{2,1,0:T(8,128)(2,1)} %bitcast.24, bf16[2,128,256]{2,1,0:T(8,128)(2,1)} %bitcast.25, bf16[2,128,256]{2,1,0:T(8,128)(2,1)} %bitcast.26), custom_call_target="tpu_custom_call" | custom-call | tf_op jit(solution)/shard_map/turn/pallas_call | solution.py:210
  122.4 2.9 %collective-permute-done.9.refs_7_ = bf16[2,16,5120]{2,1,0:T(8,128)(2,1)} collective-permute-done((bf16[2,16,5120]{2,1,0:T(8,128)(2,1)}, bf16[2,16,5120]{2,1,0:T(8,128)(2,1)}, u32[]{:S(2)}, u32[]{:S(2)}) %collective-permute-start.9) | collective-permute-done | bytes 327712 | tf_op jit(solution)/shard_map/ppermute | solution.py:310
  125.8 0.6 collective-permute-start.32
  126.3 5.9 %collective-permute-done.17.refs_15_ = bf16[2,16,5120]{2,1,0:T(8,128)(2,1)} collective-permute-done((bf16[2,16,5120]{2,1,0:T(8,128)(2,1)}, bf16[2,16,5120]{2,1,0:T(8,128)(2,1)}, u32[]{:S(2)}, u32[]{:S(2)}) %collective-permute-start.17) | collective-permute-done | bytes 327712 | tf_op jit(solution)/shard_map/ppermute | solution.py:310
  132.8 0.6 collective-permute-start.33
  133.4 5.9 %collective-permute-done.25.refs_23_ = bf16[2,16,5120]{2,1,0:T(8,128)(2,1)} collective-permute-done((bf16[2,16,5120]{2,1,0:T(8,128)(2,1)}, bf16[2,16,5120]{2,1,0:T(8,128)(2,1)}, u32[]{:S(2)}, u32[]{:S(2)}) %collective-permute-start.25) | collective-permute-done | bytes 327712 | tf_op jit(solution)/shard_map/ppermute | solution.py:310
  139.4 12.6 %early.1.partial = f32[2,256,5120]{2,1,0:T(8,128)} custom-call(bf16[2,256,768]{2,1,0:T(8,128)(2,1)} %get-tuple-element.24.weights, bf16[2,16,5120]{2,1,0:T(8,128)(2,1)} %get-tuple-element.25.refs_0_, bf16[2,16,5120]{2,1,0:T(8,128)(2,1)} %copy-done, bf16[2,16,5120]{2,1,0:T(8,128)(2,1)} %copy-done.1, bf16[2,16,5120]{2,1,0:T(8,128)(2,1)} %copy-done.9, ...), custom_call_target="tpu_custom_call" | custom-call | flops 4026531840 | bytes 18350080 | tf_op jit(solution)/shard_map/early/pallas_call | solution.py:274
  152.0 1.3 collective-permute-done.33.refs_7_
  153.4 11.5 %late.1 = bf16[256,80,128]{2,1,0:T(8,128)(2,1)} custom-call(bf16[2,256,256]{2,1,0:T(8,128)(2,1)} %get-tuple-element.23.weights, f32[2,256,5120]{2,1,0:T(8,128)} %early.1.partial, bf16[2,16,5120]{2,1,0:T(8,128)(2,1)} %copy-done.4, bf16[2,16,5120]{2,1,0:T(8,128)(2,1)} %copy-done.13, bf16[2,16,5120]{2,1,0:T(8,128)(2,1)} %collective-permute-done.28.refs_2_, ...), custom_call_target="tpu_custom_call" | custom-call | flops 1342177280 | bytes 13107200 | tf_op jit(solution)/shard_map/late/pallas_call | solution.py:293
  (73 shorter events, 2.6 us)
Async XLA Ops:
  5.0 21.8 %collective-permute-start.3 = (bf16[2,16,5120]{2,1,0:T(8,128)(2,1)}, bf16[2,16,5120]{2,1,0:T(8,128)(2,1)S(1)}, u32[]{:S(2)}, u32[]{:S(2)}) collective-permute-start(bf16[2,16,5120]{2,1,0:T(8,128)(2,1)} %get-tuple-element.25.refs_0_), channel_id=1, source_target_pairs={{0,8},{8,0},{16,24},{24,16},{1,9},{9,1},{17,25},{25,17},{2,10},{10... | collective-permute-start | bytes 983048 | tf_op jit(solution)/shard_map/ppermute | solution.py:310
  8.0 21.4 %collective-permute-start.4 = (bf16[2,16,5120]{2,1,0:T(8,128)(2,1)}, bf16[2,16,5120]{2,1,0:T(8,128)(2,1)S(1)}, u32[]{:S(2)}, u32[]{:S(2)}) collective-permute-start(bf16[2,16,5120]{2,1,0:T(8,128)(2,1)} %get-tuple-element.25.refs_0_), channel_id=1, source_target_pairs={{0,16},{8,24},{16,0},{24,8},{1,17},{9,25},{17,1},{25,9},{2,18},{10... | collective-permute-start | bytes 983048 | tf_op jit(solution)/shard_map/ppermute | solution.py:310
  12.3 12.5 %collective-permute-start = (bf16[2,8,16,256]{3,2,1,0:T(8,128)(2,1)}, bf16[2,8,16,256]{3,2,1,0:T(8,128)(2,1)S(1)}, u32[]{:S(2)}, u32[]{:S(2)}) collective-permute-start(bf16[2,8,16,256]{3,2,1,0:T(8,128)(2,1)} %get-tuple-element.20), channel_id=1, source_target_pairs={{0,8},{8,0},{16,24},{24,16},{1,9},{9,1},{17,25},{25,17},{2,10},{10... | collective-permute-start | bytes 393224 | tf_op jit(solution)/shard_map/ppermute | solution.py:310
  12.8 12.1 %collective-permute-start.1 = (bf16[2,8,16,256]{3,2,1,0:T(8,128)(2,1)}, bf16[2,8,16,256]{3,2,1,0:T(8,128)(2,1)S(1)}, u32[]{:S(2)}, u32[]{:S(2)}) collective-permute-start(bf16[2,8,16,256]{3,2,1,0:T(8,128)(2,1)} %get-tuple-element.21), channel_id=1, source_target_pairs={{0,16},{8,24},{16,0},{24,8},{1,17},{9,25},{17,1},{25,9},{2,18},{10... | collective-permute-start | bytes 393224 | tf_op jit(solution)/shard_map/ppermute | solution.py:310
  12.8 13.7 %collective-permute-start.2 = (bf16[2,8,16,256]{3,2,1,0:T(8,128)(2,1)}, bf16[2,8,16,256]{3,2,1,0:T(8,128)(2,1)S(1)}, u32[]{:S(2)}, u32[]{:S(2)}) collective-permute-start(bf16[2,8,16,256]{3,2,1,0:T(8,128)(2,1)} %get-tuple-element.22), channel_id=1, source_target_pairs={{0,24},{8,16},{16,8},{24,0},{1,25},{9,17},{17,9},{25,1},{2,26},{10... | collective-permute-start | bytes 393224 | tf_op jit(solution)/shard_map/ppermute | solution.py:310
  24.8 94.6 %copy-start.17 = (bf16[2,8,16,256]{3,2,1,0:T(8,128)(2,1)}, bf16[2,8,16,256]{3,2,1,0:T(8,128)(2,1)S(1)}, u32[]{:S(2)}) copy-start(bf16[2,8,16,256]{3,2,1,0:T(8,128)(2,1)S(1)} %collective-permute-done) | copy-start | bytes 393220
  24.8 9.1 %collective-permute-start.6 = (bf16[2,16,5120]{2,1,0:T(8,128)(2,1)S(1)}, bf16[2,16,5120]{2,1,0:T(8,128)(2,1)S(1)}, u32[]{:S(2)}, u32[]{:S(2)}) collective-permute-start(bf16[2,16,5120]{2,1,0:T(8,128)(2,1)S(1)} %copy-done.20), channel_id=1, source_target_pairs={{0,1},{1,0},{2,3},{3,2},{4,5},{5,4},{6,7},{7,6},{8,9},{9,8},{10,11... | collective-permute-start | bytes 983048 | tf_op jit(solution)/shard_map/ppermute | solution.py:310
  24.9 94.5 %copy-start.18 = (bf16[2,8,16,256]{3,2,1,0:T(8,128)(2,1)}, bf16[2,8,16,256]{3,2,1,0:T(8,128)(2,1)S(1)}, u32[]{:S(2)}) copy-start(bf16[2,8,16,256]{3,2,1,0:T(8,128)(2,1)S(1)} %collective-permute-done.1) | copy-start | bytes 393220
  24.9 24.3 %collective-permute-start.10 = (bf16[2,16,5120]{2,1,0:T(8,128)(2,1)}, bf16[2,16,5120]{2,1,0:T(8,128)(2,1)S(1)}, u32[]{:S(2)}, u32[]{:S(2)}) collective-permute-start(bf16[2,16,5120]{2,1,0:T(8,128)(2,1)} %get-tuple-element.27), channel_id=1, source_target_pairs={{0,2},{1,3},{2,0},{3,1},{4,6},{5,7},{6,4},{7,5},{8,10},{9,11},{10,... | collective-permute-start | bytes 983048 | tf_op jit(solution)/shard_map/ppermute | solution.py:310
  26.6 28.6 %collective-permute-start.14 = (bf16[2,16,5120]{2,1,0:T(8,128)(2,1)S(1)}, bf16[2,16,5120]{2,1,0:T(8,128)(2,1)S(1)}, u32[]{:S(2)}, u32[]{:S(2)}) collective-permute-start(bf16[2,16,5120]{2,1,0:T(8,128)(2,1)S(1)} %copy-done.21), channel_id=1, source_target_pairs={{0,3},{1,2},{2,1},{3,0},{4,7},{5,6},{6,5},{7,4},{8,11},{9,10},{10,... | collective-permute-start | bytes 983048 | tf_op jit(solution)/shard_map/ppermute | solution.py:310
  26.8 112.5 %copy-start = (bf16[2,16,5120]{2,1,0:T(8,128)(2,1)}, bf16[2,16,5120]{2,1,0:T(8,128)(2,1)S(1)}, u32[]{:S(2)}) copy-start(bf16[2,16,5120]{2,1,0:T(8,128)(2,1)S(1)} %collective-permute-done.3.refs_1_) | copy-start | bytes 983044
  26.8 28.8 %collective-permute-start.18 = (bf16[2,16,5120]{2,1,0:T(8,128)(2,1)}, bf16[2,16,5120]{2,1,0:T(8,128)(2,1)S(1)}, u32[]{:S(2)}, u32[]{:S(2)}) collective-permute-start(bf16[2,16,5120]{2,1,0:T(8,128)(2,1)} %get-tuple-element.29), channel_id=1, source_target_pairs={{0,4},{1,5},{2,6},{3,7},{4,0},{5,1},{6,2},{7,3},{8,12},{9,13},{10,... | collective-permute-start | bytes 983048 | tf_op jit(solution)/shard_map/ppermute | solution.py:310
  29.4 109.9 %copy-start.1 = (bf16[2,16,5120]{2,1,0:T(8,128)(2,1)}, bf16[2,16,5120]{2,1,0:T(8,128)(2,1)S(1)}, u32[]{:S(2)}) copy-start(bf16[2,16,5120]{2,1,0:T(8,128)(2,1)S(1)} %collective-permute-done.4.refs_2_) | copy-start | bytes 983044
  29.4 43.1 %collective-permute-start.22 = (bf16[2,16,5120]{2,1,0:T(8,128)(2,1)}, bf16[2,16,5120]{2,1,0:T(8,128)(2,1)S(1)}, u32[]{:S(2)}, u32[]{:S(2)}) collective-permute-start(bf16[2,16,5120]{2,1,0:T(8,128)(2,1)} %get-tuple-element.30), channel_id=1, source_target_pairs={{0,5},{1,4},{2,7},{3,6},{4,1},{5,0},{6,3},{7,2},{8,13},{9,12},{10,... | collective-permute-start | bytes 983048 | tf_op jit(solution)/shard_map/ppermute | solution.py:310
  33.9 105.4 %copy-start.2 = (bf16[2,16,5120]{2,1,0:T(8,128)(2,1)}, bf16[2,16,5120]{2,1,0:T(8,128)(2,1)S(1)}, u32[]{:S(2)}) copy-start(bf16[2,16,5120]{2,1,0:T(8,128)(2,1)S(1)} %collective-permute-done.6.refs_4_) | copy-start | bytes 983044
  33.9 39.1 %collective-permute-start.26 = (bf16[2,16,5120]{2,1,0:T(8,128)(2,1)}, bf16[2,16,5120]{2,1,0:T(8,128)(2,1)S(1)}, u32[]{:S(2)}, u32[]{:S(2)}) collective-permute-start(bf16[2,16,5120]{2,1,0:T(8,128)(2,1)} %get-tuple-element.31), channel_id=1, source_target_pairs={{0,6},{1,7},{2,4},{3,5},{4,2},{5,3},{6,0},{7,1},{8,14},{9,15},{10,... | collective-permute-start | bytes 983048 | tf_op jit(solution)/shard_map/ppermute | solution.py:310
  49.2 90.1 %copy-start.3 = (bf16[2,16,5120]{2,1,0:T(8,128)(2,1)}, bf16[2,16,5120]{2,1,0:T(8,128)(2,1)S(1)}, u32[]{:S(2)}) copy-start(bf16[2,16,5120]{2,1,0:T(8,128)(2,1)S(1)} %collective-permute-done.10.refs_8_) | copy-start | bytes 983044
  49.2 25.3 %collective-permute-start.30 = (bf16[2,16,5120]{2,1,0:T(8,128)(2,1)}, bf16[2,16,5120]{2,1,0:T(8,128)(2,1)S(1)}, u32[]{:S(2)}, u32[]{:S(2)}) collective-permute-start(bf16[2,16,5120]{2,1,0:T(8,128)(2,1)} %get-tuple-element.32), channel_id=1, source_target_pairs={{0,7},{1,6},{2,5},{3,4},{4,3},{5,2},{6,1},{7,0},{8,15},{9,14},{10,... | collective-permute-start | bytes 983048 | tf_op jit(solution)/shard_map/ppermute | solution.py:310
  55.1 84.2 %copy-start.5 = (bf16[2,16,5120]{2,1,0:T(8,128)(2,1)}, bf16[2,16,5120]{2,1,0:T(8,128)(2,1)S(1)}, u32[]{:S(2)}) copy-start(bf16[2,16,5120]{2,1,0:T(8,128)(2,1)S(1)} %collective-permute-done.14.refs_12_) | copy-start | bytes 983044
  55.1 19.9 %collective-permute-start.5 = (bf16[2,16,5120]{2,1,0:T(8,128)(2,1)S(1)}, bf16[2,16,5120]{2,1,0:T(8,128)(2,1)S(1)}, u32[]{:S(2)}, u32[]{:S(2)}) collective-permute-start(bf16[2,16,5120]{2,1,0:T(8,128)(2,1)S(1)} %collective-permute-done.3.refs_1_), channel_id=1, source_target_pairs={{0,16},{8,24},{16,0},{24,8},{1,17},{9,25},{17,1},{25,9},{2,18},{10... | collective-permute-start | bytes 983048 | tf_op jit(solution)/shard_map/ppermute | solution.py:310
  55.6 83.7 %copy-start.7 = (bf16[2,16,5120]{2,1,0:T(8,128)(2,1)}, bf16[2,16,5120]{2,1,0:T(8,128)(2,1)S(1)}, u32[]{:S(2)}) copy-start(bf16[2,16,5120]{2,1,0:T(8,128)(2,1)S(1)} %collective-permute-done.18.refs_16_) | copy-start | bytes 983044
  55.6 20.9 %collective-permute-start.7 = (bf16[2,16,5120]{2,1,0:T(8,128)(2,1)S(1)}, bf16[2,16,5120]{2,1,0:T(8,128)(2,1)}, u32[]{:S(2)}, u32[]{:S(2)}) collective-permute-start(bf16[2,16,5120]{2,1,0:T(8,128)(2,1)S(1)} %collective-permute-done.6.refs_4_), channel_id=1, source_target_pairs={{0,16},{8,24},{16,0},{24,8},{1,17},{9,25},{17,1},{25,9},{2,18},{10... | collective-permute-start | bytes 983048 | tf_op jit(solution)/shard_map/ppermute | solution.py:310
  72.5 66.9 %copy-start.8 = (bf16[2,16,5120]{2,1,0:T(8,128)(2,1)}, bf16[2,16,5120]{2,1,0:T(8,128)(2,1)S(1)}, u32[]{:S(2)}) copy-start(bf16[2,16,5120]{2,1,0:T(8,128)(2,1)S(1)} %collective-permute-done.22.refs_20_) | copy-start | bytes 983044
  72.5 10.5 %collective-permute-start.8 = (bf16[2,16,5120]{2,1,0:T(8,128)(2,1)S(1)}, bf16[2,16,5120]{2,1,0:T(8,128)(2,1)S(1)}, u32[]{:S(2)}, u32[]{:S(2)}) collective-permute-start(bf16[2,16,5120]{2,1,0:T(8,128)(2,1)S(1)} %collective-permute-done.6.refs_4_), channel_id=1, source_target_pairs={{0,8},{8,0},{16,24},{24,16},{1,9},{9,1},{17,25},{25,17},{2,10},{10... | collective-permute-start | bytes 983048 | tf_op jit(solution)/shard_map/ppermute | solution.py:310
  73.0 79.0 %copy-start.4 = (bf16[2,16,5120]{2,1,0:T(8,128)(2,1)}, bf16[2,16,5120]{2,1,0:T(8,128)(2,1)S(1)}, u32[]{:S(2)}) copy-start(bf16[2,16,5120]{2,1,0:T(8,128)(2,1)S(1)} %collective-permute-done.26.refs_0_) | copy-start | bytes 983044
  73.0 17.1 %collective-permute-start.11 = (bf16[2,16,5120]{2,1,0:T(8,128)(2,1)S(1)}, bf16[2,16,5120]{2,1,0:T(8,128)(2,1)}, u32[]{:S(2)}, u32[]{:S(2)}) collective-permute-start(bf16[2,16,5120]{2,1,0:T(8,128)(2,1)S(1)} %collective-permute-done.10.refs_8_), channel_id=1, source_target_pairs={{0,8},{8,0},{16,24},{24,16},{1,9},{9,1},{17,25},{25,17},{2,10},{10... | collective-permute-start | bytes 983048 | tf_op jit(solution)/shard_map/ppermute | solution.py:310
  74.5 77.5 %copy-start.6 = (bf16[2,16,5120]{2,1,0:T(8,128)(2,1)}, bf16[2,16,5120]{2,1,0:T(8,128)(2,1)S(1)}, u32[]{:S(2)}) copy-start(bf16[2,16,5120]{2,1,0:T(8,128)(2,1)S(1)} %collective-permute-done.30.refs_4_) | copy-start | bytes 983044
  74.5 16.1 %collective-permute-start.12 = (bf16[2,16,5120]{2,1,0:T(8,128)(2,1)S(1)}, bf16[2,16,5120]{2,1,0:T(8,128)(2,1)S(1)}, u32[]{:S(2)}, u32[]{:S(2)}) collective-permute-start(bf16[2,16,5120]{2,1,0:T(8,128)(2,1)S(1)} %collective-permute-done.10.refs_8_), channel_id=1, source_target_pairs={{0,16},{8,24},{16,0},{24,8},{1,17},{9,25},{17,1},{25,9},{2,18},{10... | collective-permute-start | bytes 983048 | tf_op jit(solution)/shard_map/ppermute | solution.py:310
  75.0 64.3 %copy-start.9 = (bf16[2,16,5120]{2,1,0:T(8,128)(2,1)}, bf16[2,16,5120]{2,1,0:T(8,128)(2,1)S(1)}, u32[]{:S(2)}) copy-start(bf16[2,16,5120]{2,1,0:T(8,128)(2,1)S(1)} %collective-permute-done.5.refs_3_) | copy-start | bytes 983044
  75.0 17.2 %collective-permute-start.15 = (bf16[2,16,5120]{2,1,0:T(8,128)(2,1)S(1)}, bf16[2,16,5120]{2,1,0:T(8,128)(2,1)}, u32[]{:S(2)}, u32[]{:S(2)}) collective-permute-start(bf16[2,16,5120]{2,1,0:T(8,128)(2,1)S(1)} %collective-permute-done.14.refs_12_), channel_id=1, source_target_pairs={{0,16},{8,24},{16,0},{24,8},{1,17},{9,25},{17,1},{25,9},{2,18},{10... | collective-permute-start | bytes 983048 | tf_op jit(solution)/shard_map/ppermute | solution.py:310
  76.6 20.5 %collective-permute-start.16 = (bf16[2,16,5120]{2,1,0:T(8,128)(2,1)S(1)}, bf16[2,16,5120]{2,1,0:T(8,128)(2,1)S(1)}, u32[]{:S(2)}, u32[]{:S(2)}) collective-permute-start(bf16[2,16,5120]{2,1,0:T(8,128)(2,1)S(1)} %collective-permute-done.14.refs_12_), channel_id=1, source_target_pairs={{0,8},{8,0},{16,24},{24,16},{1,9},{9,1},{17,25},{25,17},{2,10},{10... | collective-permute-start | bytes 983048 | tf_op jit(solution)/shard_map/ppermute | solution.py:310
  83.0 35.6 %copy-start.10 = (bf16[2,16,5120]{2,1,0:T(8,128)(2,1)}, bf16[2,16,5120]{2,1,0:T(8,128)(2,1)S(1)}, u32[]{:S(2)}) copy-start(bf16[2,16,5120]{2,1,0:T(8,128)(2,1)S(1)} %collective-permute-done.8.refs_6_) | copy-start | bytes 983044
  83.0 21.2 %collective-permute-start.19 = (bf16[2,16,5120]{2,1,0:T(8,128)(2,1)S(1)}, bf16[2,16,5120]{2,1,0:T(8,128)(2,1)}, u32[]{:S(2)}, u32[]{:S(2)}) collective-permute-start(bf16[2,16,5120]{2,1,0:T(8,128)(2,1)S(1)} %collective-permute-done.18.refs_16_), channel_id=1, source_target_pairs={{0,8},{8,0},{16,24},{24,16},{1,9},{9,1},{17,25},{25,17},{2,10},{10... | collective-permute-start | bytes 983048 | tf_op jit(solution)/shard_map/ppermute | solution.py:310
  90.2 14.6 %collective-permute-start.20 = (bf16[2,16,5120]{2,1,0:T(8,128)(2,1)S(1)}, bf16[2,16,5120]{2,1,0:T(8,128)(2,1)S(1)}, u32[]{:S(2)}, u32[]{:S(2)}) collective-permute-start(bf16[2,16,5120]{2,1,0:T(8,128)(2,1)S(1)} %collective-permute-done.18.refs_16_), channel_id=1, source_target_pairs={{0,16},{8,24},{16,0},{24,8},{1,17},{9,25},{17,1},{25,9},{2,18},{10... | collective-permute-start | bytes 983048 | tf_op jit(solution)/shard_map/ppermute | solution.py:310
  90.7 28.6 %copy-start.11 = (bf16[2,16,5120]{2,1,0:T(8,128)(2,1)}, bf16[2,16,5120]{2,1,0:T(8,128)(2,1)S(1)}, u32[]{:S(2)}) copy-start(bf16[2,16,5120]{2,1,0:T(8,128)(2,1)S(1)} %collective-permute-done.12.refs_10_) | copy-start | bytes 983044
  90.7 16.4 %collective-permute-start.23 = (bf16[2,16,5120]{2,1,0:T(8,128)(2,1)S(1)}, bf16[2,16,5120]{2,1,0:T(8,128)(2,1)}, u32[]{:S(2)}, u32[]{:S(2)}) collective-permute-start(bf16[2,16,5120]{2,1,0:T(8,128)(2,1)S(1)} %collective-permute-done.22.refs_20_), channel_id=1, source_target_pairs={{0,16},{8,24},{16,0},{24,8},{1,17},{9,25},{17,1},{25,9},{2,18},{10... | collective-permute-start | bytes 983048 | tf_op jit(solution)/shard_map/ppermute | solution.py:310
  92.2 18.9 %collective-permute-start.24 = (bf16[2,16,5120]{2,1,0:T(8,128)(2,1)S(1)}, bf16[2,16,5120]{2,1,0:T(8,128)(2,1)S(1)}, u32[]{:S(2)}, u32[]{:S(2)}) collective-permute-start(bf16[2,16,5120]{2,1,0:T(8,128)(2,1)S(1)} %collective-permute-done.22.refs_20_), channel_id=1, source_target_pairs={{0,8},{8,0},{16,24},{24,16},{1,9},{9,1},{17,25},{25,17},{2,10},{10... | collective-permute-start | bytes 983048 | tf_op jit(solution)/shard_map/ppermute | solution.py:310
  97.1 21.1 %collective-permute-start.27 = (bf16[2,16,5120]{2,1,0:T(8,128)(2,1)S(1)}, bf16[2,16,5120]{2,1,0:T(8,128)(2,1)S(1)}, u32[]{:S(2)}, u32[]{:S(2)}) collective-permute-start(bf16[2,16,5120]{2,1,0:T(8,128)(2,1)S(1)} %collective-permute-done.26.refs_0_), channel_id=1, source_target_pairs={{0,8},{8,0},{16,24},{24,16},{1,9},{9,1},{17,25},{25,17},{2,10},{10... | collective-permute-start | bytes 983048 | tf_op jit(solution)/shard_map/ppermute | solution.py:310
  104.2 14.4 %collective-permute-start.31 = (bf16[2,16,5120]{2,1,0:T(8,128)(2,1)S(1)}, bf16[2,16,5120]{2,1,0:T(8,128)(2,1)S(1)}, u32[]{:S(2)}, u32[]{:S(2)}) collective-permute-start(bf16[2,16,5120]{2,1,0:T(8,128)(2,1)S(1)} %collective-permute-done.30.refs_4_), channel_id=1, source_target_pairs={{0,16},{8,24},{16,0},{24,8},{1,17},{9,25},{17,1},{25,9},{2,18},{10... | collective-permute-start | bytes 983048 | tf_op jit(solution)/shard_map/ppermute | solution.py:310
  104.7 20.6 %collective-permute-start.9 = (bf16[2,16,5120]{2,1,0:T(8,128)(2,1)}, bf16[2,16,5120]{2,1,0:T(8,128)(2,1)}, u32[]{:S(2)}, u32[]{:S(2)}) collective-permute-start(bf16[2,16,5120]{2,1,0:T(8,128)(2,1)} %collective-permute-done.7.refs_5_), channel_id=1, source_target_pairs={{0,8},{8,0},{16,24},{24,16},{1,9},{9,1},{17,25},{25,17},{2,10},{10... | collective-permute-start | bytes 983048 | tf_op jit(solution)/shard_map/ppermute | solution.py:310
  107.1 18.7 %collective-permute-start.13 = (bf16[2,16,5120]{2,1,0:T(8,128)(2,1)}, bf16[2,16,5120]{2,1,0:T(8,128)(2,1)}, u32[]{:S(2)}, u32[]{:S(2)}) collective-permute-start(bf16[2,16,5120]{2,1,0:T(8,128)(2,1)} %collective-permute-done.11.refs_9_), channel_id=1, source_target_pairs={{0,16},{8,24},{16,0},{24,8},{1,17},{9,25},{17,1},{25,9},{2,18},{10... | collective-permute-start | bytes 983048 | tf_op jit(solution)/shard_map/ppermute | solution.py:310
  111.1 21.2 %collective-permute-start.17 = (bf16[2,16,5120]{2,1,0:T(8,128)(2,1)}, bf16[2,16,5120]{2,1,0:T(8,128)(2,1)}, u32[]{:S(2)}, u32[]{:S(2)}) collective-permute-start(bf16[2,16,5120]{2,1,0:T(8,128)(2,1)} %collective-permute-done.15.refs_13_), channel_id=1, source_target_pairs={{0,8},{8,0},{16,24},{24,16},{1,9},{9,1},{17,25},{25,17},{2,10},{10... | collective-permute-start | bytes 983048 | tf_op jit(solution)/shard_map/ppermute | solution.py:310
  118.1 14.7 %collective-permute-start.21 = (bf16[2,16,5120]{2,1,0:T(8,128)(2,1)}, bf16[2,16,5120]{2,1,0:T(8,128)(2,1)}, u32[]{:S(2)}, u32[]{:S(2)}) collective-permute-start(bf16[2,16,5120]{2,1,0:T(8,128)(2,1)} %collective-permute-done.19.refs_17_), channel_id=1, source_target_pairs={{0,16},{8,24},{16,0},{24,8},{1,17},{9,25},{17,1},{25,9},{2,18},{10... | collective-permute-start | bytes 983048 | tf_op jit(solution)/shard_map/ppermute | solution.py:310
  118.7 20.7 %collective-permute-start.25 = (bf16[2,16,5120]{2,1,0:T(8,128)(2,1)}, bf16[2,16,5120]{2,1,0:T(8,128)(2,1)}, u32[]{:S(2)}, u32[]{:S(2)}) collective-permute-start(bf16[2,16,5120]{2,1,0:T(8,128)(2,1)} %collective-permute-done.23.refs_21_), channel_id=1, source_target_pairs={{0,8},{8,0},{16,24},{24,16},{1,9},{9,1},{17,25},{25,17},{2,10},{10... | collective-permute-start | bytes 983048 | tf_op jit(solution)/shard_map/ppermute | solution.py:310
  125.3 26.7 %collective-permute-start.28 = (bf16[2,16,5120]{2,1,0:T(8,128)(2,1)S(1)}, bf16[2,16,5120]{2,1,0:T(8,128)(2,1)}, u32[]{:S(2)}, u32[]{:S(2)}) collective-permute-start(bf16[2,16,5120]{2,1,0:T(8,128)(2,1)S(1)} %collective-permute-done.26.refs_0_), channel_id=1, source_target_pairs={{0,16},{8,24},{16,0},{24,8},{1,17},{9,25},{17,1},{25,9},{2,18},{10... | collective-permute-start | bytes 983048 | tf_op jit(solution)/shard_map/ppermute | solution.py:310
  125.8 26.2 %collective-permute-start.32 = (bf16[2,16,5120]{2,1,0:T(8,128)(2,1)S(1)}, bf16[2,16,5120]{2,1,0:T(8,128)(2,1)}, u32[]{:S(2)}, u32[]{:S(2)}) collective-permute-start(bf16[2,16,5120]{2,1,0:T(8,128)(2,1)S(1)} %collective-permute-done.30.refs_4_), channel_id=1, source_target_pairs={{0,8},{8,0},{16,24},{24,16},{1,9},{9,1},{17,25},{25,17},{2,10},{10... | collective-permute-start | bytes 983048 | tf_op jit(solution)/shard_map/ppermute | solution.py:310
  132.3 19.7 %collective-permute-start.29 = (bf16[2,16,5120]{2,1,0:T(8,128)(2,1)}, bf16[2,16,5120]{2,1,0:T(8,128)(2,1)}, u32[]{:S(2)}, u32[]{:S(2)}) collective-permute-start(bf16[2,16,5120]{2,1,0:T(8,128)(2,1)} %copy-done.13), channel_id=1, source_target_pairs={{0,16},{8,24},{16,0},{24,8},{1,17},{9,25},{17,1},{25,9},{2,18},{10... | collective-permute-start | bytes 983048 | tf_op jit(solution)/shard_map/ppermute | solution.py:310
  132.8 20.6 %collective-permute-start.33 = (bf16[2,16,5120]{2,1,0:T(8,128)(2,1)}, bf16[2,16,5120]{2,1,0:T(8,128)(2,1)}, u32[]{:S(2)}, u32[]{:S(2)}) collective-permute-start(bf16[2,16,5120]{2,1,0:T(8,128)(2,1)} %copy-done.15), channel_id=1, source_target_pairs={{0,8},{8,0},{16,24},{24,16},{1,9},{9,1},{17,25},{25,17},{2,10},{10... | collective-permute-start | bytes 983048 | tf_op jit(solution)/shard_map/ppermute | solution.py:310
  (8 other events, 87.9 us)

commit v2 on v1

--- a/solution.py
+++ b/solution.py
@@ -11,6 +11,8 @@
 
 
 LANES = 128
+KERNEL_VMEM = 16 << 20
+VMEM_WHOLE = pl.BlockSpec(memory_space=pltpu.VMEM)
 
 
 def dft_table(fine):
@@ -150,7 +152,9 @@
             ],
         ),
         out_shape=shapes,
-        compiler_params=pltpu.CompilerParams(dimension_semantics=("arbitrary",)),
+        compiler_params=pltpu.CompilerParams(
+            dimension_semantics=("arbitrary",), vmem_limit_bytes=KERNEL_VMEM
+        ),
         cost_estimate=pl.CostEstimate(
             flops=8 * 10**8, bytes_accessed=4 * 10**6, transcendentals=0
         ),
@@ -185,6 +189,7 @@
         out_specs=[vmem] * stn,
         out_shape=[shape] * stn,
         scratch_shapes=[pltpu.VMEM((freq * slots, LANES), jnp.float32)],
+        compiler_params=pltpu.CompilerParams(vmem_limit_bytes=KERNEL_VMEM),
         name="mask",
     )(info, count, ids.reshape(1, freq * slots), weights)
 
@@ -213,34 +218,43 @@
             jax.ShapeDtypeStruct((2, width, 2 * len(parts) * size), jnp.bfloat16)
             for size in (cut, rows - cut)
         ],
+        compiler_params=pltpu.CompilerParams(vmem_limit_bytes=KERNEL_VMEM),
         name="turn",
     )(*parts)
 
 
-def gather_rows(places, pieces, data):
+def gather_rows(places, pieces, here, data):
     slots = pieces[0].shape[1]
     span = data.shape[0] // (2 * (max(g for g, _ in places) + 1))
     low = min(j for _, j in places)
     for (g, j), piece in zip(places, pieces):
         for q in range(2):
             row = (2 * g + q) * span + (j - low) * slots
-            data[row : row + slots, :] = piece[q]
-
-
-def early_body(places, weights, *refs):
+            data[row : row + slots, :] = piece[q, :, here]
+
+
+def columns(tile):
+    return pl.ds(pl.multiple_of(pl.program_id(0) * tile, tile), tile)
+
+
+def early_body(places, tile, weights, *refs):
     pieces, out, data = refs[: len(places)], refs[-2], refs[-1]
-    gather_rows(places, pieces, data)
+    here = columns(tile)
+    gather_rows(places, pieces, here, data)
     for q in range(2):
-        out[q] = jnp.dot(weights[q], data[...], preferred_element_type=jnp.float32)
+        out[q, :, here] = jnp.dot(
+            weights[q], data[...], preferred_element_type=jnp.float32
+        )
 
 
 def late_body(places, tile, pitch, weights, partial, *refs):
     pieces = refs[: len(places)]
     out, data, wide = refs[len(places) :]
-    gather_rows(places, pieces, data)
+    here = columns(tile)
+    gather_rows(places, pieces, here, data)
     beams = weights.shape[1]
     for q in range(2):
-        part = partial[q] + jnp.dot(
+        part = partial[q, :, here] + jnp.dot(
             weights[q], data[...], preferred_element_type=jnp.float32
         )
         for j in range(tile // LANES):
@@ -252,56 +266,41 @@
         out[b] = wide[pl.ds(b * pitch, high), :].astype(jnp.bfloat16)
 
 
-def beam_specs(weights, pieces, tile):
+def beam_early(weights, pieces, tile):
     _, beams, depth = weights.shape
-    _, slots, total = pieces[0][2].shape
-    specs = [pl.BlockSpec((2, beams, depth), lambda n: (0, 0, 0))]
-    parts = [pl.BlockSpec((2, slots, tile), lambda n: (0, 0, n))] * len(pieces)
-    sum_spec = pl.BlockSpec((2, beams, tile), lambda n: (0, 0, n))
-    cost = pl.CostEstimate(
-        flops=4 * beams * depth * total,
-        bytes_accessed=2 * (depth + 4 * beams) * total,
-        transcendentals=0,
-    )
-    places = [(g, j) for g, j, _ in pieces]
-    return beams, depth, total, specs, parts, sum_spec, cost, places
-
-
-def beam_early(weights, pieces, tile):
-    beams, depth, total, specs, parts, sum_spec, cost, places = beam_specs(
-        weights, pieces, tile
-    )
-    return pl.pallas_call(
-        functools.partial(early_body, places),
+    total = pieces[0][2].shape[2]
+    return pl.pallas_call(
+        functools.partial(early_body, [(g, j) for g, j, _ in pieces], tile),
         grid=(total // tile,),
-        in_specs=specs + parts,
-        out_specs=sum_spec,
+        in_specs=[VMEM_WHOLE] * (1 + len(pieces)),
+        out_specs=VMEM_WHOLE,
         out_shape=jax.ShapeDtypeStruct((2, beams, total), jnp.float32),
         scratch_shapes=[pltpu.VMEM((depth, tile), jnp.bfloat16)],
-        compiler_params=pltpu.CompilerParams(dimension_semantics=("arbitrary",)),
-        cost_estimate=cost,
+        compiler_params=pltpu.CompilerParams(
+            dimension_semantics=("arbitrary",), vmem_limit_bytes=KERNEL_VMEM
+        ),
         name="early",
     )(weights, *[piece for _, _, piece in pieces])
 
 
 def beam_late(weights, partial, pieces, tile):
-    beams, depth, total, specs, parts, sum_spec, cost, places = beam_specs(
-        weights, pieces, tile
-    )
+    _, beams, depth = weights.shape
+    total = pieces[0][2].shape[2]
     high = 2 * tile // LANES
     pitch = high + 1
     return pl.pallas_call(
-        functools.partial(late_body, places, tile, pitch),
+        functools.partial(late_body, [(g, j) for g, j, _ in pieces], tile, pitch),
         grid=(total // tile,),
-        in_specs=specs + [sum_spec] + parts,
+        in_specs=[VMEM_WHOLE] * (2 + len(pieces)),
         out_specs=pl.BlockSpec((beams, high, LANES), lambda n: (0, n, 0)),
         out_shape=jax.ShapeDtypeStruct((beams, 2 * total // LANES, LANES), jnp.bfloat16),
         scratch_shapes=[
             pltpu.VMEM((depth, tile), jnp.bfloat16),
             pltpu.VMEM((beams * pitch, LANES), jnp.float32),
         ],
-        compiler_params=pltpu.CompilerParams(dimension_semantics=("arbitrary",)),
-        cost_estimate=cost,
+        compiler_params=pltpu.CompilerParams(
+            dimension_semantics=("arbitrary",), vmem_limit_bytes=KERNEL_VMEM
+        ),
         name="late",
     )(weights, partial, *[piece for _, _, piece in pieces])
 
@@ -331,6 +330,7 @@
     view = view.transpose(0, 1, 2, 4, 3, 5).reshape(
         slots, polars, chans // 2, 4 * samples // LANES, LANES
     )
+    view = pltpu.with_memory_space_constraint(view, pltpu.HBM)
     table = cos_sin(fine)
     planes = freq // 2
     held = {}

time: 167 us -> 158 us (0.946)
  Pallas kernels: 47.1 us -> 28.3 us
  starting transfers between devices: 31.9 us -> 38.3 us
  waiting for transfers between devices: 84.2 us -> 88.2 us
    pallas_call x2, Pallas kernels: 24.1 us -> 11.9 us  [the longest x1 6.12 us: beam_late(): pl.pallas_call(functools.partial(late_body, [(g, j) for g, j, _ in pieces...]
    ppermute x34, starting transfers between devices: 31.9 us -> 38.3 us  [swap(): return lax.ppermute(array, axis, [(i, i ^ step) for i in range(size)])]
    ppermute x34, waiting for transfers between devices: 84.2 us -> 88.2 us  [swap(): return lax.ppermute(array, axis, [(i, i ^ step) for i in range(size)])]
    pallas_call x4, Pallas kernels: 17.9 us -> 14.5 us  [spectra_pair(): pl.pallas_call(functools.partial(spectra_body, (slots, taps, frames_out,...]
    pallas_call x1, Pallas kernels: 3.02 us -> 1.03 us  [turn_weights(): pl.pallas_call(functools.partial(turn_body, cut), out_shape=[jax.ShapeDty...]
  transfers between devices with their start and end apart: 34 -> 34, of which waited for: 14 -> 16; matrix products, arithmetic and copies ran while one was open for 0% -> 0% of each run, Pallas kernels for 19% -> 12%
where the time goes in v2:
time: 158 us; the launch traced here: 157 us
  waiting for transfers between devices  88.2 us (56%)
  starting transfers between devices  38.3 us (24%)
  Pallas kernels  28.3 us (18%)
  local copies, waits for them, and re-layouts  1.68 us (1%)
    ppermute x34, waiting for transfers between devices, swap(): return lax.ppermute(array, axis, [(i, i ^ step) for i in range(size)])  88.2 us
    ppermute x34, starting transfers between devices, swap(): return lax.ppermute(array, axis, [(i, i ^ step) for i in range(size)])  38.3 us
    pallas_call x4, Pallas kernels, spectra_pair(): pl.pallas_call(functools.partial(spectra_body, (slots, taps, frames_out,...  14.5 us
    pallas_call x1, Pallas kernels, beam_late(): pl.pallas_call(functools.partial(late_body, [(g, j) for g, j, _ in pieces...  6.12 us
    pallas_call x1, Pallas kernels, beam_early(): pl.pallas_call(functools.partial(early_body, [(g, j) for g, j, _ in piece...  5.81 us
  transfers between devices with their start and end apart: 34, of which 16 were waited for; matrix products, arithmetic and copies ran while one was open for 0% of the time, Pallas kernels for 12%

profile of v2, /device:TPU:0, one launch (start us, length us, event | category | flops | bytes accessed | tf_op | source)
XLA Modules:
  0.0 157.3 jit_solution(16138357044887632550)
XLA Ops:
  0.1 0.9 copy-done
  1.0 0.7 copy-done.3
  1.8 3.7 %spectra.4 = (bf16[2,16,5120]{2,1,0:T(8,128)(2,1)S(1)}, bf16[2,16,5120]{2,1,0:T(8,128)(2,1)S(1)}) custom-call(s32[2]{0:T(128)S(1)} %pad_add_fusion.info, bf16[16,2,4,168,128]{4,3,2,1,0:T(8,128)(2,1)} %bitcast.24, f32[12,256]{1,0:T(8,128)S(1)} %copy-done.3, bf16[256,512]{1,0:T(8,128)(2,1)S(1)} %copy-done), custom_call_target="tpu_custom_call" | custom-call | flops 800000000 | bytes 4000000 | tf_op jit(solution)/shard_map/spectra/pallas_call | solution.py:136
  5.5 3.0 %collective-permute-start.3 = (bf16[2,16,5120]{2,1,0:T(8,128)(2,1)S(1)}, bf16[2,16,5120]{2,1,0:T(8,128)(2,1)S(1)}, u32[]{:S(2)}, u32[]{:S(2)}) collective-permute-start(bf16[2,16,5120]{2,1,0:T(8,128)(2,1)S(1)} %get-tuple-element.25.refs_0_), channel_id=1, source_target_pairs={{0,8},{8,0},{16,24},{24,16},{1,9},{9,1},{17,25},{25,17},{2,10},{10... | collective-permute-start | bytes 983048 | tf_op jit(solution)/shard_map/ppermute | solution.py:309
  8.5 1.5 collective-permute-start.4
  10.7 0.8 mask.1
  11.5 0.6 collective-permute-start
  12.1 2.9 %collective-permute-start.2 = (bf16[2,8,16,256]{3,2,1,0:T(8,128)(2,1)S(1)}, bf16[2,8,16,256]{3,2,1,0:T(8,128)(2,1)S(1)}, u32[]{:S(2)}, u32[]{:S(2)}) collective-permute-start(bf16[2,8,16,256]{3,2,1,0:T(8,128)(2,1)S(1)} %get-tuple-element.22), channel_id=1, source_target_pairs={{0,24},{8,16},{16,8},{24,0},{1,25},{9,17},{17,9},{25,1},{2,26},{10... | collective-permute-start | bytes 393224 | tf_op jit(solution)/shard_map/ppermute | solution.py:309
  15.0 3.6 %spectra.5 = (bf16[2,16,5120]{2,1,0:T(8,128)(2,1)S(1)}, bf16[2,16,5120]{2,1,0:T(8,128)(2,1)S(1)}) custom-call(s32[2]{0:T(128)S(1)} %pad_add_fusion.info, bf16[16,2,4,168,128]{4,3,2,1,0:T(8,128)(2,1)} %bitcast.25, f32[12,256]{1,0:T(8,128)S(1)} %copy-done.4, bf16[256,512]{1,0:T(8,128)(2,1)S(1)} %copy-done.1), custom_call_target="tpu_custom_call" | custom-call | flops 800000000 | bytes 4000000 | tf_op jit(solution)/shard_map/spectra/pallas_call | solution.py:136
  18.7 3.6 %spectra.6 = (bf16[2,16,5120]{2,1,0:T(8,128)(2,1)S(1)}, bf16[2,16,5120]{2,1,0:T(8,128)(2,1)S(1)}) custom-call(s32[2]{0:T(128)S(1)} %pad_add_fusion.info, bf16[16,2,4,168,128]{4,3,2,1,0:T(8,128)(2,1)} %bitcast.26, f32[12,256]{1,0:T(8,128)S(1)} %copy-done.4, bf16[256,512]{1,0:T(8,128)(2,1)S(1)} %copy-done.1), custom_call_target="tpu_custom_call" | custom-call | flops 800000000 | bytes 4000000 | tf_op jit(solution)/shard_map/spectra/pallas_call | solution.py:136
  22.4 0.9 collective-permute-done.1
  23.3 1.6 %collective-permute-start.10 = (bf16[2,16,5120]{2,1,0:T(8,128)(2,1)S(1)}, bf16[2,16,5120]{2,1,0:T(8,128)(2,1)S(1)}, u32[]{:S(2)}, u32[]{:S(2)}) collective-permute-start(bf16[2,16,5120]{2,1,0:T(8,128)(2,1)S(1)} %get-tuple-element.27), channel_id=1, source_target_pairs={{0,2},{1,3},{2,0},{3,1},{4,6},{5,7},{6,4},{7,5},{8,10},{9,11},{10,... | collective-permute-start | bytes 983048 | tf_op jit(solution)/shard_map/ppermute | solution.py:309
  24.9 2.7 %collective-permute-start.18 = (bf16[2,16,5120]{2,1,0:T(8,128)(2,1)S(1)}, bf16[2,16,5120]{2,1,0:T(8,128)(2,1)S(1)}, u32[]{:S(2)}, u32[]{:S(2)}) collective-permute-start(bf16[2,16,5120]{2,1,0:T(8,128)(2,1)S(1)} %get-tuple-element.29), channel_id=1, source_target_pairs={{0,4},{1,5},{2,6},{3,7},{4,0},{5,1},{6,2},{7,3},{8,12},{9,13},{10,... | collective-permute-start | bytes 983048 | tf_op jit(solution)/shard_map/ppermute | solution.py:309
  27.5 3.6 %spectra.7 = (bf16[2,16,5120]{2,1,0:T(8,128)(2,1)S(1)}, bf16[2,16,5120]{2,1,0:T(8,128)(2,1)S(1)}) custom-call(s32[2]{0:T(128)S(1)} %pad_add_fusion.info, bf16[16,2,4,168,128]{4,3,2,1,0:T(8,128)(2,1)} %bitcast.27, f32[12,256]{1,0:T(8,128)S(1)} %copy-done.4, bf16[256,512]{1,0:T(8,128)(2,1)S(1)} %copy-done.1), custom_call_target="tpu_custom_call" | custom-call | flops 800000000 | bytes 4000000 | tf_op jit(solution)/shard_map/spectra/pallas_call | solution.py:136
  31.3 3.6 %collective-permute-start.26 = (bf16[2,16,5120]{2,1,0:T(8,128)(2,1)S(1)}, bf16[2,16,5120]{2,1,0:T(8,128)(2,1)S(1)}, u32[]{:S(2)}, u32[]{:S(2)}) collective-permute-start(bf16[2,16,5120]{2,1,0:T(8,128)(2,1)S(1)} %get-tuple-element.31), channel_id=1, source_target_pairs={{0,6},{1,7},{2,4},{3,5},{4,2},{5,3},{6,0},{7,1},{8,14},{9,15},{10,... | collective-permute-start | bytes 983048 | tf_op jit(solution)/shard_map/ppermute | solution.py:309
  34.9 11.6 %collective-permute-done.10.refs_8_ = bf16[2,16,5120]{2,1,0:T(8,128)(2,1)S(1)} collective-permute-done((bf16[2,16,5120]{2,1,0:T(8,128)(2,1)S(1)}, bf16[2,16,5120]{2,1,0:T(8,128)(2,1)S(1)}, u32[]{:S(2)}, u32[]{:S(2)}) %collective-permute-start.10) | collective-permute-done | bytes 327712 | tf_op jit(solution)/shard_map/ppermute | solution.py:309
  46.5 4.3 %collective-permute-done.14.refs_12_ = bf16[2,16,5120]{2,1,0:T(8,128)(2,1)S(1)} collective-permute-done((bf16[2,16,5120]{2,1,0:T(8,128)(2,1)S(1)}, bf16[2,16,5120]{2,1,0:T(8,128)(2,1)S(1)}, u32[]{:S(2)}, u32[]{:S(2)}) %collective-permute-start.14) | collective-permute-done | bytes 327712 | tf_op jit(solution)/shard_map/ppermute | solution.py:309
  50.8 2.0 %collective-permute-start.7 = (bf16[2,16,5120]{2,1,0:T(8,128)(2,1)S(1)}, bf16[2,16,5120]{2,1,0:T(8,128)(2,1)S(1)}, u32[]{:S(2)}, u32[]{:S(2)}) collective-permute-start(bf16[2,16,5120]{2,1,0:T(8,128)(2,1)S(1)} %collective-permute-done.6.refs_4_), channel_id=1, source_target_pairs={{0,16},{8,24},{16,0},{24,8},{1,17},{9,25},{17,1},{25,9},{2,18},{10... | collective-permute-start | bytes 983048 | tf_op jit(solution)/shard_map/ppermute | solution.py:309
  52.9 17.8 %collective-permute-done.22.refs_20_ = bf16[2,16,5120]{2,1,0:T(8,128)(2,1)S(1)} collective-permute-done((bf16[2,16,5120]{2,1,0:T(8,128)(2,1)S(1)}, bf16[2,16,5120]{2,1,0:T(8,128)(2,1)S(1)}, u32[]{:S(2)}, u32[]{:S(2)}) %collective-permute-start.22) | collective-permute-done | bytes 327712 | tf_op jit(solution)/shard_map/ppermute | solution.py:309
  70.6 0.9 collective-permute-start.8
  71.5 1.2 collective-permute-start.11
  72.6 1.5 collective-permute-start.12
  74.7 0.9 collective-permute-start.16
  75.6 5.6 %collective-permute-done.8.refs_6_ = bf16[2,16,5120]{2,1,0:T(8,128)(2,1)S(1)} collective-permute-done((bf16[2,16,5120]{2,1,0:T(8,128)(2,1)S(1)}, bf16[2,16,5120]{2,1,0:T(8,128)(2,1)S(1)}, u32[]{:S(2)}, u32[]{:S(2)}) %collective-permute-start.8) | collective-permute-done | bytes 327712 | tf_op jit(solution)/shard_map/ppermute | solution.py:309
  81.2 0.9 collective-permute-start.19
  82.1 6.2 %collective-permute-done.11.refs_9_ = bf16[2,16,5120]{2,1,0:T(8,128)(2,1)S(1)} collective-permute-done((bf16[2,16,5120]{2,1,0:T(8,128)(2,1)S(1)}, bf16[2,16,5120]{2,1,0:T(8,128)(2,1)S(1)}, u32[]{:S(2)}, u32[]{:S(2)}) %collective-permute-start.11) | collective-permute-done | bytes 327712 | tf_op jit(solution)/shard_map/ppermute | solution.py:309
  88.2 1.5 collective-permute-start.20
  90.3 0.9 collective-permute-start.24
  91.1 4.1 %collective-permute-done.16.refs_14_ = bf16[2,16,5120]{2,1,0:T(8,128)(2,1)S(1)} collective-permute-done((bf16[2,16,5120]{2,1,0:T(8,128)(2,1)S(1)}, bf16[2,16,5120]{2,1,0:T(8,128)(2,1)S(1)}, u32[]{:S(2)}, u32[]{:S(2)}) %collective-permute-start.16) | collective-permute-done | bytes 327712 | tf_op jit(solution)/shard_map/ppermute | solution.py:309
  95.2 0.9 collective-permute-start.27
  96.1 6.2 %collective-permute-done.19.refs_17_ = bf16[2,16,5120]{2,1,0:T(8,128)(2,1)S(1)} collective-permute-done((bf16[2,16,5120]{2,1,0:T(8,128)(2,1)S(1)}, bf16[2,16,5120]{2,1,0:T(8,128)(2,1)S(1)}, u32[]{:S(2)}, u32[]{:S(2)}) %collective-permute-start.19) | collective-permute-done | bytes 327712 | tf_op jit(solution)/shard_map/ppermute | solution.py:309
  102.3 1.5 collective-permute-start.31
  104.6 1.5 collective-permute-start.13
  106.1 3.2 %collective-permute-done.24.refs_22_ = bf16[2,16,5120]{2,1,0:T(8,128)(2,1)S(1)} collective-permute-done((bf16[2,16,5120]{2,1,0:T(8,128)(2,1)S(1)}, bf16[2,16,5120]{2,1,0:T(8,128)(2,1)S(1)}, u32[]{:S(2)}, u32[]{:S(2)}) %collective-permute-start.24) | collective-permute-done | bytes 327712 | tf_op jit(solution)/shard_map/ppermute | solution.py:309
  109.3 0.9 collective-permute-start.17
  110.2 6.2 %collective-permute-done.27.refs_1_ = bf16[2,16,5120]{2,1,0:T(8,128)(2,1)S(1)} collective-permute-done((bf16[2,16,5120]{2,1,0:T(8,128)(2,1)S(1)}, bf16[2,16,5120]{2,1,0:T(8,128)(2,1)S(1)}, u32[]{:S(2)}, u32[]{:S(2)}) %collective-permute-start.27) | collective-permute-done | bytes 327712 | tf_op jit(solution)/shard_map/ppermute | solution.py:309
  116.3 1.5 collective-permute-start.21
  118.3 5.0 %collective-permute-done.9.refs_7_ = bf16[2,16,5120]{2,1,0:T(8,128)(2,1)S(1)} collective-permute-done((bf16[2,16,5120]{2,1,0:T(8,128)(2,1)S(1)}, bf16[2,16,5120]{2,1,0:T(8,128)(2,1)S(1)}, u32[]{:S(2)}, u32[]{:S(2)}) %collective-permute-start.9) | collective-permute-done | bytes 327712 | tf_op jit(solution)/shard_map/ppermute | solution.py:309
  123.3 0.9 collective-permute-start.25
  124.2 1.2 collective-permute-start.32
  125.4 5.0 %collective-permute-done.17.refs_15_ = bf16[2,16,5120]{2,1,0:T(8,128)(2,1)S(1)} collective-permute-done((bf16[2,16,5120]{2,1,0:T(8,128)(2,1)S(1)}, bf16[2,16,5120]{2,1,0:T(8,128)(2,1)S(1)}, u32[]{:S(2)}, u32[]{:S(2)}) %collective-permute-start.17) | collective-permute-done | bytes 327712 | tf_op jit(solution)/shard_map/ppermute | solution.py:309
  130.4 1.5 collective-permute-start.29
  132.4 1.0 turn.1
  133.4 3.9 %collective-permute-done.25.refs_23_ = bf16[2,16,5120]{2,1,0:T(8,128)(2,1)S(1)} collective-permute-done((bf16[2,16,5120]{2,1,0:T(8,128)(2,1)S(1)}, bf16[2,16,5120]{2,1,0:T(8,128)(2,1)S(1)}, u32[]{:S(2)}, u32[]{:S(2)}) %collective-permute-start.25) | collective-permute-done | bytes 327712 | tf_op jit(solution)/shard_map/ppermute | solution.py:309
  137.4 5.8 %early.1.partial = f32[2,256,5120]{2,1,0:T(8,128)S(1)} custom-call(bf16[2,256,768]{2,1,0:T(8,128)(2,1)S(1)} %get-tuple-element.24.weights, bf16[2,16,5120]{2,1,0:T(8,128)(2,1)S(1)} %get-tuple-element.25.refs_0_, bf16[2,16,5120]{2,1,0:T(8,128)(2,1)S(1)} %collective-permute-done.3.refs_1_, bf16[2,16,5120]{2,1,0:T(8,128)(2,1)S(1)} %collective-permute-done.4.refs_2_, ...), custom_call_target="tpu_custom_call" | custom-call | tf_op jit(solution)/shard_map/early/pallas_call | solution.py:272
  143.2 1.2 collective-permute-done.32.refs_6_
  144.4 6.8 %collective-permute-done.33.refs_7_ = bf16[2,16,5120]{2,1,0:T(8,128)(2,1)S(1)} collective-permute-done((bf16[2,16,5120]{2,1,0:T(8,128)(2,1)S(1)}, bf16[2,16,5120]{2,1,0:T(8,128)(2,1)S(1)}, u32[]{:S(2)}, u32[]{:S(2)}) %collective-permute-start.33) | collective-permute-done | bytes 327712 | tf_op jit(solution)/shard_map/ppermute | solution.py:309
  151.2 6.1 %late.1 = bf16[256,80,128]{2,1,0:T(8,128)(2,1)} custom-call(bf16[2,256,256]{2,1,0:T(8,128)(2,1)S(1)} %get-tuple-element.23.weights, f32[2,256,5120]{2,1,0:T(8,128)S(1)} %early.1.partial, bf16[2,16,5120]{2,1,0:T(8,128)(2,1)S(1)} %collective-permute-done.26.refs_0_, bf16[2,16,5120]{2,1,0:T(8,128)(2,1)S(1)} %collective-permute-done.27.refs_1_, ...), custom_call_target="tpu_custom_call" | custom-call | tf_op jit(solution)/shard_map/late/pallas_call | solution.py:291
  (41 shorter events, 3.3 us)
Async XLA Ops:
  0.0 15.0 %copy-start.4 = (f32[12,256]{1,0:T(8,128)S(1)}, f32[12,256]{1,0:T(8,128)}, u32[]{:S(2)}) copy-start(f32[12,256]{1,0:T(8,128)} %taps_ref.7) | copy-start | bytes 36868
  0.0 10.7 %copy-start.5 = (s32[128]{0:T(128)S(1)}, s32[128]{0:T(128)}, u32[]{:S(2)}) copy-start(s32[128]{0:T(128)} %param.9) | copy-start | bytes 1540
  0.1 0.9 copy-start
  1.0 0.7 copy-start.3
  1.7 8.9 %copy-start.2 = (bf16[1,2,128,1024]{3,2,1,0:T(8,128)(2,1)S(1)}, bf16[1,2,128,1024]{3,2,1,0:T(8,128)(2,1)}, u32[]{:S(2)}) copy-start(bf16[1,2,128,1024]{3,2,1,0:T(8,128)(2,1)} %param.8) | copy-start | bytes 1572868
  1.8 13.3 %copy-start.1 = (bf16[256,512]{1,0:T(8,128)(2,1)S(1)}, bf16[256,512]{1,0:T(8,128)(2,1)}, u32[]{:S(2)}) copy-start(bf16[256,512]{1,0:T(8,128)(2,1)} %constant.14.table) | copy-start | bytes 786436
  5.5 19.4 %collective-permute-start.3 = (bf16[2,16,5120]{2,1,0:T(8,128)(2,1)S(1)}, bf16[2,16,5120]{2,1,0:T(8,128)(2,1)S(1)}, u32[]{:S(2)}, u32[]{:S(2)}) collective-permute-start(bf16[2,16,5120]{2,1,0:T(8,128)(2,1)S(1)} %get-tuple-element.25.refs_0_), channel_id=1, source_target_pairs={{0,8},{8,0},{16,24},{24,16},{1,9},{9,1},{17,25},{25,17},{2,10},{10... | collective-permute-start | bytes 983048 | tf_op jit(solution)/shard_map/ppermute | solution.py:309
  8.5 22.6 %collective-permute-start.4 = (bf16[2,16,5120]{2,1,0:T(8,128)(2,1)S(1)}, bf16[2,16,5120]{2,1,0:T(8,128)(2,1)S(1)}, u32[]{:S(2)}, u32[]{:S(2)}) collective-permute-start(bf16[2,16,5120]{2,1,0:T(8,128)(2,1)S(1)} %get-tuple-element.25.refs_0_), channel_id=1, source_target_pairs={{0,16},{8,24},{16,0},{24,8},{1,17},{9,25},{17,1},{25,9},{2,18},{10... | collective-permute-start | bytes 983048 | tf_op jit(solution)/shard_map/ppermute | solution.py:309
  11.5 10.8 %collective-permute-start = (bf16[2,8,16,256]{3,2,1,0:T(8,128)(2,1)S(1)}, bf16[2,8,16,256]{3,2,1,0:T(8,128)(2,1)S(1)}, u32[]{:S(2)}, u32[]{:S(2)}) collective-permute-start(bf16[2,8,16,256]{3,2,1,0:T(8,128)(2,1)S(1)} %get-tuple-element.20), channel_id=1, source_target_pairs={{0,8},{8,0},{16,24},{24,16},{1,9},{9,1},{17,25},{25,17},{2,10},{10... | collective-permute-start | bytes 393224 | tf_op jit(solution)/shard_map/ppermute | solution.py:309
  12.1 11.2 %collective-permute-start.1 = (bf16[2,8,16,256]{3,2,1,0:T(8,128)(2,1)S(1)}, bf16[2,8,16,256]{3,2,1,0:T(8,128)(2,1)S(1)}, u32[]{:S(2)}, u32[]{:S(2)}) collective-permute-start(bf16[2,8,16,256]{3,2,1,0:T(8,128)(2,1)S(1)} %get-tuple-element.21), channel_id=1, source_target_pairs={{0,16},{8,24},{16,0},{24,8},{1,17},{9,25},{17,1},{25,9},{2,18},{10... | collective-permute-start | bytes 393224 | tf_op jit(solution)/shard_map/ppermute | solution.py:309
  12.1 12.7 %collective-permute-start.2 = (bf16[2,8,16,256]{3,2,1,0:T(8,128)(2,1)S(1)}, bf16[2,8,16,256]{3,2,1,0:T(8,128)(2,1)S(1)}, u32[]{:S(2)}, u32[]{:S(2)}) collective-permute-start(bf16[2,8,16,256]{3,2,1,0:T(8,128)(2,1)S(1)} %get-tuple-element.22), channel_id=1, source_target_pairs={{0,24},{8,16},{16,8},{24,0},{1,25},{9,17},{17,9},{25,1},{2,26},{10... | collective-permute-start | bytes 393224 | tf_op jit(solution)/shard_map/ppermute | solution.py:309
  22.3 9.0 %collective-permute-start.6 = (bf16[2,16,5120]{2,1,0:T(8,128)(2,1)S(1)}, bf16[2,16,5120]{2,1,0:T(8,128)(2,1)S(1)}, u32[]{:S(2)}, u32[]{:S(2)}) collective-permute-start(bf16[2,16,5120]{2,1,0:T(8,128)(2,1)S(1)} %get-tuple-element.26), channel_id=1, source_target_pairs={{0,1},{1,0},{2,3},{3,2},{4,5},{5,4},{6,7},{7,6},{8,9},{9,8},{10,11... | collective-permute-start | bytes 983048 | tf_op jit(solution)/shard_map/ppermute | solution.py:309
  23.3 23.3 %collective-permute-start.10 = (bf16[2,16,5120]{2,1,0:T(8,128)(2,1)S(1)}, bf16[2,16,5120]{2,1,0:T(8,128)(2,1)S(1)}, u32[]{:S(2)}, u32[]{:S(2)}) collective-permute-start(bf16[2,16,5120]{2,1,0:T(8,128)(2,1)S(1)} %get-tuple-element.27), channel_id=1, source_target_pairs={{0,2},{1,3},{2,0},{3,1},{4,6},{5,7},{6,4},{7,5},{8,10},{9,11},{10,... | collective-permute-start | bytes 983048 | tf_op jit(solution)/shard_map/ppermute | solution.py:309
  24.8 26.0 %collective-permute-start.14 = (bf16[2,16,5120]{2,1,0:T(8,128)(2,1)S(1)}, bf16[2,16,5120]{2,1,0:T(8,128)(2,1)S(1)}, u32[]{:S(2)}, u32[]{:S(2)}) collective-permute-start(bf16[2,16,5120]{2,1,0:T(8,128)(2,1)S(1)} %get-tuple-element.28), channel_id=1, source_target_pairs={{0,3},{1,2},{2,1},{3,0},{4,7},{5,6},{6,5},{7,4},{8,11},{9,10},{10,... | collective-permute-start | bytes 983048 | tf_op jit(solution)/shard_map/ppermute | solution.py:309
  24.9 26.0 %collective-permute-start.18 = (bf16[2,16,5120]{2,1,0:T(8,128)(2,1)S(1)}, bf16[2,16,5120]{2,1,0:T(8,128)(2,1)S(1)}, u32[]{:S(2)}, u32[]{:S(2)}) collective-permute-start(bf16[2,16,5120]{2,1,0:T(8,128)(2,1)S(1)} %get-tuple-element.29), channel_id=1, source_target_pairs={{0,4},{1,5},{2,6},{3,7},{4,0},{5,1},{6,2},{7,3},{8,12},{9,13},{10,... | collective-permute-start | bytes 983048 | tf_op jit(solution)/shard_map/ppermute | solution.py:309
  31.1 39.5 %collective-permute-start.22 = (bf16[2,16,5120]{2,1,0:T(8,128)(2,1)S(1)}, bf16[2,16,5120]{2,1,0:T(8,128)(2,1)S(1)}, u32[]{:S(2)}, u32[]{:S(2)}) collective-permute-start(bf16[2,16,5120]{2,1,0:T(8,128)(2,1)S(1)} %get-tuple-element.30), channel_id=1, source_target_pairs={{0,5},{1,4},{2,7},{3,6},{4,1},{5,0},{6,3},{7,2},{8,13},{9,12},{10,... | collective-permute-start | bytes 983048 | tf_op jit(solution)/shard_map/ppermute | solution.py:309
  31.3 40.2 %collective-permute-start.26 = (bf16[2,16,5120]{2,1,0:T(8,128)(2,1)S(1)}, bf16[2,16,5120]{2,1,0:T(8,128)(2,1)S(1)}, u32[]{:S(2)}, u32[]{:S(2)}) collective-permute-start(bf16[2,16,5120]{2,1,0:T(8,128)(2,1)S(1)} %get-tuple-element.31), channel_id=1, source_target_pairs={{0,6},{1,7},{2,4},{3,5},{4,2},{5,3},{6,0},{7,1},{8,14},{9,15},{10,... | collective-permute-start | bytes 983048 | tf_op jit(solution)/shard_map/ppermute | solution.py:309
  46.5 26.1 %collective-permute-start.30 = (bf16[2,16,5120]{2,1,0:T(8,128)(2,1)S(1)}, bf16[2,16,5120]{2,1,0:T(8,128)(2,1)S(1)}, u32[]{:S(2)}, u32[]{:S(2)}) collective-permute-start(bf16[2,16,5120]{2,1,0:T(8,128)(2,1)S(1)} %get-tuple-element.32), channel_id=1, source_target_pairs={{0,7},{1,6},{2,5},{3,4},{4,3},{5,2},{6,1},{7,0},{8,15},{9,14},{10,... | collective-permute-start | bytes 983048 | tf_op jit(solution)/shard_map/ppermute | solution.py:309
  50.8 23.3 %collective-permute-start.5 = (bf16[2,16,5120]{2,1,0:T(8,128)(2,1)S(1)}, bf16[2,16,5120]{2,1,0:T(8,128)(2,1)S(1)}, u32[]{:S(2)}, u32[]{:S(2)}) collective-permute-start(bf16[2,16,5120]{2,1,0:T(8,128)(2,1)S(1)} %collective-permute-done.3.refs_1_), channel_id=1, source_target_pairs={{0,16},{8,24},{16,0},{24,8},{1,17},{9,25},{17,1},{25,9},{2,18},{10... | collective-permute-start | bytes 983048 | tf_op jit(solution)/shard_map/ppermute | solution.py:309
  50.8 23.9 %collective-permute-start.7 = (bf16[2,16,5120]{2,1,0:T(8,128)(2,1)S(1)}, bf16[2,16,5120]{2,1,0:T(8,128)(2,1)S(1)}, u32[]{:S(2)}, u32[]{:S(2)}) collective-permute-start(bf16[2,16,5120]{2,1,0:T(8,128)(2,1)S(1)} %collective-permute-done.6.refs_4_), channel_id=1, source_target_pairs={{0,16},{8,24},{16,0},{24,8},{1,17},{9,25},{17,1},{25,9},{2,18},{10... | collective-permute-start | bytes 983048 | tf_op jit(solution)/shard_map/ppermute | solution.py:309
  70.6 10.6 %collective-permute-start.8 = (bf16[2,16,5120]{2,1,0:T(8,128)(2,1)S(1)}, bf16[2,16,5120]{2,1,0:T(8,128)(2,1)S(1)}, u32[]{:S(2)}, u32[]{:S(2)}) collective-permute-start(bf16[2,16,5120]{2,1,0:T(8,128)(2,1)S(1)} %collective-permute-done.6.refs_4_), channel_id=1, source_target_pairs={{0,8},{8,0},{16,24},{24,16},{1,9},{9,1},{17,25},{25,17},{2,10},{10... | collective-permute-start | bytes 983048 | tf_op jit(solution)/shard_map/ppermute | solution.py:309
  71.5 16.7 %collective-permute-start.11 = (bf16[2,16,5120]{2,1,0:T(8,128)(2,1)S(1)}, bf16[2,16,5120]{2,1,0:T(8,128)(2,1)S(1)}, u32[]{:S(2)}, u32[]{:S(2)}) collective-permute-start(bf16[2,16,5120]{2,1,0:T(8,128)(2,1)S(1)} %collective-permute-done.10.refs_8_), channel_id=1, source_target_pairs={{0,8},{8,0},{16,24},{24,16},{1,9},{9,1},{17,25},{25,17},{2,10},{10... | collective-permute-start | bytes 983048 | tf_op jit(solution)/shard_map/ppermute | solution.py:309
  72.6 17.1 %collective-permute-start.12 = (bf16[2,16,5120]{2,1,0:T(8,128)(2,1)S(1)}, bf16[2,16,5120]{2,1,0:T(8,128)(2,1)S(1)}, u32[]{:S(2)}, u32[]{:S(2)}) collective-permute-start(bf16[2,16,5120]{2,1,0:T(8,128)(2,1)S(1)} %collective-permute-done.10.refs_8_), channel_id=1, source_target_pairs={{0,16},{8,24},{16,0},{24,8},{1,17},{9,25},{17,1},{25,9},{2,18},{10... | collective-permute-start | bytes 983048 | tf_op jit(solution)/shard_map/ppermute | solution.py:309
  74.2 16.1 %collective-permute-start.15 = (bf16[2,16,5120]{2,1,0:T(8,128)(2,1)S(1)}, bf16[2,16,5120]{2,1,0:T(8,128)(2,1)S(1)}, u32[]{:S(2)}, u32[]{:S(2)}) collective-permute-start(bf16[2,16,5120]{2,1,0:T(8,128)(2,1)S(1)} %collective-permute-done.14.refs_12_), channel_id=1, source_target_pairs={{0,16},{8,24},{16,0},{24,8},{1,17},{9,25},{17,1},{25,9},{2,18},{10... | collective-permute-start | bytes 983048 | tf_op jit(solution)/shard_map/ppermute | solution.py:309
  74.7 20.6 %collective-permute-start.16 = (bf16[2,16,5120]{2,1,0:T(8,128)(2,1)S(1)}, bf16[2,16,5120]{2,1,0:T(8,128)(2,1)S(1)}, u32[]{:S(2)}, u32[]{:S(2)}) collective-permute-start(bf16[2,16,5120]{2,1,0:T(8,128)(2,1)S(1)} %collective-permute-done.14.refs_12_), channel_id=1, source_target_pairs={{0,8},{8,0},{16,24},{24,16},{1,9},{9,1},{17,25},{25,17},{2,10},{10... | collective-permute-start | bytes 983048 | tf_op jit(solution)/shard_map/ppermute | solution.py:309
  81.2 21.1 %collective-permute-start.19 = (bf16[2,16,5120]{2,1,0:T(8,128)(2,1)S(1)}, bf16[2,16,5120]{2,1,0:T(8,128)(2,1)S(1)}, u32[]{:S(2)}, u32[]{:S(2)}) collective-permute-start(bf16[2,16,5120]{2,1,0:T(8,128)(2,1)S(1)} %collective-permute-done.18.refs_16_), channel_id=1, source_target_pairs={{0,8},{8,0},{16,24},{24,16},{1,9},{9,1},{17,25},{25,17},{2,10},{10... | collective-permute-start | bytes 983048 | tf_op jit(solution)/shard_map/ppermute | solution.py:309
  88.2 15.6 %collective-permute-start.20 = (bf16[2,16,5120]{2,1,0:T(8,128)(2,1)S(1)}, bf16[2,16,5120]{2,1,0:T(8,128)(2,1)S(1)}, u32[]{:S(2)}, u32[]{:S(2)}) collective-permute-start(bf16[2,16,5120]{2,1,0:T(8,128)(2,1)S(1)} %collective-permute-done.18.refs_16_), channel_id=1, source_target_pairs={{0,16},{8,24},{16,0},{24,8},{1,17},{9,25},{17,1},{25,9},{2,18},{10... | collective-permute-start | bytes 983048 | tf_op jit(solution)/shard_map/ppermute | solution.py:309
  89.7 14.8 %collective-permute-start.23 = (bf16[2,16,5120]{2,1,0:T(8,128)(2,1)S(1)}, bf16[2,16,5120]{2,1,0:T(8,128)(2,1)S(1)}, u32[]{:S(2)}, u32[]{:S(2)}) collective-permute-start(bf16[2,16,5120]{2,1,0:T(8,128)(2,1)S(1)} %collective-permute-done.22.refs_20_), channel_id=1, source_target_pairs={{0,16},{8,24},{16,0},{24,8},{1,17},{9,25},{17,1},{25,9},{2,18},{10... | collective-permute-start | bytes 983048 | tf_op jit(solution)/shard_map/ppermute | solution.py:309
  90.3 19.0 %collective-permute-start.24 = (bf16[2,16,5120]{2,1,0:T(8,128)(2,1)S(1)}, bf16[2,16,5120]{2,1,0:T(8,128)(2,1)S(1)}, u32[]{:S(2)}, u32[]{:S(2)}) collective-permute-start(bf16[2,16,5120]{2,1,0:T(8,128)(2,1)S(1)} %collective-permute-done.22.refs_20_), channel_id=1, source_target_pairs={{0,8},{8,0},{16,24},{24,16},{1,9},{9,1},{17,25},{25,17},{2,10},{10... | collective-permute-start | bytes 983048 | tf_op jit(solution)/shard_map/ppermute | solution.py:309
  95.2 21.1 %collective-permute-start.27 = (bf16[2,16,5120]{2,1,0:T(8,128)(2,1)S(1)}, bf16[2,16,5120]{2,1,0:T(8,128)(2,1)S(1)}, u32[]{:S(2)}, u32[]{:S(2)}) collective-permute-start(bf16[2,16,5120]{2,1,0:T(8,128)(2,1)S(1)} %collective-permute-done.26.refs_0_), channel_id=1, source_target_pairs={{0,8},{8,0},{16,24},{24,16},{1,9},{9,1},{17,25},{25,17},{2,10},{10... | collective-permute-start | bytes 983048 | tf_op jit(solution)/shard_map/ppermute | solution.py:309
  102.3 15.6 %collective-permute-start.31 = (bf16[2,16,5120]{2,1,0:T(8,128)(2,1)S(1)}, bf16[2,16,5120]{2,1,0:T(8,128)(2,1)S(1)}, u32[]{:S(2)}, u32[]{:S(2)}) collective-permute-start(bf16[2,16,5120]{2,1,0:T(8,128)(2,1)S(1)} %collective-permute-done.30.refs_4_), channel_id=1, source_target_pairs={{0,16},{8,24},{16,0},{24,8},{1,17},{9,25},{17,1},{25,9},{2,18},{10... | collective-permute-start | bytes 983048 | tf_op jit(solution)/shard_map/ppermute | solution.py:309
  103.8 19.5 %collective-permute-start.9 = (bf16[2,16,5120]{2,1,0:T(8,128)(2,1)S(1)}, bf16[2,16,5120]{2,1,0:T(8,128)(2,1)S(1)}, u32[]{:S(2)}, u32[]{:S(2)}) collective-permute-start(bf16[2,16,5120]{2,1,0:T(8,128)(2,1)S(1)} %collective-permute-done.7.refs_5_), channel_id=1, source_target_pairs={{0,8},{8,0},{16,24},{24,16},{1,9},{9,1},{17,25},{25,17},{2,10},{10... | collective-permute-start | bytes 983048 | tf_op jit(solution)/shard_map/ppermute | solution.py:309
  104.6 19.6 %collective-permute-start.13 = (bf16[2,16,5120]{2,1,0:T(8,128)(2,1)S(1)}, bf16[2,16,5120]{2,1,0:T(8,128)(2,1)S(1)}, u32[]{:S(2)}, u32[]{:S(2)}) collective-permute-start(bf16[2,16,5120]{2,1,0:T(8,128)(2,1)S(1)} %collective-permute-done.11.refs_9_), channel_id=1, source_target_pairs={{0,16},{8,24},{16,0},{24,8},{1,17},{9,25},{17,1},{25,9},{2,18},{10... | collective-permute-start | bytes 983048 | tf_op jit(solution)/shard_map/ppermute | solution.py:309
  109.3 21.1 %collective-permute-start.17 = (bf16[2,16,5120]{2,1,0:T(8,128)(2,1)S(1)}, bf16[2,16,5120]{2,1,0:T(8,128)(2,1)S(1)}, u32[]{:S(2)}, u32[]{:S(2)}) collective-permute-start(bf16[2,16,5120]{2,1,0:T(8,128)(2,1)S(1)} %collective-permute-done.15.refs_13_), channel_id=1, source_target_pairs={{0,8},{8,0},{16,24},{24,16},{1,9},{9,1},{17,25},{25,17},{2,10},{10... | collective-permute-start | bytes 983048 | tf_op jit(solution)/shard_map/ppermute | solution.py:309
  116.3 15.6 %collective-permute-start.21 = (bf16[2,16,5120]{2,1,0:T(8,128)(2,1)S(1)}, bf16[2,16,5120]{2,1,0:T(8,128)(2,1)S(1)}, u32[]{:S(2)}, u32[]{:S(2)}) collective-permute-start(bf16[2,16,5120]{2,1,0:T(8,128)(2,1)S(1)} %collective-permute-done.19.refs_17_), channel_id=1, source_target_pairs={{0,16},{8,24},{16,0},{24,8},{1,17},{9,25},{17,1},{25,9},{2,18},{10... | collective-permute-start | bytes 983048 | tf_op jit(solution)/shard_map/ppermute | solution.py:309
  117.8 25.4 %collective-permute-start.28 = (bf16[2,16,5120]{2,1,0:T(8,128)(2,1)S(1)}, bf16[2,16,5120]{2,1,0:T(8,128)(2,1)S(1)}, u32[]{:S(2)}, u32[]{:S(2)}) collective-permute-start(bf16[2,16,5120]{2,1,0:T(8,128)(2,1)S(1)} %collective-permute-done.26.refs_0_), channel_id=1, source_target_pairs={{0,16},{8,24},{16,0},{24,8},{1,17},{9,25},{17,1},{25,9},{2,18},{10... | collective-permute-start | bytes 983048 | tf_op jit(solution)/shard_map/ppermute | solution.py:309
  123.3 14.0 %collective-permute-start.25 = (bf16[2,16,5120]{2,1,0:T(8,128)(2,1)S(1)}, bf16[2,16,5120]{2,1,0:T(8,128)(2,1)S(1)}, u32[]{:S(2)}, u32[]{:S(2)}) collective-permute-start(bf16[2,16,5120]{2,1,0:T(8,128)(2,1)S(1)} %collective-permute-done.23.refs_21_), channel_id=1, source_target_pairs={{0,8},{8,0},{16,24},{24,16},{1,9},{9,1},{17,25},{25,17},{2,10},{10... | collective-permute-start | bytes 983048 | tf_op jit(solution)/shard_map/ppermute | solution.py:309
  124.2 20.2 %collective-permute-start.32 = (bf16[2,16,5120]{2,1,0:T(8,128)(2,1)S(1)}, bf16[2,16,5120]{2,1,0:T(8,128)(2,1)S(1)}, u32[]{:S(2)}, u32[]{:S(2)}) collective-permute-start(bf16[2,16,5120]{2,1,0:T(8,128)(2,1)S(1)} %collective-permute-done.30.refs_4_), channel_id=1, source_target_pairs={{0,8},{8,0},{16,24},{24,16},{1,9},{9,1},{17,25},{25,17},{2,10},{10... | collective-permute-start | bytes 983048 | tf_op jit(solution)/shard_map/ppermute | solution.py:309
  130.4 14.0 %collective-permute-start.29 = (bf16[2,16,5120]{2,1,0:T(8,128)(2,1)S(1)}, bf16[2,16,5120]{2,1,0:T(8,128)(2,1)S(1)}, u32[]{:S(2)}, u32[]{:S(2)}) collective-permute-start(bf16[2,16,5120]{2,1,0:T(8,128)(2,1)S(1)} %collective-permute-done.27.refs_1_), channel_id=1, source_target_pairs={{0,16},{8,24},{16,0},{24,8},{1,17},{9,25},{17,1},{25,9},{2,18},{10... | collective-permute-start | bytes 983048 | tf_op jit(solution)/shard_map/ppermute | solution.py:309
  131.9 19.3 %collective-permute-start.33 = (bf16[2,16,5120]{2,1,0:T(8,128)(2,1)S(1)}, bf16[2,16,5120]{2,1,0:T(8,128)(2,1)S(1)}, u32[]{:S(2)}, u32[]{:S(2)}) collective-permute-start(bf16[2,16,5120]{2,1,0:T(8,128)(2,1)S(1)} %collective-permute-done.31.refs_5_), channel_id=1, source_target_pairs={{0,8},{8,0},{16,24},{24,16},{1,9},{9,1},{17,25},{25,17},{2,10},{10... | collective-permute-start | bytes 983048 | tf_op jit(solution)/shard_map/ppermute | solution.py:309

commit v3 on v2

--- a/solution.py
+++ b/solution.py
@@ -77,22 +77,23 @@
     return jnp.asarray(both.astype(np.float32)).astype(jnp.bfloat16)
 
 
-def spectra_body(dims, info, volt, taps_ref, table, *refs):
-    slots, taps, frames_out, per_pair, pitch, split = dims
-    outs, wide, rows = refs[:-2], refs[-2], refs[-1]
+def spectra_body(dims, plane, near, info, volt, taps_ref, table, out0, out1, wide, rows):
+    taps, frames_out, per_pair, pitch, chunk = dims
     blocks = frames_out + taps - 1
     core = info[1] & 1
     fine = 2 * LANES
-    for s in range(slots):
-        wide[pl.ds(s * pitch, per_pair), :] = volt[s, 0, 0].astype(jnp.float32)
-    for turn in range(2):
+    polar = pl.program_id(0)
+    for s in range(chunk):
+        part = volt[s, 0, 0] if near else volt[s, polar, (info[1] >> 1) ^ plane]
+        wide[pl.ds(s * pitch, per_pair), :] = part.astype(jnp.float32)
+    for turn, out in ((0, out0), (1, out1)):
         base = jnp.bitwise_xor(core, turn) * (per_pair // 2)
         for q in range(2):
             for half in range(2):
                 lane = half * LANES
                 coef = [taps_ref[t : t + 1, lane : lane + LANES] for t in range(taps)]
                 data = [
-                    wide[pl.ds(base + 2 * (2 * i + half) + q, slots, stride=pitch), :]
+                    wide[pl.ds(base + 2 * (2 * i + half) + q, chunk, stride=pitch), :]
                     for i in range(blocks)
                 ]
                 for m in range(frames_out):
@@ -100,66 +101,73 @@
                     for t in range(1, taps):
                         total = total + coef[t] * data[m + t]
                     col = q * fine + lane
-                    rows[m * slots : (m + 1) * slots, col : col + LANES] = total.astype(
-                        jnp.bfloat16
+                    rows[m * chunk : (m + 1) * chunk, col : col + LANES] = total.astype(
+                        rows.dtype
                     )
-        first = jnp.dot(rows[:, :fine], table[...], preferred_element_type=jnp.float32)
-        second = jnp.dot(rows[:, fine:], table[...], preferred_element_type=jnp.float32)
-        real = (first[:, :fine] + second[:, fine:]).astype(jnp.bfloat16)
-        imag = (second[:, :fine] - first[:, fine:]).astype(jnp.bfloat16)
-
-        def put(out):
-            for m in range(frames_out):
-                span = slice(m * fine, (m + 1) * fine)
-                out[0, :, span] = real[m * slots : (m + 1) * slots]
-                out[1, :, span] = imag[m * slots : (m + 1) * slots]
-
-        if not split:
-            put(outs[turn])
-        else:
-            for p in range(len(outs) // 2):
-                pl.when(pl.program_id(0) == p)(functools.partial(put, outs[2 * p + turn]))
-
-
-def spectra_pair(info, plane, view, filter_taps, table, split):
+        left, right = (
+            rows[:, q * fine : (q + 1) * fine].astype(jnp.bfloat16) for q in range(2)
+        )
+        first = jnp.dot(left, table[...], preferred_element_type=jnp.float32)
+        second = jnp.dot(right, table[...], preferred_element_type=jnp.float32)
+        real = first[:, :fine] + second[:, fine:]
+        imag = second[:, :fine] - first[:, fine:]
+        for m in range(frames_out):
+            lead = m * fine
+            if not near:
+                lead = pl.multiple_of(polar * (frames_out * fine) + lead, LANES)
+            here = slice(m * chunk, (m + 1) * chunk)
+            out[0, :, pl.ds(lead, fine)] = real[here].astype(jnp.bfloat16)
+            out[1, :, pl.ds(lead, fine)] = imag[here].astype(jnp.bfloat16)
+
+
+def spectra_pair(info, plane, view, filter_taps, table):
     slots, polars, _, per_pair, _ = view.shape
     taps, fine = filter_taps.shape
     frames_out = per_pair // 8 - taps + 1
     width = frames_out * fine
     pitch = per_pair + 1
-    if split:
-        shapes = [jax.ShapeDtypeStruct((2, slots, width), jnp.bfloat16)] * (2 * polars)
-        out_specs = [pl.BlockSpec((2, slots, width), lambda p, info: (0, 0, 0))] * len(shapes)
+    near = plane == 0
+    shapes = [jax.ShapeDtypeStruct((2, slots, polars * width), jnp.bfloat16)] * 2
+    if near:
+        chunk = slots // 2
+        keep = [pltpu.with_memory_space_constraint(x, pltpu.HBM) for x in (view, filter_taps, table)]
+        grid = (polars, slots // chunk)
+        in_specs = [
+            pl.BlockSpec(
+                (chunk, 1, 1, per_pair, LANES), lambda p, h, info: (h, p, info[1] >> 1, 0, 0)
+            ),
+            pl.BlockSpec((taps, fine), lambda p, h, info: (0, 0)),
+            pl.BlockSpec((fine, 2 * fine), lambda p, h, info: (0, 0)),
+        ]
+        out_specs = [pl.BlockSpec((2, chunk, width), lambda p, h, info: (0, h, p))] * 2
+        kind = jnp.float32
     else:
-        shapes = [jax.ShapeDtypeStruct((2, slots, polars * width), jnp.bfloat16)] * 2
-        out_specs = [pl.BlockSpec((2, slots, width), lambda p, info: (0, 0, p))] * 2
-    return pl.pallas_call(
-        functools.partial(spectra_body, (slots, taps, frames_out, per_pair, pitch, split)),
+        chunk = slots
+        keep = [view, filter_taps, table]
+        grid = (polars,)
+        in_specs = [VMEM_WHOLE] * 3
+        out_specs = [VMEM_WHOLE] * 2
+        kind = jnp.bfloat16
+    return pl.pallas_call(
+        functools.partial(
+            spectra_body, (taps, frames_out, per_pair, pitch, chunk), plane, near
+        ),
         grid_spec=pltpu.PrefetchScalarGridSpec(
             num_scalar_prefetch=1,
-            grid=(polars,),
-            in_specs=[
-                pl.BlockSpec(
-                    (slots, 1, 1, per_pair, LANES), lambda p, info: (0, p, (info[1] >> 1) ^ plane, 0, 0)
-                ),
-                pl.BlockSpec((taps, fine), lambda p, info: (0, 0)),
-                pl.BlockSpec((fine, 2 * fine), lambda p, info: (0, 0)),
-            ],
+            grid=grid,
+            in_specs=in_specs,
             out_specs=out_specs,
             scratch_shapes=[
-                pltpu.VMEM((slots * pitch, LANES), jnp.float32),
-                pltpu.VMEM((frames_out * slots, 2 * fine), jnp.bfloat16),
+                pltpu.VMEM((chunk * pitch, LANES), jnp.float32),
+                pltpu.VMEM((frames_out * chunk, 2 * fine), kind),
             ],
         ),
         out_shape=shapes,
         compiler_params=pltpu.CompilerParams(
-            dimension_semantics=("arbitrary",), vmem_limit_bytes=KERNEL_VMEM
-        ),
-        cost_estimate=pl.CostEstimate(
-            flops=8 * 10**8, bytes_accessed=4 * 10**6, transcendentals=0
+            dimension_semantics=("arbitrary",) * len(grid), vmem_limit_bytes=KERNEL_VMEM
         ),
         name="spectra",
-    )(info, view, filter_taps, table)
+    )(info, *keep)
 
 
 def mask_body(info, count, ids, weights, *refs):
@@ -330,13 +338,11 @@
     view = view.transpose(0, 1, 2, 4, 3, 5).reshape(
         slots, polars, chans // 2, 4 * samples // LANES, LANES
     )
-    view = pltpu.with_memory_space_constraint(view, pltpu.HBM)
     table = cos_sin(fine)
     planes = freq // 2
     held = {}
     for jz in range(planes):
-        split = False
-        made = spectra_pair(info, jz, view, filter_taps, table, split)
+        made = spectra_pair(info, jz, view, filter_taps, table)
         for i, piece in enumerate(made):
             j, p = 2 * jz + i % 2, i // 2
             held[j, p] = piece if j == 0 else swap(piece, "freq", j, freq)
@@ -352,7 +358,7 @@
         (g, j, piece) for (j, _), group in have.items() for g, piece in group.items()
     ]
     partial = beam_early(w_early, [e for e in every if e[1] < freq - 2], 4 * LANES)
-    out = beam_late(w_late, partial, [e for e in every if e[1] >= freq - 2], 4 * LANES)
+    out = beam_late(w_late, partial, [e for e in every if e[1] >= freq - 2], 20 * LANES)
     high = out.shape[1] // 2
     return out.reshape(out.shape[0], high, 2, LANES).transpose(0, 2, 1, 3).reshape(
         out.shape[0], 2, 1, high * LANES

time: 158 us -> 153 us (0.968)
  Pallas kernels: 28.3 us -> 23.2 us
  starting transfers between devices: 38.3 us -> 43 us
  waiting for transfers between devices: 88.2 us -> 84.8 us
  local copies, waits for them, and re-layouts: 1.68 us -> 0.02 us
    ppermute x34, starting transfers between devices: 38.3 us -> 43 us  [swap(): return lax.ppermute(array, axis, [(i, i ^ step) for i in range(size)])]
    ppermute x34, waiting for transfers between devices: 88.2 us -> 84.8 us  [swap(): return lax.ppermute(array, axis, [(i, i ^ step) for i in range(size)])]
    pallas_call x4, Pallas kernels: 14.5 us -> 11.8 us  [spectra_pair(): pl.pallas_call(functools.partial(spectra_body, (taps, frames_out, per_pai...]
    pallas_call x1, Pallas kernels: 6.12 us -> 3.7 us  [beam_late(): pl.pallas_call(functools.partial(late_body, [(g, j) for g, j, _ in pieces...]
    unnamed x12 -> x10, local copies, waits for them, and re-layouts: 1.68 us -> 0.02 us
  transfers between devices with their start and end apart: 34 -> 34, of which waited for: 16 -> 15; matrix products, arithmetic and copies ran while one was open for 0% -> 0% of each run, Pallas kernels for 12% -> 10%
where the time goes in v3:
time: 153 us; the launch traced here: 152 us
  waiting for transfers between devices  84.8 us (55%)
  starting transfers between devices  43 us (28%)
  Pallas kernels  23.2 us (15%)
    ppermute x34, waiting for transfers between devices, swap(): return lax.ppermute(array, axis, [(i, i ^ step) for i in range(size)])  84.8 us
    ppermute x34, starting transfers between devices, swap(): return lax.ppermute(array, axis, [(i, i ^ step) for i in range(size)])  43 us
    pallas_call x4, Pallas kernels, spectra_pair(): pl.pallas_call(functools.partial(spectra_body, (taps, frames_out, per_pai...  11.8 us
    pallas_call x1, Pallas kernels, beam_early(): pl.pallas_call(functools.partial(early_body, [(g, j) for g, j, _ in piece...  5.84 us
    pallas_call x1, Pallas kernels, beam_late(): pl.pallas_call(functools.partial(late_body, [(g, j) for g, j, _ in pieces...  3.7 us
  transfers between devices with their start and end apart: 34, of which 15 were waited for; matrix products, arithmetic and copies ran while one was open for 0% of the time, Pallas kernels for 10%

profile of v3, /device:TPU:0, one launch (start us, length us, event | category | flops | bytes accessed | tf_op | source)
XLA Modules:
  0.0 151.9 jit_solution(16010986196033455453)
XLA Ops:
  0.1 4.5 %spectra.4 = (bf16[2,16,5120]{2,1,0:T(8,128)(2,1)S(1)}, bf16[2,16,5120]{2,1,0:T(8,128)(2,1)S(1)}) custom-call(s32[2]{0:T(128)S(1)} %pad_add_fusion.info, bf16[16,2,4,168,128]{4,3,2,1,0:T(8,128)(2,1)} %bitcast.18, f32[12,256]{1,0:T(8,128)} %taps_ref.7, bf16[256,512]{1,0:T(8,128)(2,1)} %constant.14.table), custom_call_target="tpu_custom_call" | custom-call | tf_op jit(solution)/shard_map/spectra/pallas_call | solution.py:151
  4.6 3.1 %collective-permute-start.3 = (bf16[2,16,5120]{2,1,0:T(8,128)(2,1)S(1)}, bf16[2,16,5120]{2,1,0:T(8,128)(2,1)S(1)}, u32[]{:S(2)}, u32[]{:S(2)}) collective-permute-start(bf16[2,16,5120]{2,1,0:T(8,128)(2,1)S(1)} %get-tuple-element.25.refs_0_), channel_id=1, source_target_pairs={{0,8},{8,0},{16,24},{24,16},{1,9},{9,1},{17,25},{25,17},{2,10},{10... | collective-permute-start | bytes 983048 | tf_op jit(solution)/shard_map/ppermute | solution.py:317
  8.3 0.8 mask.1
  9.2 2.0 %collective-permute-start.1 = (bf16[2,8,16,256]{3,2,1,0:T(8,128)(2,1)S(1)}, bf16[2,8,16,256]{3,2,1,0:T(8,128)(2,1)S(1)}, u32[]{:S(2)}, u32[]{:S(2)}) collective-permute-start(bf16[2,8,16,256]{3,2,1,0:T(8,128)(2,1)S(1)} %get-tuple-element.21), channel_id=1, source_target_pairs={{0,16},{8,24},{16,0},{24,8},{1,17},{9,25},{17,1},{25,9},{2,18},{10... | collective-permute-start | bytes 393224 | tf_op jit(solution)/shard_map/ppermute | solution.py:317
  11.2 1.4 collective-permute-start.2
  12.7 1.5 %collective-permute-start.4 = (bf16[2,16,5120]{2,1,0:T(8,128)(2,1)S(1)}, bf16[2,16,5120]{2,1,0:T(8,128)(2,1)S(1)}, u32[]{:S(2)}, u32[]{:S(2)}) collective-permute-start(bf16[2,16,5120]{2,1,0:T(8,128)(2,1)S(1)} %get-tuple-element.25.refs_0_), channel_id=1, source_target_pairs={{0,16},{8,24},{16,0},{24,8},{1,17},{9,25},{17,1},{25,9},{2,18},{10... | collective-permute-start | bytes 983048 | tf_op jit(solution)/shard_map/ppermute | solution.py:317
  14.2 2.5 %spectra.5 = (bf16[2,16,5120]{2,1,0:T(8,128)(2,1)S(1)}, bf16[2,16,5120]{2,1,0:T(8,128)(2,1)S(1)}) custom-call(s32[2]{0:T(128)S(1)} %pad_add_fusion.info, bf16[16,2,4,168,128]{4,3,2,1,0:T(8,128)(2,1)S(1)} %bitcast.19, f32[12,256]{1,0:T(8,128)S(1)} %copy-done.3, bf16[256,512]{1,0:T(8,128)(2,1)S(1)} %copy-done.1), custom_call_target="tpu_custom_call" | custom-call | tf_op jit(solution)/shard_map/spectra/pallas_call | solution.py:151
  16.6 2.5 %spectra.6 = (bf16[2,16,5120]{2,1,0:T(8,128)(2,1)S(1)}, bf16[2,16,5120]{2,1,0:T(8,128)(2,1)S(1)}) custom-call(s32[2]{0:T(128)S(1)} %pad_add_fusion.info, bf16[16,2,4,168,128]{4,3,2,1,0:T(8,128)(2,1)S(1)} %bitcast.20, f32[12,256]{1,0:T(8,128)S(1)} %copy-done.3, bf16[256,512]{1,0:T(8,128)(2,1)S(1)} %copy-done.1), custom_call_target="tpu_custom_call" | custom-call | tf_op jit(solution)/shard_map/spectra/pallas_call | solution.py:151
  19.2 1.9 %collective-permute-start.10 = (bf16[2,16,5120]{2,1,0:T(8,128)(2,1)S(1)}, bf16[2,16,5120]{2,1,0:T(8,128)(2,1)S(1)}, u32[]{:S(2)}, u32[]{:S(2)}) collective-permute-start(bf16[2,16,5120]{2,1,0:T(8,128)(2,1)S(1)} %get-tuple-element.27), channel_id=1, source_target_pairs={{0,2},{1,3},{2,0},{3,1},{4,6},{5,7},{6,4},{7,5},{8,10},{9,11},{10,... | collective-permute-start | bytes 983048 | tf_op jit(solution)/shard_map/ppermute | solution.py:317
  21.1 1.1 collective-permute-done.2
  22.3 2.6 %collective-permute-start.18 = (bf16[2,16,5120]{2,1,0:T(8,128)(2,1)S(1)}, bf16[2,16,5120]{2,1,0:T(8,128)(2,1)S(1)}, u32[]{:S(2)}, u32[]{:S(2)}) collective-permute-start(bf16[2,16,5120]{2,1,0:T(8,128)(2,1)S(1)} %get-tuple-element.29), channel_id=1, source_target_pairs={{0,4},{1,5},{2,6},{3,7},{4,0},{5,1},{6,2},{7,3},{8,12},{9,13},{10,... | collective-permute-start | bytes 983048 | tf_op jit(solution)/shard_map/ppermute | solution.py:317
  24.9 2.4 %spectra.7 = (bf16[2,16,5120]{2,1,0:T(8,128)(2,1)S(1)}, bf16[2,16,5120]{2,1,0:T(8,128)(2,1)S(1)}) custom-call(s32[2]{0:T(128)S(1)} %pad_add_fusion.info, bf16[16,2,4,168,128]{4,3,2,1,0:T(8,128)(2,1)S(1)} %bitcast.21, f32[12,256]{1,0:T(8,128)S(1)} %copy-done.3, bf16[256,512]{1,0:T(8,128)(2,1)S(1)} %copy-done.1), custom_call_target="tpu_custom_call" | custom-call | tf_op jit(solution)/shard_map/spectra/pallas_call | solution.py:151
  27.4 1.3 collective-permute-start.22
  28.7 2.5 %collective-permute-start.26 = (bf16[2,16,5120]{2,1,0:T(8,128)(2,1)S(1)}, bf16[2,16,5120]{2,1,0:T(8,128)(2,1)S(1)}, u32[]{:S(2)}, u32[]{:S(2)}) collective-permute-start(bf16[2,16,5120]{2,1,0:T(8,128)(2,1)S(1)} %get-tuple-element.31), channel_id=1, source_target_pairs={{0,6},{1,7},{2,4},{3,5},{4,2},{5,3},{6,0},{7,1},{8,14},{9,15},{10,... | collective-permute-start | bytes 983048 | tf_op jit(solution)/shard_map/ppermute | solution.py:317
  31.2 10.7 %collective-permute-done.10.refs_8_ = bf16[2,16,5120]{2,1,0:T(8,128)(2,1)S(1)} collective-permute-done((bf16[2,16,5120]{2,1,0:T(8,128)(2,1)S(1)}, bf16[2,16,5120]{2,1,0:T(8,128)(2,1)S(1)}, u32[]{:S(2)}, u32[]{:S(2)}) %collective-permute-start.10) | collective-permute-done | bytes 327712 | tf_op jit(solution)/shard_map/ppermute | solution.py:317
  41.8 0.9 collective-permute-start.30
  42.7 5.4 %collective-permute-done.14.refs_12_ = bf16[2,16,5120]{2,1,0:T(8,128)(2,1)S(1)} collective-permute-done((bf16[2,16,5120]{2,1,0:T(8,128)(2,1)S(1)}, bf16[2,16,5120]{2,1,0:T(8,128)(2,1)S(1)}, u32[]{:S(2)}, u32[]{:S(2)}) %collective-permute-start.14) | collective-permute-done | bytes 327712 | tf_op jit(solution)/shard_map/ppermute | solution.py:317
  48.1 2.5 %collective-permute-start.5 = (bf16[2,16,5120]{2,1,0:T(8,128)(2,1)S(1)}, bf16[2,16,5120]{2,1,0:T(8,128)(2,1)S(1)}, u32[]{:S(2)}, u32[]{:S(2)}) collective-permute-start(bf16[2,16,5120]{2,1,0:T(8,128)(2,1)S(1)} %collective-permute-done.3.refs_1_), channel_id=1, source_target_pairs={{0,16},{8,24},{16,0},{24,8},{1,17},{9,25},{17,1},{25,9},{2,18},{10... | collective-permute-start | bytes 983048 | tf_op jit(solution)/shard_map/ppermute | solution.py:317
  50.6 19.0 %collective-permute-done.22.refs_20_ = bf16[2,16,5120]{2,1,0:T(8,128)(2,1)S(1)} collective-permute-done((bf16[2,16,5120]{2,1,0:T(8,128)(2,1)S(1)}, bf16[2,16,5120]{2,1,0:T(8,128)(2,1)S(1)}, u32[]{:S(2)}, u32[]{:S(2)}) %collective-permute-start.22) | collective-permute-done | bytes 327712 | tf_op jit(solution)/shard_map/ppermute | solution.py:317
  69.6 1.5 collective-permute-start.8
  71.1 0.5 collective-permute-start.11
  72.2 1.5 collective-permute-start.15
  73.7 1.5 collective-permute-start.16
  75.2 5.0 %collective-permute-done.8.refs_6_ = bf16[2,16,5120]{2,1,0:T(8,128)(2,1)S(1)} collective-permute-done((bf16[2,16,5120]{2,1,0:T(8,128)(2,1)S(1)}, bf16[2,16,5120]{2,1,0:T(8,128)(2,1)S(1)}, u32[]{:S(2)}, u32[]{:S(2)}) %collective-permute-start.8) | collective-permute-done | bytes 327712 | tf_op jit(solution)/shard_map/ppermute | solution.py:317
  80.2 1.5 collective-permute-start.19
  81.7 5.5 %collective-permute-done.11.refs_9_ = bf16[2,16,5120]{2,1,0:T(8,128)(2,1)S(1)} collective-permute-done((bf16[2,16,5120]{2,1,0:T(8,128)(2,1)S(1)}, bf16[2,16,5120]{2,1,0:T(8,128)(2,1)S(1)}, u32[]{:S(2)}, u32[]{:S(2)}) %collective-permute-start.11) | collective-permute-done | bytes 327712 | tf_op jit(solution)/shard_map/ppermute | solution.py:317
  87.7 1.5 collective-permute-start.23
  89.3 1.5 collective-permute-start.24
  90.8 3.5 %collective-permute-done.16.refs_14_ = bf16[2,16,5120]{2,1,0:T(8,128)(2,1)S(1)} collective-permute-done((bf16[2,16,5120]{2,1,0:T(8,128)(2,1)S(1)}, bf16[2,16,5120]{2,1,0:T(8,128)(2,1)S(1)}, u32[]{:S(2)}, u32[]{:S(2)}) %collective-permute-start.16) | collective-permute-done | bytes 327712 | tf_op jit(solution)/shard_map/ppermute | solution.py:317
  94.2 1.5 collective-permute-start.27
  95.7 5.5 %collective-permute-done.19.refs_17_ = bf16[2,16,5120]{2,1,0:T(8,128)(2,1)S(1)} collective-permute-done((bf16[2,16,5120]{2,1,0:T(8,128)(2,1)S(1)}, bf16[2,16,5120]{2,1,0:T(8,128)(2,1)S(1)}, u32[]{:S(2)}, u32[]{:S(2)}) %collective-permute-start.19) | collective-permute-done | bytes 327712 | tf_op jit(solution)/shard_map/ppermute | solution.py:317
  101.8 1.5 collective-permute-start.9
  103.3 1.5 %collective-permute-start.13 = (bf16[2,16,5120]{2,1,0:T(8,128)(2,1)S(1)}, bf16[2,16,5120]{2,1,0:T(8,128)(2,1)S(1)}, u32[]{:S(2)}, u32[]{:S(2)}) collective-permute-start(bf16[2,16,5120]{2,1,0:T(8,128)(2,1)S(1)} %collective-permute-done.11.refs_9_), channel_id=1, source_target_pairs={{0,16},{8,24},{16,0},{24,8},{1,17},{9,25},{17,1},{25,9},{2,18},{10... | collective-permute-start | bytes 983048 | tf_op jit(solution)/shard_map/ppermute | solution.py:317
  104.8 3.5 %collective-permute-done.24.refs_22_ = bf16[2,16,5120]{2,1,0:T(8,128)(2,1)S(1)} collective-permute-done((bf16[2,16,5120]{2,1,0:T(8,128)(2,1)S(1)}, bf16[2,16,5120]{2,1,0:T(8,128)(2,1)S(1)}, u32[]{:S(2)}, u32[]{:S(2)}) %collective-permute-start.24) | collective-permute-done | bytes 327712 | tf_op jit(solution)/shard_map/ppermute | solution.py:317
  108.3 1.5 collective-permute-start.17
  109.8 5.5 %collective-permute-done.27.refs_1_ = bf16[2,16,5120]{2,1,0:T(8,128)(2,1)S(1)} collective-permute-done((bf16[2,16,5120]{2,1,0:T(8,128)(2,1)S(1)}, bf16[2,16,5120]{2,1,0:T(8,128)(2,1)S(1)}, u32[]{:S(2)}, u32[]{:S(2)}) %collective-permute-start.27) | collective-permute-done | bytes 327712 | tf_op jit(solution)/shard_map/ppermute | solution.py:317
  115.8 1.5 collective-permute-start.28
  117.3 5.0 %collective-permute-done.9.refs_7_ = bf16[2,16,5120]{2,1,0:T(8,128)(2,1)S(1)} collective-permute-done((bf16[2,16,5120]{2,1,0:T(8,128)(2,1)S(1)}, bf16[2,16,5120]{2,1,0:T(8,128)(2,1)S(1)}, u32[]{:S(2)}, u32[]{:S(2)}) %collective-permute-start.9) | collective-permute-done | bytes 327712 | tf_op jit(solution)/shard_map/ppermute | solution.py:317
  122.3 1.5 collective-permute-start.25
  123.8 0.5 collective-permute-start.32
  124.4 5.0 %collective-permute-done.17.refs_15_ = bf16[2,16,5120]{2,1,0:T(8,128)(2,1)S(1)} collective-permute-done((bf16[2,16,5120]{2,1,0:T(8,128)(2,1)S(1)}, bf16[2,16,5120]{2,1,0:T(8,128)(2,1)S(1)}, u32[]{:S(2)}, u32[]{:S(2)}) %collective-permute-start.17) | collective-permute-done | bytes 327712 | tf_op jit(solution)/shard_map/ppermute | solution.py:317
  129.9 1.5 collective-permute-start.33
  131.4 1.0 turn.1
  132.4 4.0 %collective-permute-done.25.refs_23_ = bf16[2,16,5120]{2,1,0:T(8,128)(2,1)S(1)} collective-permute-done((bf16[2,16,5120]{2,1,0:T(8,128)(2,1)S(1)}, bf16[2,16,5120]{2,1,0:T(8,128)(2,1)S(1)}, u32[]{:S(2)}, u32[]{:S(2)}) %collective-permute-start.25) | collective-permute-done | bytes 327712 | tf_op jit(solution)/shard_map/ppermute | solution.py:317
  136.4 5.8 %early.1.partial = f32[2,256,5120]{2,1,0:T(8,128)S(1)} custom-call(bf16[2,256,768]{2,1,0:T(8,128)(2,1)S(1)} %get-tuple-element.24.weights, bf16[2,16,5120]{2,1,0:T(8,128)(2,1)S(1)} %get-tuple-element.25.refs_0_, bf16[2,16,5120]{2,1,0:T(8,128)(2,1)S(1)} %collective-permute-done.3.refs_1_, bf16[2,16,5120]{2,1,0:T(8,128)(2,1)S(1)} %collective-permute-done.4.refs_2_, ...), custom_call_target="tpu_custom_call" | custom-call | tf_op jit(solution)/shard_map/early/pallas_call | solution.py:280
  142.2 1.2 collective-permute-done.32.refs_6_
  143.4 4.8 %collective-permute-done.33.refs_7_ = bf16[2,16,5120]{2,1,0:T(8,128)(2,1)S(1)} collective-permute-done((bf16[2,16,5120]{2,1,0:T(8,128)(2,1)S(1)}, bf16[2,16,5120]{2,1,0:T(8,128)(2,1)S(1)}, u32[]{:S(2)}, u32[]{:S(2)}) %collective-permute-start.33) | collective-permute-done | bytes 327712 | tf_op jit(solution)/shard_map/ppermute | solution.py:317
  148.3 3.7 %late.1 = bf16[256,80,128]{2,1,0:T(8,128)(2,1)} custom-call(bf16[2,256,256]{2,1,0:T(8,128)(2,1)S(1)} %get-tuple-element.23.weights, f32[2,256,5120]{2,1,0:T(8,128)S(1)} %early.1.partial, bf16[2,16,5120]{2,1,0:T(8,128)(2,1)S(1)} %collective-permute-done.26.refs_0_, bf16[2,16,5120]{2,1,0:T(8,128)(2,1)S(1)} %collective-permute-done.27.refs_1_, ...), custom_call_target="tpu_custom_call" | custom-call | tf_op jit(solution)/shard_map/late/pallas_call | solution.py:299
  (39 shorter events, 2.9 us)
Async XLA Ops:
  0.0 14.2 %copy-start.1 = (bf16[256,512]{1,0:T(8,128)(2,1)S(1)}, bf16[256,512]{1,0:T(8,128)(2,1)}, u32[]{:S(2)}) copy-start(bf16[256,512]{1,0:T(8,128)(2,1)} %constant.14.table) | copy-start | bytes 786436
  0.0 14.2 %copy-start.3 = (f32[12,256]{1,0:T(8,128)S(1)}, f32[12,256]{1,0:T(8,128)}, u32[]{:S(2)}) copy-start(f32[12,256]{1,0:T(8,128)} %taps_ref.7) | copy-start | bytes 36868
  0.0 8.3 %copy-start.4 = (s32[128]{0:T(128)S(1)}, s32[128]{0:T(128)}, u32[]{:S(2)}) copy-start(s32[128]{0:T(128)} %param.9) | copy-start | bytes 1540
  0.0 8.3 %copy-start.2 = (bf16[1,2,128,1024]{3,2,1,0:T(8,128)(2,1)S(1)}, bf16[1,2,128,1024]{3,2,1,0:T(8,128)(2,1)}, u32[]{:S(2)}) copy-start(bf16[1,2,128,1024]{3,2,1,0:T(8,128)(2,1)} %param.8) | copy-start | bytes 1572868
  0.0 14.2 %copy-start = (bf16[16,2,8,2,5376]{4,3,2,1,0:T(2,128)(2,1)S(1)}, bf16[16,2,8,2,5376]{4,3,2,1,0:T(2,128)(2,1)}, u32[]{:S(2)}) copy-start(bf16[16,2,8,2,5376]{4,3,2,1,0:T(2,128)(2,1)} %param.6) | copy-start | bytes 16515076
  4.6 17.8 %collective-permute-start.3 = (bf16[2,16,5120]{2,1,0:T(8,128)(2,1)S(1)}, bf16[2,16,5120]{2,1,0:T(8,128)(2,1)S(1)}, u32[]{:S(2)}, u32[]{:S(2)}) collective-permute-start(bf16[2,16,5120]{2,1,0:T(8,128)(2,1)S(1)} %get-tuple-element.25.refs_0_), channel_id=1, source_target_pairs={{0,8},{8,0},{16,24},{24,16},{1,9},{9,1},{17,25},{25,17},{2,10},{10... | collective-permute-start | bytes 983048 | tf_op jit(solution)/shard_map/ppermute | solution.py:317
  9.1 10.0 %collective-permute-start = (bf16[2,8,16,256]{3,2,1,0:T(8,128)(2,1)S(1)}, bf16[2,8,16,256]{3,2,1,0:T(8,128)(2,1)S(1)}, u32[]{:S(2)}, u32[]{:S(2)}) collective-permute-start(bf16[2,8,16,256]{3,2,1,0:T(8,128)(2,1)S(1)} %get-tuple-element.20), channel_id=1, source_target_pairs={{0,8},{8,0},{16,24},{24,16},{1,9},{9,1},{17,25},{25,17},{2,10},{10... | collective-permute-start | bytes 393224 | tf_op jit(solution)/shard_map/ppermute | solution.py:317
  9.2 10.0 %collective-permute-start.1 = (bf16[2,8,16,256]{3,2,1,0:T(8,128)(2,1)S(1)}, bf16[2,8,16,256]{3,2,1,0:T(8,128)(2,1)S(1)}, u32[]{:S(2)}, u32[]{:S(2)}) collective-permute-start(bf16[2,8,16,256]{3,2,1,0:T(8,128)(2,1)S(1)} %get-tuple-element.21), channel_id=1, source_target_pairs={{0,16},{8,24},{16,0},{24,8},{1,17},{9,25},{17,1},{25,9},{2,18},{10... | collective-permute-start | bytes 393224 | tf_op jit(solution)/shard_map/ppermute | solution.py:317
  11.2 11.0 %collective-permute-start.2 = (bf16[2,8,16,256]{3,2,1,0:T(8,128)(2,1)S(1)}, bf16[2,8,16,256]{3,2,1,0:T(8,128)(2,1)S(1)}, u32[]{:S(2)}, u32[]{:S(2)}) collective-permute-start(bf16[2,8,16,256]{3,2,1,0:T(8,128)(2,1)S(1)} %get-tuple-element.22), channel_id=1, source_target_pairs={{0,24},{8,16},{16,8},{24,0},{1,25},{9,17},{17,9},{25,1},{2,26},{10... | collective-permute-start | bytes 393224 | tf_op jit(solution)/shard_map/ppermute | solution.py:317
  12.7 14.7 %collective-permute-start.4 = (bf16[2,16,5120]{2,1,0:T(8,128)(2,1)S(1)}, bf16[2,16,5120]{2,1,0:T(8,128)(2,1)S(1)}, u32[]{:S(2)}, u32[]{:S(2)}) collective-permute-start(bf16[2,16,5120]{2,1,0:T(8,128)(2,1)S(1)} %get-tuple-element.25.refs_0_), channel_id=1, source_target_pairs={{0,16},{8,24},{16,0},{24,8},{1,17},{9,25},{17,1},{25,9},{2,18},{10... | collective-permute-start | bytes 983048 | tf_op jit(solution)/shard_map/ppermute | solution.py:317
  19.1 9.6 %collective-permute-start.6 = (bf16[2,16,5120]{2,1,0:T(8,128)(2,1)S(1)}, bf16[2,16,5120]{2,1,0:T(8,128)(2,1)S(1)}, u32[]{:S(2)}, u32[]{:S(2)}) collective-permute-start(bf16[2,16,5120]{2,1,0:T(8,128)(2,1)S(1)} %get-tuple-element.26), channel_id=1, source_target_pairs={{0,1},{1,0},{2,3},{3,2},{4,5},{5,4},{6,7},{7,6},{8,9},{9,8},{10,11... | collective-permute-start | bytes 983048 | tf_op jit(solution)/shard_map/ppermute | solution.py:317
  19.2 22.6 %collective-permute-start.10 = (bf16[2,16,5120]{2,1,0:T(8,128)(2,1)S(1)}, bf16[2,16,5120]{2,1,0:T(8,128)(2,1)S(1)}, u32[]{:S(2)}, u32[]{:S(2)}) collective-permute-start(bf16[2,16,5120]{2,1,0:T(8,128)(2,1)S(1)} %get-tuple-element.27), channel_id=1, source_target_pairs={{0,2},{1,3},{2,0},{3,1},{4,6},{5,7},{6,4},{7,5},{8,10},{9,11},{10,... | collective-permute-start | bytes 983048 | tf_op jit(solution)/shard_map/ppermute | solution.py:317
  22.3 25.9 %collective-permute-start.14 = (bf16[2,16,5120]{2,1,0:T(8,128)(2,1)S(1)}, bf16[2,16,5120]{2,1,0:T(8,128)(2,1)S(1)}, u32[]{:S(2)}, u32[]{:S(2)}) collective-permute-start(bf16[2,16,5120]{2,1,0:T(8,128)(2,1)S(1)} %get-tuple-element.28), channel_id=1, source_target_pairs={{0,3},{1,2},{2,1},{3,0},{4,7},{5,6},{6,5},{7,4},{8,11},{9,10},{10,... | collective-permute-start | bytes 983048 | tf_op jit(solution)/shard_map/ppermute | solution.py:317
  22.3 28.3 %collective-permute-start.18 = (bf16[2,16,5120]{2,1,0:T(8,128)(2,1)S(1)}, bf16[2,16,5120]{2,1,0:T(8,128)(2,1)S(1)}, u32[]{:S(2)}, u32[]{:S(2)}) collective-permute-start(bf16[2,16,5120]{2,1,0:T(8,128)(2,1)S(1)} %get-tuple-element.29), channel_id=1, source_target_pairs={{0,4},{1,5},{2,6},{3,7},{4,0},{5,1},{6,2},{7,3},{8,12},{9,13},{10,... | collective-permute-start | bytes 983048 | tf_op jit(solution)/shard_map/ppermute | solution.py:317
  27.4 42.2 %collective-permute-start.22 = (bf16[2,16,5120]{2,1,0:T(8,128)(2,1)S(1)}, bf16[2,16,5120]{2,1,0:T(8,128)(2,1)S(1)}, u32[]{:S(2)}, u32[]{:S(2)}) collective-permute-start(bf16[2,16,5120]{2,1,0:T(8,128)(2,1)S(1)} %get-tuple-element.30), channel_id=1, source_target_pairs={{0,5},{1,4},{2,7},{3,6},{4,1},{5,0},{6,3},{7,2},{8,13},{9,12},{10,... | collective-permute-start | bytes 983048 | tf_op jit(solution)/shard_map/ppermute | solution.py:317
  28.7 42.4 %collective-permute-start.26 = (bf16[2,16,5120]{2,1,0:T(8,128)(2,1)S(1)}, bf16[2,16,5120]{2,1,0:T(8,128)(2,1)S(1)}, u32[]{:S(2)}, u32[]{:S(2)}) collective-permute-start(bf16[2,16,5120]{2,1,0:T(8,128)(2,1)S(1)} %get-tuple-element.31), channel_id=1, source_target_pairs={{0,6},{1,7},{2,4},{3,5},{4,2},{5,3},{6,0},{7,1},{8,14},{9,15},{10,... | collective-permute-start | bytes 983048 | tf_op jit(solution)/shard_map/ppermute | solution.py:317
  41.8 29.8 %collective-permute-start.30 = (bf16[2,16,5120]{2,1,0:T(8,128)(2,1)S(1)}, bf16[2,16,5120]{2,1,0:T(8,128)(2,1)S(1)}, u32[]{:S(2)}, u32[]{:S(2)}) collective-permute-start(bf16[2,16,5120]{2,1,0:T(8,128)(2,1)S(1)} %get-tuple-element.32), channel_id=1, source_target_pairs={{0,7},{1,6},{2,5},{3,4},{4,3},{5,2},{6,1},{7,0},{8,15},{9,14},{10,... | collective-permute-start | bytes 983048 | tf_op jit(solution)/shard_map/ppermute | solution.py:317
  48.1 24.1 %collective-permute-start.5 = (bf16[2,16,5120]{2,1,0:T(8,128)(2,1)S(1)}, bf16[2,16,5120]{2,1,0:T(8,128)(2,1)S(1)}, u32[]{:S(2)}, u32[]{:S(2)}) collective-permute-start(bf16[2,16,5120]{2,1,0:T(8,128)(2,1)S(1)} %collective-permute-done.3.refs_1_), channel_id=1, source_target_pairs={{0,16},{8,24},{16,0},{24,8},{1,17},{9,25},{17,1},{25,9},{2,18},{10... | collective-permute-start | bytes 983048 | tf_op jit(solution)/shard_map/ppermute | solution.py:317
  50.6 23.1 %collective-permute-start.7 = (bf16[2,16,5120]{2,1,0:T(8,128)(2,1)S(1)}, bf16[2,16,5120]{2,1,0:T(8,128)(2,1)S(1)}, u32[]{:S(2)}, u32[]{:S(2)}) collective-permute-start(bf16[2,16,5120]{2,1,0:T(8,128)(2,1)S(1)} %collective-permute-done.6.refs_4_), channel_id=1, source_target_pairs={{0,16},{8,24},{16,0},{24,8},{1,17},{9,25},{17,1},{25,9},{2,18},{10... | collective-permute-start | bytes 983048 | tf_op jit(solution)/shard_map/ppermute | solution.py:317
  69.6 10.6 %collective-permute-start.8 = (bf16[2,16,5120]{2,1,0:T(8,128)(2,1)S(1)}, bf16[2,16,5120]{2,1,0:T(8,128)(2,1)S(1)}, u32[]{:S(2)}, u32[]{:S(2)}) collective-permute-start(bf16[2,16,5120]{2,1,0:T(8,128)(2,1)S(1)} %collective-permute-done.6.refs_4_), channel_id=1, source_target_pairs={{0,8},{8,0},{16,24},{24,16},{1,9},{9,1},{17,25},{25,17},{2,10},{10... | collective-permute-start | bytes 983048 | tf_op jit(solution)/shard_map/ppermute | solution.py:317
  71.1 16.1 %collective-permute-start.11 = (bf16[2,16,5120]{2,1,0:T(8,128)(2,1)S(1)}, bf16[2,16,5120]{2,1,0:T(8,128)(2,1)S(1)}, u32[]{:S(2)}, u32[]{:S(2)}) collective-permute-start(bf16[2,16,5120]{2,1,0:T(8,128)(2,1)S(1)} %collective-permute-done.10.refs_8_), channel_id=1, source_target_pairs={{0,8},{8,0},{16,24},{24,16},{1,9},{9,1},{17,25},{25,17},{2,10},{10... | collective-permute-start | bytes 983048 | tf_op jit(solution)/shard_map/ppermute | solution.py:317
  71.7 16.1 %collective-permute-start.12 = (bf16[2,16,5120]{2,1,0:T(8,128)(2,1)S(1)}, bf16[2,16,5120]{2,1,0:T(8,128)(2,1)S(1)}, u32[]{:S(2)}, u32[]{:S(2)}) collective-permute-start(bf16[2,16,5120]{2,1,0:T(8,128)(2,1)S(1)} %collective-permute-done.10.refs_8_), channel_id=1, source_target_pairs={{0,16},{8,24},{16,0},{24,8},{1,17},{9,25},{17,1},{25,9},{2,18},{10... | collective-permute-start | bytes 983048 | tf_op jit(solution)/shard_map/ppermute | solution.py:317
  72.2 17.1 %collective-permute-start.15 = (bf16[2,16,5120]{2,1,0:T(8,128)(2,1)S(1)}, bf16[2,16,5120]{2,1,0:T(8,128)(2,1)S(1)}, u32[]{:S(2)}, u32[]{:S(2)}) collective-permute-start(bf16[2,16,5120]{2,1,0:T(8,128)(2,1)S(1)} %collective-permute-done.14.refs_12_), channel_id=1, source_target_pairs={{0,16},{8,24},{16,0},{24,8},{1,17},{9,25},{17,1},{25,9},{2,18},{10... | collective-permute-start | bytes 983048 | tf_op jit(solution)/shard_map/ppermute | solution.py:317
  73.7 20.6 %collective-permute-start.16 = (bf16[2,16,5120]{2,1,0:T(8,128)(2,1)S(1)}, bf16[2,16,5120]{2,1,0:T(8,128)(2,1)S(1)}, u32[]{:S(2)}, u32[]{:S(2)}) collective-permute-start(bf16[2,16,5120]{2,1,0:T(8,128)(2,1)S(1)} %collective-permute-done.14.refs_12_), channel_id=1, source_target_pairs={{0,8},{8,0},{16,24},{24,16},{1,9},{9,1},{17,25},{25,17},{2,10},{10... | collective-permute-start | bytes 983048 | tf_op jit(solution)/shard_map/ppermute | solution.py:317
  80.2 21.1 %collective-permute-start.19 = (bf16[2,16,5120]{2,1,0:T(8,128)(2,1)S(1)}, bf16[2,16,5120]{2,1,0:T(8,128)(2,1)S(1)}, u32[]{:S(2)}, u32[]{:S(2)}) collective-permute-start(bf16[2,16,5120]{2,1,0:T(8,128)(2,1)S(1)} %collective-permute-done.18.refs_16_), channel_id=1, source_target_pairs={{0,8},{8,0},{16,24},{24,16},{1,9},{9,1},{17,25},{25,17},{2,10},{10... | collective-permute-start | bytes 983048 | tf_op jit(solution)/shard_map/ppermute | solution.py:317
  87.2 14.6 %collective-permute-start.20 = (bf16[2,16,5120]{2,1,0:T(8,128)(2,1)S(1)}, bf16[2,16,5120]{2,1,0:T(8,128)(2,1)S(1)}, u32[]{:S(2)}, u32[]{:S(2)}) collective-permute-start(bf16[2,16,5120]{2,1,0:T(8,128)(2,1)S(1)} %collective-permute-done.18.refs_16_), channel_id=1, source_target_pairs={{0,16},{8,24},{16,0},{24,8},{1,17},{9,25},{17,1},{25,9},{2,18},{10... | collective-permute-start | bytes 983048 | tf_op jit(solution)/shard_map/ppermute | solution.py:317
  87.7 15.5 %collective-permute-start.23 = (bf16[2,16,5120]{2,1,0:T(8,128)(2,1)S(1)}, bf16[2,16,5120]{2,1,0:T(8,128)(2,1)S(1)}, u32[]{:S(2)}, u32[]{:S(2)}) collective-permute-start(bf16[2,16,5120]{2,1,0:T(8,128)(2,1)S(1)} %collective-permute-done.22.refs_20_), channel_id=1, source_target_pairs={{0,16},{8,24},{16,0},{24,8},{1,17},{9,25},{17,1},{25,9},{2,18},{10... | collective-permute-start | bytes 983048 | tf_op jit(solution)/shard_map/ppermute | solution.py:317
  89.3 19.0 %collective-permute-start.24 = (bf16[2,16,5120]{2,1,0:T(8,128)(2,1)S(1)}, bf16[2,16,5120]{2,1,0:T(8,128)(2,1)S(1)}, u32[]{:S(2)}, u32[]{:S(2)}) collective-permute-start(bf16[2,16,5120]{2,1,0:T(8,128)(2,1)S(1)} %collective-permute-done.22.refs_20_), channel_id=1, source_target_pairs={{0,8},{8,0},{16,24},{24,16},{1,9},{9,1},{17,25},{25,17},{2,10},{10... | collective-permute-start | bytes 983048 | tf_op jit(solution)/shard_map/ppermute | solution.py:317
  94.2 21.1 %collective-permute-start.27 = (bf16[2,16,5120]{2,1,0:T(8,128)(2,1)S(1)}, bf16[2,16,5120]{2,1,0:T(8,128)(2,1)S(1)}, u32[]{:S(2)}, u32[]{:S(2)}) collective-permute-start(bf16[2,16,5120]{2,1,0:T(8,128)(2,1)S(1)} %collective-permute-done.26.refs_0_), channel_id=1, source_target_pairs={{0,8},{8,0},{16,24},{24,16},{1,9},{9,1},{17,25},{25,17},{2,10},{10... | collective-permute-start | bytes 983048 | tf_op jit(solution)/shard_map/ppermute | solution.py:317
  101.3 14.6 %collective-permute-start.31 = (bf16[2,16,5120]{2,1,0:T(8,128)(2,1)S(1)}, bf16[2,16,5120]{2,1,0:T(8,128)(2,1)S(1)}, u32[]{:S(2)}, u32[]{:S(2)}) collective-permute-start(bf16[2,16,5120]{2,1,0:T(8,128)(2,1)S(1)} %collective-permute-done.30.refs_4_), channel_id=1, source_target_pairs={{0,16},{8,24},{16,0},{24,8},{1,17},{9,25},{17,1},{25,9},{2,18},{10... | collective-permute-start | bytes 983048 | tf_op jit(solution)/shard_map/ppermute | solution.py:317
  101.8 20.6 %collective-permute-start.9 = (bf16[2,16,5120]{2,1,0:T(8,128)(2,1)S(1)}, bf16[2,16,5120]{2,1,0:T(8,128)(2,1)S(1)}, u32[]{:S(2)}, u32[]{:S(2)}) collective-permute-start(bf16[2,16,5120]{2,1,0:T(8,128)(2,1)S(1)} %collective-permute-done.7.refs_5_), channel_id=1, source_target_pairs={{0,8},{8,0},{16,24},{24,16},{1,9},{9,1},{17,25},{25,17},{2,10},{10... | collective-permute-start | bytes 983048 | tf_op jit(solution)/shard_map/ppermute | solution.py:317
  103.3 20.6 %collective-permute-start.13 = (bf16[2,16,5120]{2,1,0:T(8,128)(2,1)S(1)}, bf16[2,16,5120]{2,1,0:T(8,128)(2,1)S(1)}, u32[]{:S(2)}, u32[]{:S(2)}) collective-permute-start(bf16[2,16,5120]{2,1,0:T(8,128)(2,1)S(1)} %collective-permute-done.11.refs_9_), channel_id=1, source_target_pairs={{0,16},{8,24},{16,0},{24,8},{1,17},{9,25},{17,1},{25,9},{2,18},{10... | collective-permute-start | bytes 983048 | tf_op jit(solution)/shard_map/ppermute | solution.py:317
  108.3 21.1 %collective-permute-start.17 = (bf16[2,16,5120]{2,1,0:T(8,128)(2,1)S(1)}, bf16[2,16,5120]{2,1,0:T(8,128)(2,1)S(1)}, u32[]{:S(2)}, u32[]{:S(2)}) collective-permute-start(bf16[2,16,5120]{2,1,0:T(8,128)(2,1)S(1)} %collective-permute-done.15.refs_13_), channel_id=1, source_target_pairs={{0,8},{8,0},{16,24},{24,16},{1,9},{9,1},{17,25},{25,17},{2,10},{10... | collective-permute-start | bytes 983048 | tf_op jit(solution)/shard_map/ppermute | solution.py:317
  115.3 14.6 %collective-permute-start.21 = (bf16[2,16,5120]{2,1,0:T(8,128)(2,1)S(1)}, bf16[2,16,5120]{2,1,0:T(8,128)(2,1)S(1)}, u32[]{:S(2)}, u32[]{:S(2)}) collective-permute-start(bf16[2,16,5120]{2,1,0:T(8,128)(2,1)S(1)} %collective-permute-done.19.refs_17_), channel_id=1, source_target_pairs={{0,16},{8,24},{16,0},{24,8},{1,17},{9,25},{17,1},{25,9},{2,18},{10... | collective-permute-start | bytes 983048 | tf_op jit(solution)/shard_map/ppermute | solution.py:317
  115.8 26.4 %collective-permute-start.28 = (bf16[2,16,5120]{2,1,0:T(8,128)(2,1)S(1)}, bf16[2,16,5120]{2,1,0:T(8,128)(2,1)S(1)}, u32[]{:S(2)}, u32[]{:S(2)}) collective-permute-start(bf16[2,16,5120]{2,1,0:T(8,128)(2,1)S(1)} %collective-permute-done.26.refs_0_), channel_id=1, source_target_pairs={{0,16},{8,24},{16,0},{24,8},{1,17},{9,25},{17,1},{25,9},{2,18},{10... | collective-permute-start | bytes 983048 | tf_op jit(solution)/shard_map/ppermute | solution.py:317
  122.3 14.0 %collective-permute-start.25 = (bf16[2,16,5120]{2,1,0:T(8,128)(2,1)S(1)}, bf16[2,16,5120]{2,1,0:T(8,128)(2,1)S(1)}, u32[]{:S(2)}, u32[]{:S(2)}) collective-permute-start(bf16[2,16,5120]{2,1,0:T(8,128)(2,1)S(1)} %collective-permute-done.23.refs_21_), channel_id=1, source_target_pairs={{0,8},{8,0},{16,24},{24,16},{1,9},{9,1},{17,25},{25,17},{2,10},{10... | collective-permute-start | bytes 983048 | tf_op jit(solution)/shard_map/ppermute | solution.py:317
  123.8 19.6 %collective-permute-start.32 = (bf16[2,16,5120]{2,1,0:T(8,128)(2,1)S(1)}, bf16[2,16,5120]{2,1,0:T(8,128)(2,1)S(1)}, u32[]{:S(2)}, u32[]{:S(2)}) collective-permute-start(bf16[2,16,5120]{2,1,0:T(8,128)(2,1)S(1)} %collective-permute-done.30.refs_4_), channel_id=1, source_target_pairs={{0,8},{8,0},{16,24},{24,16},{1,9},{9,1},{17,25},{25,17},{2,10},{10... | collective-permute-start | bytes 983048 | tf_op jit(solution)/shard_map/ppermute | solution.py:317
  129.4 14.0 %collective-permute-start.29 = (bf16[2,16,5120]{2,1,0:T(8,128)(2,1)S(1)}, bf16[2,16,5120]{2,1,0:T(8,128)(2,1)S(1)}, u32[]{:S(2)}, u32[]{:S(2)}) collective-permute-start(bf16[2,16,5120]{2,1,0:T(8,128)(2,1)S(1)} %collective-permute-done.27.refs_1_), channel_id=1, source_target_pairs={{0,16},{8,24},{16,0},{24,8},{1,17},{9,25},{17,1},{25,9},{2,18},{10... | collective-permute-start | bytes 983048 | tf_op jit(solution)/shard_map/ppermute | solution.py:317
  129.9 18.4 %collective-permute-start.33 = (bf16[2,16,5120]{2,1,0:T(8,128)(2,1)S(1)}, bf16[2,16,5120]{2,1,0:T(8,128)(2,1)S(1)}, u32[]{:S(2)}, u32[]{:S(2)}) collective-permute-start(bf16[2,16,5120]{2,1,0:T(8,128)(2,1)S(1)} %collective-permute-done.31.refs_5_), channel_id=1, source_target_pairs={{0,8},{8,0},{16,24},{24,16},{1,9},{9,1},{17,25},{25,17},{2,10},{10... | collective-permute-start | bytes 983048 | tf_op jit(solution)/shard_map/ppermute | solution.py:317

commit v4 on v3

--- a/solution.py
+++ b/solution.py
@@ -104,17 +104,12 @@
                     rows[m * chunk : (m + 1) * chunk, col : col + LANES] = total.astype(
                         rows.dtype
                     )
-        left, right = (
-            rows[:, q * fine : (q + 1) * fine].astype(jnp.bfloat16) for q in range(2)
-        )
-        first = jnp.dot(left, table[...], preferred_element_type=jnp.float32)
-        second = jnp.dot(right, table[...], preferred_element_type=jnp.float32)
+        first = jnp.dot(rows[:, :fine], table[...], preferred_element_type=jnp.float32)
+        second = jnp.dot(rows[:, fine:], table[...], preferred_element_type=jnp.float32)
         real = first[:, :fine] + second[:, fine:]
         imag = second[:, :fine] - first[:, fine:]
         for m in range(frames_out):
-            lead = m * fine
-            if not near:
-                lead = pl.multiple_of(polar * (frames_out * fine) + lead, LANES)
+            lead = pl.multiple_of((polar * frames_out + m) * fine, LANES)
             here = slice(m * chunk, (m + 1) * chunk)
             out[0, :, pl.ds(lead, fine)] = real[here].astype(jnp.bfloat16)
             out[1, :, pl.ds(lead, fine)] = imag[here].astype(jnp.bfloat16)
@@ -124,47 +119,38 @@
     slots, polars, _, per_pair, _ = view.shape
     taps, fine = filter_taps.shape
     frames_out = per_pair // 8 - taps + 1
-    width = frames_out * fine
     pitch = per_pair + 1
     near = plane == 0
-    shapes = [jax.ShapeDtypeStruct((2, slots, polars * width), jnp.bfloat16)] * 2
+    shapes = [jax.ShapeDtypeStruct((2, slots, polars * frames_out * fine), jnp.bfloat16)] * 2
     if near:
-        chunk = slots // 2
         keep = [pltpu.with_memory_space_constraint(x, pltpu.HBM) for x in (view, filter_taps, table)]
-        grid = (polars, slots // chunk)
         in_specs = [
             pl.BlockSpec(
-                (chunk, 1, 1, per_pair, LANES), lambda p, h, info: (h, p, info[1] >> 1, 0, 0)
+                (slots, 1, 1, per_pair, LANES), lambda p, info: (0, p, info[1] >> 1, 0, 0)
             ),
-            pl.BlockSpec((taps, fine), lambda p, h, info: (0, 0)),
-            pl.BlockSpec((fine, 2 * fine), lambda p, h, info: (0, 0)),
+            pl.BlockSpec((taps, fine), lambda p, info: (0, 0)),
+            pl.BlockSpec((fine, 2 * fine), lambda p, info: (0, 0)),
         ]
-        out_specs = [pl.BlockSpec((2, chunk, width), lambda p, h, info: (0, h, p))] * 2
-        kind = jnp.float32
     else:
-        chunk = slots
         keep = [view, filter_taps, table]
-        grid = (polars,)
         in_specs = [VMEM_WHOLE] * 3
-        out_specs = [VMEM_WHOLE] * 2
-        kind = jnp.bfloat16
     return pl.pallas_call(
         functools.partial(
-            spectra_body, (taps, frames_out, per_pair, pitch, chunk), plane, near
+            spectra_body, (taps, frames_out, per_pair, pitch, slots), plane, near
         ),
         grid_spec=pltpu.PrefetchScalarGridSpec(
             num_scalar_prefetch=1,
-            grid=grid,
+            grid=(polars,),
             in_specs=in_specs,
-            out_specs=out_specs,
+            out_specs=[VMEM_WHOLE] * 2,
             scratch_shapes=[
-                pltpu.VMEM((chunk * pitch, LANES), jnp.float32),
-                pltpu.VMEM((frames_out * chunk, 2 * fine), kind),
+                pltpu.VMEM((slots * pitch, LANES), jnp.float32),
+                pltpu.VMEM((frames_out * slots, 2 * fine), jnp.bfloat16),
             ],
         ),
         out_shape=shapes,
         compiler_params=pltpu.CompilerParams(
-            dimension_semantics=("arbitrary",) * len(grid), vmem_limit_bytes=KERNEL_VMEM
+            dimension_semantics=("arbitrary",), vmem_limit_bytes=KERNEL_VMEM
         ),
         name="spectra",
     )(info, *keep)

time: 153 us -> 153 us (level)
  no operation moved by 1% of the time
where the time goes in v4:
time: 153 us; the launch traced here: 151 us
  waiting for transfers between devices  84.8 us (55%)
  starting transfers between devices  42.9 us (28%)
  Pallas kernels  22.6 us (15%)
    ppermute x34, waiting for transfers between devices, swap(): return lax.ppermute(array, axis, [(i, i ^ step) for i in range(size)])  84.8 us
    ppermute x34, starting transfers between devices, swap(): return lax.ppermute(array, axis, [(i, i ^ step) for i in range(size)])  42.9 us
    pallas_call x4, Pallas kernels, spectra_pair(): pl.pallas_call(functools.partial(spectra_body, (taps, frames_out, per_pai...  11.2 us
    pallas_call x1, Pallas kernels, beam_early(): pl.pallas_call(functools.partial(early_body, [(g, j) for g, j, _ in piece...  5.84 us
    pallas_call x1, Pallas kernels, beam_late(): pl.pallas_call(functools.partial(late_body, [(g, j) for g, j, _ in pieces...  3.7 us
  transfers between devices with their start and end apart: 34, of which 15 were waited for; matrix products, arithmetic and copies ran while one was open for 0% of the time, Pallas kernels for 10%

profile of v4, /device:TPU:0, one launch (start us, length us, event | category | flops | bytes accessed | tf_op | source)
XLA Modules:
  0.0 151.2 jit_solution(7473734233692468996)
XLA Ops:
  0.1 3.9 %spectra.4 = (bf16[2,16,5120]{2,1,0:T(8,128)(2,1)S(1)}, bf16[2,16,5120]{2,1,0:T(8,128)(2,1)S(1)}) custom-call(s32[2]{0:T(128)S(1)} %pad_add_fusion.info, bf16[16,2,4,168,128]{4,3,2,1,0:T(8,128)(2,1)} %bitcast.18, f32[12,256]{1,0:T(8,128)} %taps_ref.7, bf16[256,512]{1,0:T(8,128)(2,1)} %constant.14.table), custom_call_target="tpu_custom_call" | custom-call | tf_op jit(solution)/shard_map/spectra/pallas_call | solution.py:137
  4.0 3.1 %collective-permute-start.3 = (bf16[2,16,5120]{2,1,0:T(8,128)(2,1)S(1)}, bf16[2,16,5120]{2,1,0:T(8,128)(2,1)S(1)}, u32[]{:S(2)}, u32[]{:S(2)}) collective-permute-start(bf16[2,16,5120]{2,1,0:T(8,128)(2,1)S(1)} %get-tuple-element.25.refs_0_), channel_id=1, source_target_pairs={{0,8},{8,0},{16,24},{24,16},{1,9},{9,1},{17,25},{25,17},{2,10},{10... | collective-permute-start | bytes 983048 | tf_op jit(solution)/shard_map/ppermute | solution.py:303
  7.7 0.8 mask.1
  8.6 2.0 %collective-permute-start.1 = (bf16[2,8,16,256]{3,2,1,0:T(8,128)(2,1)S(1)}, bf16[2,8,16,256]{3,2,1,0:T(8,128)(2,1)S(1)}, u32[]{:S(2)}, u32[]{:S(2)}) collective-permute-start(bf16[2,8,16,256]{3,2,1,0:T(8,128)(2,1)S(1)} %get-tuple-element.21), channel_id=1, source_target_pairs={{0,16},{8,24},{16,0},{24,8},{1,17},{9,25},{17,1},{25,9},{2,18},{10... | collective-permute-start | bytes 393224 | tf_op jit(solution)/shard_map/ppermute | solution.py:303
  10.6 1.4 collective-permute-start.2
  12.1 1.5 %collective-permute-start.4 = (bf16[2,16,5120]{2,1,0:T(8,128)(2,1)S(1)}, bf16[2,16,5120]{2,1,0:T(8,128)(2,1)S(1)}, u32[]{:S(2)}, u32[]{:S(2)}) collective-permute-start(bf16[2,16,5120]{2,1,0:T(8,128)(2,1)S(1)} %get-tuple-element.25.refs_0_), channel_id=1, source_target_pairs={{0,16},{8,24},{16,0},{24,8},{1,17},{9,25},{17,1},{25,9},{2,18},{10... | collective-permute-start | bytes 983048 | tf_op jit(solution)/shard_map/ppermute | solution.py:303
  13.6 2.5 %spectra.5 = (bf16[2,16,5120]{2,1,0:T(8,128)(2,1)S(1)}, bf16[2,16,5120]{2,1,0:T(8,128)(2,1)S(1)}) custom-call(s32[2]{0:T(128)S(1)} %pad_add_fusion.info, bf16[16,2,4,168,128]{4,3,2,1,0:T(8,128)(2,1)S(1)} %bitcast.19, f32[12,256]{1,0:T(8,128)S(1)} %copy-done.3, bf16[256,512]{1,0:T(8,128)(2,1)S(1)} %copy-done.1), custom_call_target="tpu_custom_call" | custom-call | tf_op jit(solution)/shard_map/spectra/pallas_call | solution.py:137
  16.1 2.5 %spectra.6 = (bf16[2,16,5120]{2,1,0:T(8,128)(2,1)S(1)}, bf16[2,16,5120]{2,1,0:T(8,128)(2,1)S(1)}) custom-call(s32[2]{0:T(128)S(1)} %pad_add_fusion.info, bf16[16,2,4,168,128]{4,3,2,1,0:T(8,128)(2,1)S(1)} %bitcast.20, f32[12,256]{1,0:T(8,128)S(1)} %copy-done.3, bf16[256,512]{1,0:T(8,128)(2,1)S(1)} %copy-done.1), custom_call_target="tpu_custom_call" | custom-call | tf_op jit(solution)/shard_map/spectra/pallas_call | solution.py:137
  18.6 1.9 %collective-permute-start.10 = (bf16[2,16,5120]{2,1,0:T(8,128)(2,1)S(1)}, bf16[2,16,5120]{2,1,0:T(8,128)(2,1)S(1)}, u32[]{:S(2)}, u32[]{:S(2)}) collective-permute-start(bf16[2,16,5120]{2,1,0:T(8,128)(2,1)S(1)} %get-tuple-element.27), channel_id=1, source_target_pairs={{0,2},{1,3},{2,0},{3,1},{4,6},{5,7},{6,4},{7,5},{8,10},{9,11},{10,... | collective-permute-start | bytes 983048 | tf_op jit(solution)/shard_map/ppermute | solution.py:303
  20.5 1.1 collective-permute-done.2
  21.6 2.6 %collective-permute-start.18 = (bf16[2,16,5120]{2,1,0:T(8,128)(2,1)S(1)}, bf16[2,16,5120]{2,1,0:T(8,128)(2,1)S(1)}, u32[]{:S(2)}, u32[]{:S(2)}) collective-permute-start(bf16[2,16,5120]{2,1,0:T(8,128)(2,1)S(1)} %get-tuple-element.29), channel_id=1, source_target_pairs={{0,4},{1,5},{2,6},{3,7},{4,0},{5,1},{6,2},{7,3},{8,12},{9,13},{10,... | collective-permute-start | bytes 983048 | tf_op jit(solution)/shard_map/ppermute | solution.py:303
  24.2 2.5 %spectra.7 = (bf16[2,16,5120]{2,1,0:T(8,128)(2,1)S(1)}, bf16[2,16,5120]{2,1,0:T(8,128)(2,1)S(1)}) custom-call(s32[2]{0:T(128)S(1)} %pad_add_fusion.info, bf16[16,2,4,168,128]{4,3,2,1,0:T(8,128)(2,1)S(1)} %bitcast.21, f32[12,256]{1,0:T(8,128)S(1)} %copy-done.3, bf16[256,512]{1,0:T(8,128)(2,1)S(1)} %copy-done.1), custom_call_target="tpu_custom_call" | custom-call | tf_op jit(solution)/shard_map/spectra/pallas_call | solution.py:137
  26.7 1.4 collective-permute-start.22
  28.1 2.5 %collective-permute-start.26 = (bf16[2,16,5120]{2,1,0:T(8,128)(2,1)S(1)}, bf16[2,16,5120]{2,1,0:T(8,128)(2,1)S(1)}, u32[]{:S(2)}, u32[]{:S(2)}) collective-permute-start(bf16[2,16,5120]{2,1,0:T(8,128)(2,1)S(1)} %get-tuple-element.31), channel_id=1, source_target_pairs={{0,6},{1,7},{2,4},{3,5},{4,2},{5,3},{6,0},{7,1},{8,14},{9,15},{10,... | collective-permute-start | bytes 983048 | tf_op jit(solution)/shard_map/ppermute | solution.py:303
  30.5 10.8 %collective-permute-done.10.refs_8_ = bf16[2,16,5120]{2,1,0:T(8,128)(2,1)S(1)} collective-permute-done((bf16[2,16,5120]{2,1,0:T(8,128)(2,1)S(1)}, bf16[2,16,5120]{2,1,0:T(8,128)(2,1)S(1)}, u32[]{:S(2)}, u32[]{:S(2)}) %collective-permute-start.10) | collective-permute-done | bytes 327712 | tf_op jit(solution)/shard_map/ppermute | solution.py:303
  41.3 0.8 collective-permute-start.30
  42.2 5.5 %collective-permute-done.14.refs_12_ = bf16[2,16,5120]{2,1,0:T(8,128)(2,1)S(1)} collective-permute-done((bf16[2,16,5120]{2,1,0:T(8,128)(2,1)S(1)}, bf16[2,16,5120]{2,1,0:T(8,128)(2,1)S(1)}, u32[]{:S(2)}, u32[]{:S(2)}) %collective-permute-start.14) | collective-permute-done | bytes 327712 | tf_op jit(solution)/shard_map/ppermute | solution.py:303
  47.6 2.4 %collective-permute-start.5 = (bf16[2,16,5120]{2,1,0:T(8,128)(2,1)S(1)}, bf16[2,16,5120]{2,1,0:T(8,128)(2,1)S(1)}, u32[]{:S(2)}, u32[]{:S(2)}) collective-permute-start(bf16[2,16,5120]{2,1,0:T(8,128)(2,1)S(1)} %collective-permute-done.3.refs_1_), channel_id=1, source_target_pairs={{0,16},{8,24},{16,0},{24,8},{1,17},{9,25},{17,1},{25,9},{2,18},{10... | collective-permute-start | bytes 983048 | tf_op jit(solution)/shard_map/ppermute | solution.py:303
  50.1 18.9 %collective-permute-done.22.refs_20_ = bf16[2,16,5120]{2,1,0:T(8,128)(2,1)S(1)} collective-permute-done((bf16[2,16,5120]{2,1,0:T(8,128)(2,1)S(1)}, bf16[2,16,5120]{2,1,0:T(8,128)(2,1)S(1)}, u32[]{:S(2)}, u32[]{:S(2)}) %collective-permute-start.22) | collective-permute-done | bytes 327712 | tf_op jit(solution)/shard_map/ppermute | solution.py:303
  69.0 1.5 collective-permute-start.8
  70.5 0.5 collective-permute-start.11
  71.5 1.5 %collective-permute-start.15 = (bf16[2,16,5120]{2,1,0:T(8,128)(2,1)S(1)}, bf16[2,16,5120]{2,1,0:T(8,128)(2,1)S(1)}, u32[]{:S(2)}, u32[]{:S(2)}) collective-permute-start(bf16[2,16,5120]{2,1,0:T(8,128)(2,1)S(1)} %collective-permute-done.14.refs_12_), channel_id=1, source_target_pairs={{0,16},{8,24},{16,0},{24,8},{1,17},{9,25},{17,1},{25,9},{2,18},{10... | collective-permute-start | bytes 983048 | tf_op jit(solution)/shard_map/ppermute | solution.py:303
  73.1 1.5 collective-permute-start.16
  74.6 5.0 %collective-permute-done.8.refs_6_ = bf16[2,16,5120]{2,1,0:T(8,128)(2,1)S(1)} collective-permute-done((bf16[2,16,5120]{2,1,0:T(8,128)(2,1)S(1)}, bf16[2,16,5120]{2,1,0:T(8,128)(2,1)S(1)}, u32[]{:S(2)}, u32[]{:S(2)}) %collective-permute-start.8) | collective-permute-done | bytes 327712 | tf_op jit(solution)/shard_map/ppermute | solution.py:303
  79.6 1.5 collective-permute-start.19
  81.1 5.5 %collective-permute-done.11.refs_9_ = bf16[2,16,5120]{2,1,0:T(8,128)(2,1)S(1)} collective-permute-done((bf16[2,16,5120]{2,1,0:T(8,128)(2,1)S(1)}, bf16[2,16,5120]{2,1,0:T(8,128)(2,1)S(1)}, u32[]{:S(2)}, u32[]{:S(2)}) %collective-permute-start.11) | collective-permute-done | bytes 327712 | tf_op jit(solution)/shard_map/ppermute | solution.py:303
  87.1 1.5 %collective-permute-start.23 = (bf16[2,16,5120]{2,1,0:T(8,128)(2,1)S(1)}, bf16[2,16,5120]{2,1,0:T(8,128)(2,1)S(1)}, u32[]{:S(2)}, u32[]{:S(2)}) collective-permute-start(bf16[2,16,5120]{2,1,0:T(8,128)(2,1)S(1)} %collective-permute-done.22.refs_20_), channel_id=1, source_target_pairs={{0,16},{8,24},{16,0},{24,8},{1,17},{9,25},{17,1},{25,9},{2,18},{10... | collective-permute-start | bytes 983048 | tf_op jit(solution)/shard_map/ppermute | solution.py:303
  88.6 1.5 collective-permute-start.24
  90.1 3.5 %collective-permute-done.16.refs_14_ = bf16[2,16,5120]{2,1,0:T(8,128)(2,1)S(1)} collective-permute-done((bf16[2,16,5120]{2,1,0:T(8,128)(2,1)S(1)}, bf16[2,16,5120]{2,1,0:T(8,128)(2,1)S(1)}, u32[]{:S(2)}, u32[]{:S(2)}) %collective-permute-start.16) | collective-permute-done | bytes 327712 | tf_op jit(solution)/shard_map/ppermute | solution.py:303
  93.6 1.5 collective-permute-start.27
  95.1 5.5 %collective-permute-done.19.refs_17_ = bf16[2,16,5120]{2,1,0:T(8,128)(2,1)S(1)} collective-permute-done((bf16[2,16,5120]{2,1,0:T(8,128)(2,1)S(1)}, bf16[2,16,5120]{2,1,0:T(8,128)(2,1)S(1)}, u32[]{:S(2)}, u32[]{:S(2)}) %collective-permute-start.19) | collective-permute-done | bytes 327712 | tf_op jit(solution)/shard_map/ppermute | solution.py:303
  101.1 1.5 collective-permute-start.9
  102.6 1.5 %collective-permute-start.13 = (bf16[2,16,5120]{2,1,0:T(8,128)(2,1)S(1)}, bf16[2,16,5120]{2,1,0:T(8,128)(2,1)S(1)}, u32[]{:S(2)}, u32[]{:S(2)}) collective-permute-start(bf16[2,16,5120]{2,1,0:T(8,128)(2,1)S(1)} %collective-permute-done.11.refs_9_), channel_id=1, source_target_pairs={{0,16},{8,24},{16,0},{24,8},{1,17},{9,25},{17,1},{25,9},{2,18},{10... | collective-permute-start | bytes 983048 | tf_op jit(solution)/shard_map/ppermute | solution.py:303
  104.2 3.5 %collective-permute-done.24.refs_22_ = bf16[2,16,5120]{2,1,0:T(8,128)(2,1)S(1)} collective-permute-done((bf16[2,16,5120]{2,1,0:T(8,128)(2,1)S(1)}, bf16[2,16,5120]{2,1,0:T(8,128)(2,1)S(1)}, u32[]{:S(2)}, u32[]{:S(2)}) %collective-permute-start.24) | collective-permute-done | bytes 327712 | tf_op jit(solution)/shard_map/ppermute | solution.py:303
  107.7 1.5 collective-permute-start.17
  109.2 5.5 %collective-permute-done.27.refs_1_ = bf16[2,16,5120]{2,1,0:T(8,128)(2,1)S(1)} collective-permute-done((bf16[2,16,5120]{2,1,0:T(8,128)(2,1)S(1)}, bf16[2,16,5120]{2,1,0:T(8,128)(2,1)S(1)}, u32[]{:S(2)}, u32[]{:S(2)}) %collective-permute-start.27) | collective-permute-done | bytes 327712 | tf_op jit(solution)/shard_map/ppermute | solution.py:303
  115.2 1.5 %collective-permute-start.28 = (bf16[2,16,5120]{2,1,0:T(8,128)(2,1)S(1)}, bf16[2,16,5120]{2,1,0:T(8,128)(2,1)S(1)}, u32[]{:S(2)}, u32[]{:S(2)}) collective-permute-start(bf16[2,16,5120]{2,1,0:T(8,128)(2,1)S(1)} %collective-permute-done.26.refs_0_), channel_id=1, source_target_pairs={{0,16},{8,24},{16,0},{24,8},{1,17},{9,25},{17,1},{25,9},{2,18},{10... | collective-permute-start | bytes 983048 | tf_op jit(solution)/shard_map/ppermute | solution.py:303
  116.7 5.0 %collective-permute-done.9.refs_7_ = bf16[2,16,5120]{2,1,0:T(8,128)(2,1)S(1)} collective-permute-done((bf16[2,16,5120]{2,1,0:T(8,128)(2,1)S(1)}, bf16[2,16,5120]{2,1,0:T(8,128)(2,1)S(1)}, u32[]{:S(2)}, u32[]{:S(2)}) %collective-permute-start.9) | collective-permute-done | bytes 327712 | tf_op jit(solution)/shard_map/ppermute | solution.py:303
  121.7 1.5 collective-permute-start.25
  123.2 0.5 collective-permute-start.32
  123.7 5.0 %collective-permute-done.17.refs_15_ = bf16[2,16,5120]{2,1,0:T(8,128)(2,1)S(1)} collective-permute-done((bf16[2,16,5120]{2,1,0:T(8,128)(2,1)S(1)}, bf16[2,16,5120]{2,1,0:T(8,128)(2,1)S(1)}, u32[]{:S(2)}, u32[]{:S(2)}) %collective-permute-start.17) | collective-permute-done | bytes 327712 | tf_op jit(solution)/shard_map/ppermute | solution.py:303
  129.2 1.5 collective-permute-start.33
  130.7 1.0 turn.1
  131.8 4.0 %collective-permute-done.25.refs_23_ = bf16[2,16,5120]{2,1,0:T(8,128)(2,1)S(1)} collective-permute-done((bf16[2,16,5120]{2,1,0:T(8,128)(2,1)S(1)}, bf16[2,16,5120]{2,1,0:T(8,128)(2,1)S(1)}, u32[]{:S(2)}, u32[]{:S(2)}) %collective-permute-start.25) | collective-permute-done | bytes 327712 | tf_op jit(solution)/shard_map/ppermute | solution.py:303
  135.7 5.8 %early.1.partial = f32[2,256,5120]{2,1,0:T(8,128)S(1)} custom-call(bf16[2,256,768]{2,1,0:T(8,128)(2,1)S(1)} %get-tuple-element.24.weights, bf16[2,16,5120]{2,1,0:T(8,128)(2,1)S(1)} %get-tuple-element.25.refs_0_, bf16[2,16,5120]{2,1,0:T(8,128)(2,1)S(1)} %collective-permute-done.3.refs_1_, bf16[2,16,5120]{2,1,0:T(8,128)(2,1)S(1)} %collective-permute-done.4.refs_2_, ...), custom_call_target="tpu_custom_call" | custom-call | tf_op jit(solution)/shard_map/early/pallas_call | solution.py:266
  141.6 1.2 collective-permute-done.32.refs_6_
  142.8 4.7 %collective-permute-done.33.refs_7_ = bf16[2,16,5120]{2,1,0:T(8,128)(2,1)S(1)} collective-permute-done((bf16[2,16,5120]{2,1,0:T(8,128)(2,1)S(1)}, bf16[2,16,5120]{2,1,0:T(8,128)(2,1)S(1)}, u32[]{:S(2)}, u32[]{:S(2)}) %collective-permute-start.33) | collective-permute-done | bytes 327712 | tf_op jit(solution)/shard_map/ppermute | solution.py:303
  147.5 3.7 %late.1 = bf16[256,80,128]{2,1,0:T(8,128)(2,1)} custom-call(bf16[2,256,256]{2,1,0:T(8,128)(2,1)S(1)} %get-tuple-element.23.weights, f32[2,256,5120]{2,1,0:T(8,128)S(1)} %early.1.partial, bf16[2,16,5120]{2,1,0:T(8,128)(2,1)S(1)} %collective-permute-done.26.refs_0_, bf16[2,16,5120]{2,1,0:T(8,128)(2,1)S(1)} %collective-permute-done.27.refs_1_, ...), custom_call_target="tpu_custom_call" | custom-call | tf_op jit(solution)/shard_map/late/pallas_call | solution.py:285
  (39 shorter events, 2.9 us)
Async XLA Ops:
  0.0 13.6 %copy-start.1 = (bf16[256,512]{1,0:T(8,128)(2,1)S(1)}, bf16[256,512]{1,0:T(8,128)(2,1)}, u32[]{:S(2)}) copy-start(bf16[256,512]{1,0:T(8,128)(2,1)} %constant.14.table) | copy-start | bytes 786436
  0.0 13.6 %copy-start.3 = (f32[12,256]{1,0:T(8,128)S(1)}, f32[12,256]{1,0:T(8,128)}, u32[]{:S(2)}) copy-start(f32[12,256]{1,0:T(8,128)} %taps_ref.7) | copy-start | bytes 36868
  0.0 7.7 %copy-start.4 = (s32[128]{0:T(128)S(1)}, s32[128]{0:T(128)}, u32[]{:S(2)}) copy-start(s32[128]{0:T(128)} %param.9) | copy-start | bytes 1540
  0.0 7.7 %copy-start.2 = (bf16[1,2,128,1024]{3,2,1,0:T(8,128)(2,1)S(1)}, bf16[1,2,128,1024]{3,2,1,0:T(8,128)(2,1)}, u32[]{:S(2)}) copy-start(bf16[1,2,128,1024]{3,2,1,0:T(8,128)(2,1)} %param.8) | copy-start | bytes 1572868
  0.0 13.6 %copy-start = (bf16[16,2,8,2,5376]{4,3,2,1,0:T(2,128)(2,1)S(1)}, bf16[16,2,8,2,5376]{4,3,2,1,0:T(2,128)(2,1)}, u32[]{:S(2)}) copy-start(bf16[16,2,8,2,5376]{4,3,2,1,0:T(2,128)(2,1)} %param.6) | copy-start | bytes 16515076
  4.0 17.7 %collective-permute-start.3 = (bf16[2,16,5120]{2,1,0:T(8,128)(2,1)S(1)}, bf16[2,16,5120]{2,1,0:T(8,128)(2,1)S(1)}, u32[]{:S(2)}, u32[]{:S(2)}) collective-permute-start(bf16[2,16,5120]{2,1,0:T(8,128)(2,1)S(1)} %get-tuple-element.25.refs_0_), channel_id=1, source_target_pairs={{0,8},{8,0},{16,24},{24,16},{1,9},{9,1},{17,25},{25,17},{2,10},{10... | collective-permute-start | bytes 983048 | tf_op jit(solution)/shard_map/ppermute | solution.py:303
  8.5 10.0 %collective-permute-start = (bf16[2,8,16,256]{3,2,1,0:T(8,128)(2,1)S(1)}, bf16[2,8,16,256]{3,2,1,0:T(8,128)(2,1)S(1)}, u32[]{:S(2)}, u32[]{:S(2)}) collective-permute-start(bf16[2,8,16,256]{3,2,1,0:T(8,128)(2,1)S(1)} %get-tuple-element.20), channel_id=1, source_target_pairs={{0,8},{8,0},{16,24},{24,16},{1,9},{9,1},{17,25},{25,17},{2,10},{10... | collective-permute-start | bytes 393224 | tf_op jit(solution)/shard_map/ppermute | solution.py:303
  8.6 10.0 %collective-permute-start.1 = (bf16[2,8,16,256]{3,2,1,0:T(8,128)(2,1)S(1)}, bf16[2,8,16,256]{3,2,1,0:T(8,128)(2,1)S(1)}, u32[]{:S(2)}, u32[]{:S(2)}) collective-permute-start(bf16[2,8,16,256]{3,2,1,0:T(8,128)(2,1)S(1)} %get-tuple-element.21), channel_id=1, source_target_pairs={{0,16},{8,24},{16,0},{24,8},{1,17},{9,25},{17,1},{25,9},{2,18},{10... | collective-permute-start | bytes 393224 | tf_op jit(solution)/shard_map/ppermute | solution.py:303
  10.6 11.0 %collective-permute-start.2 = (bf16[2,8,16,256]{3,2,1,0:T(8,128)(2,1)S(1)}, bf16[2,8,16,256]{3,2,1,0:T(8,128)(2,1)S(1)}, u32[]{:S(2)}, u32[]{:S(2)}) collective-permute-start(bf16[2,8,16,256]{3,2,1,0:T(8,128)(2,1)S(1)} %get-tuple-element.22), channel_id=1, source_target_pairs={{0,24},{8,16},{16,8},{24,0},{1,25},{9,17},{17,9},{25,1},{2,26},{10... | collective-permute-start | bytes 393224 | tf_op jit(solution)/shard_map/ppermute | solution.py:303
  12.1 14.6 %collective-permute-start.4 = (bf16[2,16,5120]{2,1,0:T(8,128)(2,1)S(1)}, bf16[2,16,5120]{2,1,0:T(8,128)(2,1)S(1)}, u32[]{:S(2)}, u32[]{:S(2)}) collective-permute-start(bf16[2,16,5120]{2,1,0:T(8,128)(2,1)S(1)} %get-tuple-element.25.refs_0_), channel_id=1, source_target_pairs={{0,16},{8,24},{16,0},{24,8},{1,17},{9,25},{17,1},{25,9},{2,18},{10... | collective-permute-start | bytes 983048 | tf_op jit(solution)/shard_map/ppermute | solution.py:303
  18.5 9.5 %collective-permute-start.6 = (bf16[2,16,5120]{2,1,0:T(8,128)(2,1)S(1)}, bf16[2,16,5120]{2,1,0:T(8,128)(2,1)S(1)}, u32[]{:S(2)}, u32[]{:S(2)}) collective-permute-start(bf16[2,16,5120]{2,1,0:T(8,128)(2,1)S(1)} %get-tuple-element.26), channel_id=1, source_target_pairs={{0,1},{1,0},{2,3},{3,2},{4,5},{5,4},{6,7},{7,6},{8,9},{9,8},{10,11... | collective-permute-start | bytes 983048 | tf_op jit(solution)/shard_map/ppermute | solution.py:303
  18.6 22.7 %collective-permute-start.10 = (bf16[2,16,5120]{2,1,0:T(8,128)(2,1)S(1)}, bf16[2,16,5120]{2,1,0:T(8,128)(2,1)S(1)}, u32[]{:S(2)}, u32[]{:S(2)}) collective-permute-start(bf16[2,16,5120]{2,1,0:T(8,128)(2,1)S(1)} %get-tuple-element.27), channel_id=1, source_target_pairs={{0,2},{1,3},{2,0},{3,1},{4,6},{5,7},{6,4},{7,5},{8,10},{9,11},{10,... | collective-permute-start | bytes 983048 | tf_op jit(solution)/shard_map/ppermute | solution.py:303
  21.6 26.0 %collective-permute-start.14 = (bf16[2,16,5120]{2,1,0:T(8,128)(2,1)S(1)}, bf16[2,16,5120]{2,1,0:T(8,128)(2,1)S(1)}, u32[]{:S(2)}, u32[]{:S(2)}) collective-permute-start(bf16[2,16,5120]{2,1,0:T(8,128)(2,1)S(1)} %get-tuple-element.28), channel_id=1, source_target_pairs={{0,3},{1,2},{2,1},{3,0},{4,7},{5,6},{6,5},{7,4},{8,11},{9,10},{10,... | collective-permute-start | bytes 983048 | tf_op jit(solution)/shard_map/ppermute | solution.py:303
  21.6 28.4 %collective-permute-start.18 = (bf16[2,16,5120]{2,1,0:T(8,128)(2,1)S(1)}, bf16[2,16,5120]{2,1,0:T(8,128)(2,1)S(1)}, u32[]{:S(2)}, u32[]{:S(2)}) collective-permute-start(bf16[2,16,5120]{2,1,0:T(8,128)(2,1)S(1)} %get-tuple-element.29), channel_id=1, source_target_pairs={{0,4},{1,5},{2,6},{3,7},{4,0},{5,1},{6,2},{7,3},{8,12},{9,13},{10,... | collective-permute-start | bytes 983048 | tf_op jit(solution)/shard_map/ppermute | solution.py:303
  26.7 42.3 %collective-permute-start.22 = (bf16[2,16,5120]{2,1,0:T(8,128)(2,1)S(1)}, bf16[2,16,5120]{2,1,0:T(8,128)(2,1)S(1)}, u32[]{:S(2)}, u32[]{:S(2)}) collective-permute-start(bf16[2,16,5120]{2,1,0:T(8,128)(2,1)S(1)} %get-tuple-element.30), channel_id=1, source_target_pairs={{0,5},{1,4},{2,7},{3,6},{4,1},{5,0},{6,3},{7,2},{8,13},{9,12},{10,... | collective-permute-start | bytes 983048 | tf_op jit(solution)/shard_map/ppermute | solution.py:303
  28.1 42.4 %collective-permute-start.26 = (bf16[2,16,5120]{2,1,0:T(8,128)(2,1)S(1)}, bf16[2,16,5120]{2,1,0:T(8,128)(2,1)S(1)}, u32[]{:S(2)}, u32[]{:S(2)}) collective-permute-start(bf16[2,16,5120]{2,1,0:T(8,128)(2,1)S(1)} %get-tuple-element.31), channel_id=1, source_target_pairs={{0,6},{1,7},{2,4},{3,5},{4,2},{5,3},{6,0},{7,1},{8,14},{9,15},{10,... | collective-permute-start | bytes 983048 | tf_op jit(solution)/shard_map/ppermute | solution.py:303
  41.3 29.7 %collective-permute-start.30 = (bf16[2,16,5120]{2,1,0:T(8,128)(2,1)S(1)}, bf16[2,16,5120]{2,1,0:T(8,128)(2,1)S(1)}, u32[]{:S(2)}, u32[]{:S(2)}) collective-permute-start(bf16[2,16,5120]{2,1,0:T(8,128)(2,1)S(1)} %get-tuple-element.32), channel_id=1, source_target_pairs={{0,7},{1,6},{2,5},{3,4},{4,3},{5,2},{6,1},{7,0},{8,15},{9,14},{10,... | collective-permute-start | bytes 983048 | tf_op jit(solution)/shard_map/ppermute | solution.py:303
  47.6 23.9 %collective-permute-start.5 = (bf16[2,16,5120]{2,1,0:T(8,128)(2,1)S(1)}, bf16[2,16,5120]{2,1,0:T(8,128)(2,1)S(1)}, u32[]{:S(2)}, u32[]{:S(2)}) collective-permute-start(bf16[2,16,5120]{2,1,0:T(8,128)(2,1)S(1)} %collective-permute-done.3.refs_1_), channel_id=1, source_target_pairs={{0,16},{8,24},{16,0},{24,8},{1,17},{9,25},{17,1},{25,9},{2,18},{10... | collective-permute-start | bytes 983048 | tf_op jit(solution)/shard_map/ppermute | solution.py:303
  50.0 23.0 %collective-permute-start.7 = (bf16[2,16,5120]{2,1,0:T(8,128)(2,1)S(1)}, bf16[2,16,5120]{2,1,0:T(8,128)(2,1)S(1)}, u32[]{:S(2)}, u32[]{:S(2)}) collective-permute-start(bf16[2,16,5120]{2,1,0:T(8,128)(2,1)S(1)} %collective-permute-done.6.refs_4_), channel_id=1, source_target_pairs={{0,16},{8,24},{16,0},{24,8},{1,17},{9,25},{17,1},{25,9},{2,18},{10... | collective-permute-start | bytes 983048 | tf_op jit(solution)/shard_map/ppermute | solution.py:303
  69.0 10.6 %collective-permute-start.8 = (bf16[2,16,5120]{2,1,0:T(8,128)(2,1)S(1)}, bf16[2,16,5120]{2,1,0:T(8,128)(2,1)S(1)}, u32[]{:S(2)}, u32[]{:S(2)}) collective-permute-start(bf16[2,16,5120]{2,1,0:T(8,128)(2,1)S(1)} %collective-permute-done.6.refs_4_), channel_id=1, source_target_pairs={{0,8},{8,0},{16,24},{24,16},{1,9},{9,1},{17,25},{25,17},{2,10},{10... | collective-permute-start | bytes 983048 | tf_op jit(solution)/shard_map/ppermute | solution.py:303
  70.5 16.1 %collective-permute-start.11 = (bf16[2,16,5120]{2,1,0:T(8,128)(2,1)S(1)}, bf16[2,16,5120]{2,1,0:T(8,128)(2,1)S(1)}, u32[]{:S(2)}, u32[]{:S(2)}) collective-permute-start(bf16[2,16,5120]{2,1,0:T(8,128)(2,1)S(1)} %collective-permute-done.10.refs_8_), channel_id=1, source_target_pairs={{0,8},{8,0},{16,24},{24,16},{1,9},{9,1},{17,25},{25,17},{2,10},{10... | collective-permute-start | bytes 983048 | tf_op jit(solution)/shard_map/ppermute | solution.py:303
  71.0 16.1 %collective-permute-start.12 = (bf16[2,16,5120]{2,1,0:T(8,128)(2,1)S(1)}, bf16[2,16,5120]{2,1,0:T(8,128)(2,1)S(1)}, u32[]{:S(2)}, u32[]{:S(2)}) collective-permute-start(bf16[2,16,5120]{2,1,0:T(8,128)(2,1)S(1)} %collective-permute-done.10.refs_8_), channel_id=1, source_target_pairs={{0,16},{8,24},{16,0},{24,8},{1,17},{9,25},{17,1},{25,9},{2,18},{10... | collective-permute-start | bytes 983048 | tf_op jit(solution)/shard_map/ppermute | solution.py:303
  71.5 17.1 %collective-permute-start.15 = (bf16[2,16,5120]{2,1,0:T(8,128)(2,1)S(1)}, bf16[2,16,5120]{2,1,0:T(8,128)(2,1)S(1)}, u32[]{:S(2)}, u32[]{:S(2)}) collective-permute-start(bf16[2,16,5120]{2,1,0:T(8,128)(2,1)S(1)} %collective-permute-done.14.refs_12_), channel_id=1, source_target_pairs={{0,16},{8,24},{16,0},{24,8},{1,17},{9,25},{17,1},{25,9},{2,18},{10... | collective-permute-start | bytes 983048 | tf_op jit(solution)/shard_map/ppermute | solution.py:303
  73.1 20.6 %collective-permute-start.16 = (bf16[2,16,5120]{2,1,0:T(8,128)(2,1)S(1)}, bf16[2,16,5120]{2,1,0:T(8,128)(2,1)S(1)}, u32[]{:S(2)}, u32[]{:S(2)}) collective-permute-start(bf16[2,16,5120]{2,1,0:T(8,128)(2,1)S(1)} %collective-permute-done.14.refs_12_), channel_id=1, source_target_pairs={{0,8},{8,0},{16,24},{24,16},{1,9},{9,1},{17,25},{25,17},{2,10},{10... | collective-permute-start | bytes 983048 | tf_op jit(solution)/shard_map/ppermute | solution.py:303
  79.6 21.1 %collective-permute-start.19 = (bf16[2,16,5120]{2,1,0:T(8,128)(2,1)S(1)}, bf16[2,16,5120]{2,1,0:T(8,128)(2,1)S(1)}, u32[]{:S(2)}, u32[]{:S(2)}) collective-permute-start(bf16[2,16,5120]{2,1,0:T(8,128)(2,1)S(1)} %collective-permute-done.18.refs_16_), channel_id=1, source_target_pairs={{0,8},{8,0},{16,24},{24,16},{1,9},{9,1},{17,25},{25,17},{2,10},{10... | collective-permute-start | bytes 983048 | tf_op jit(solution)/shard_map/ppermute | solution.py:303
  86.6 14.6 %collective-permute-start.20 = (bf16[2,16,5120]{2,1,0:T(8,128)(2,1)S(1)}, bf16[2,16,5120]{2,1,0:T(8,128)(2,1)S(1)}, u32[]{:S(2)}, u32[]{:S(2)}) collective-permute-start(bf16[2,16,5120]{2,1,0:T(8,128)(2,1)S(1)} %collective-permute-done.18.refs_16_), channel_id=1, source_target_pairs={{0,16},{8,24},{16,0},{24,8},{1,17},{9,25},{17,1},{25,9},{2,18},{10... | collective-permute-start | bytes 983048 | tf_op jit(solution)/shard_map/ppermute | solution.py:303
  87.1 15.5 %collective-permute-start.23 = (bf16[2,16,5120]{2,1,0:T(8,128)(2,1)S(1)}, bf16[2,16,5120]{2,1,0:T(8,128)(2,1)S(1)}, u32[]{:S(2)}, u32[]{:S(2)}) collective-permute-start(bf16[2,16,5120]{2,1,0:T(8,128)(2,1)S(1)} %collective-permute-done.22.refs_20_), channel_id=1, source_target_pairs={{0,16},{8,24},{16,0},{24,8},{1,17},{9,25},{17,1},{25,9},{2,18},{10... | collective-permute-start | bytes 983048 | tf_op jit(solution)/shard_map/ppermute | solution.py:303
  88.6 19.0 %collective-permute-start.24 = (bf16[2,16,5120]{2,1,0:T(8,128)(2,1)S(1)}, bf16[2,16,5120]{2,1,0:T(8,128)(2,1)S(1)}, u32[]{:S(2)}, u32[]{:S(2)}) collective-permute-start(bf16[2,16,5120]{2,1,0:T(8,128)(2,1)S(1)} %collective-permute-done.22.refs_20_), channel_id=1, source_target_pairs={{0,8},{8,0},{16,24},{24,16},{1,9},{9,1},{17,25},{25,17},{2,10},{10... | collective-permute-start | bytes 983048 | tf_op jit(solution)/shard_map/ppermute | solution.py:303
  93.6 21.1 %collective-permute-start.27 = (bf16[2,16,5120]{2,1,0:T(8,128)(2,1)S(1)}, bf16[2,16,5120]{2,1,0:T(8,128)(2,1)S(1)}, u32[]{:S(2)}, u32[]{:S(2)}) collective-permute-start(bf16[2,16,5120]{2,1,0:T(8,128)(2,1)S(1)} %collective-permute-done.26.refs_0_), channel_id=1, source_target_pairs={{0,8},{8,0},{16,24},{24,16},{1,9},{9,1},{17,25},{25,17},{2,10},{10... | collective-permute-start | bytes 983048 | tf_op jit(solution)/shard_map/ppermute | solution.py:303
  100.6 14.6 %collective-permute-start.31 = (bf16[2,16,5120]{2,1,0:T(8,128)(2,1)S(1)}, bf16[2,16,5120]{2,1,0:T(8,128)(2,1)S(1)}, u32[]{:S(2)}, u32[]{:S(2)}) collective-permute-start(bf16[2,16,5120]{2,1,0:T(8,128)(2,1)S(1)} %collective-permute-done.30.refs_4_), channel_id=1, source_target_pairs={{0,16},{8,24},{16,0},{24,8},{1,17},{9,25},{17,1},{25,9},{2,18},{10... | collective-permute-start | bytes 983048 | tf_op jit(solution)/shard_map/ppermute | solution.py:303
  101.1 20.6 %collective-permute-start.9 = (bf16[2,16,5120]{2,1,0:T(8,128)(2,1)S(1)}, bf16[2,16,5120]{2,1,0:T(8,128)(2,1)S(1)}, u32[]{:S(2)}, u32[]{:S(2)}) collective-permute-start(bf16[2,16,5120]{2,1,0:T(8,128)(2,1)S(1)} %collective-permute-done.7.refs_5_), channel_id=1, source_target_pairs={{0,8},{8,0},{16,24},{24,16},{1,9},{9,1},{17,25},{25,17},{2,10},{10... | collective-permute-start | bytes 983048 | tf_op jit(solution)/shard_map/ppermute | solution.py:303
  102.6 20.6 %collective-permute-start.13 = (bf16[2,16,5120]{2,1,0:T(8,128)(2,1)S(1)}, bf16[2,16,5120]{2,1,0:T(8,128)(2,1)S(1)}, u32[]{:S(2)}, u32[]{:S(2)}) collective-permute-start(bf16[2,16,5120]{2,1,0:T(8,128)(2,1)S(1)} %collective-permute-done.11.refs_9_), channel_id=1, source_target_pairs={{0,16},{8,24},{16,0},{24,8},{1,17},{9,25},{17,1},{25,9},{2,18},{10... | collective-permute-start | bytes 983048 | tf_op jit(solution)/shard_map/ppermute | solution.py:303
  107.7 21.1 %collective-permute-start.17 = (bf16[2,16,5120]{2,1,0:T(8,128)(2,1)S(1)}, bf16[2,16,5120]{2,1,0:T(8,128)(2,1)S(1)}, u32[]{:S(2)}, u32[]{:S(2)}) collective-permute-start(bf16[2,16,5120]{2,1,0:T(8,128)(2,1)S(1)} %collective-permute-done.15.refs_13_), channel_id=1, source_target_pairs={{0,8},{8,0},{16,24},{24,16},{1,9},{9,1},{17,25},{25,17},{2,10},{10... | collective-permute-start | bytes 983048 | tf_op jit(solution)/shard_map/ppermute | solution.py:303
  114.7 14.6 %collective-permute-start.21 = (bf16[2,16,5120]{2,1,0:T(8,128)(2,1)S(1)}, bf16[2,16,5120]{2,1,0:T(8,128)(2,1)S(1)}, u32[]{:S(2)}, u32[]{:S(2)}) collective-permute-start(bf16[2,16,5120]{2,1,0:T(8,128)(2,1)S(1)} %collective-permute-done.19.refs_17_), channel_id=1, source_target_pairs={{0,16},{8,24},{16,0},{24,8},{1,17},{9,25},{17,1},{25,9},{2,18},{10... | collective-permute-start | bytes 983048 | tf_op jit(solution)/shard_map/ppermute | solution.py:303
  115.2 26.4 %collective-permute-start.28 = (bf16[2,16,5120]{2,1,0:T(8,128)(2,1)S(1)}, bf16[2,16,5120]{2,1,0:T(8,128)(2,1)S(1)}, u32[]{:S(2)}, u32[]{:S(2)}) collective-permute-start(bf16[2,16,5120]{2,1,0:T(8,128)(2,1)S(1)} %collective-permute-done.26.refs_0_), channel_id=1, source_target_pairs={{0,16},{8,24},{16,0},{24,8},{1,17},{9,25},{17,1},{25,9},{2,18},{10... | collective-permute-start | bytes 983048 | tf_op jit(solution)/shard_map/ppermute | solution.py:303
  121.7 14.0 %collective-permute-start.25 = (bf16[2,16,5120]{2,1,0:T(8,128)(2,1)S(1)}, bf16[2,16,5120]{2,1,0:T(8,128)(2,1)S(1)}, u32[]{:S(2)}, u32[]{:S(2)}) collective-permute-start(bf16[2,16,5120]{2,1,0:T(8,128)(2,1)S(1)} %collective-permute-done.23.refs_21_), channel_id=1, source_target_pairs={{0,8},{8,0},{16,24},{24,16},{1,9},{9,1},{17,25},{25,17},{2,10},{10... | collective-permute-start | bytes 983048 | tf_op jit(solution)/shard_map/ppermute | solution.py:303
  123.2 19.6 %collective-permute-start.32 = (bf16[2,16,5120]{2,1,0:T(8,128)(2,1)S(1)}, bf16[2,16,5120]{2,1,0:T(8,128)(2,1)S(1)}, u32[]{:S(2)}, u32[]{:S(2)}) collective-permute-start(bf16[2,16,5120]{2,1,0:T(8,128)(2,1)S(1)} %collective-permute-done.30.refs_4_), channel_id=1, source_target_pairs={{0,8},{8,0},{16,24},{24,16},{1,9},{9,1},{17,25},{25,17},{2,10},{10... | collective-permute-start | bytes 983048 | tf_op jit(solution)/shard_map/ppermute | solution.py:303
  128.7 14.0 %collective-permute-start.29 = (bf16[2,16,5120]{2,1,0:T(8,128)(2,1)S(1)}, bf16[2,16,5120]{2,1,0:T(8,128)(2,1)S(1)}, u32[]{:S(2)}, u32[]{:S(2)}) collective-permute-start(bf16[2,16,5120]{2,1,0:T(8,128)(2,1)S(1)} %collective-permute-done.27.refs_1_), channel_id=1, source_target_pairs={{0,16},{8,24},{16,0},{24,8},{1,17},{9,25},{17,1},{25,9},{2,18},{10... | collective-permute-start | bytes 983048 | tf_op jit(solution)/shard_map/ppermute | solution.py:303
  129.2 18.3 %collective-permute-start.33 = (bf16[2,16,5120]{2,1,0:T(8,128)(2,1)S(1)}, bf16[2,16,5120]{2,1,0:T(8,128)(2,1)S(1)}, u32[]{:S(2)}, u32[]{:S(2)}) collective-permute-start(bf16[2,16,5120]{2,1,0:T(8,128)(2,1)S(1)} %collective-permute-done.31.refs_5_), channel_id=1, source_target_pairs={{0,8},{8,0},{16,24},{24,16},{1,9},{9,1},{17,25},{25,17},{2,10},{10... | collective-permute-start | bytes 983048 | tf_op jit(solution)/shard_map/ppermute | solution.py:303

commit v5 on v4

--- a/solution.py
+++ b/solution.py
@@ -241,14 +241,16 @@
         )
 
 
-def late_body(places, tile, pitch, weights, partial, *refs):
+def late_body(places, shifts, tile, first, pitch, weights, partial, *refs):
     pieces = refs[: len(places)]
-    out, data, wide = refs[len(places) :]
-    here = columns(tile)
-    gather_rows(places, pieces, here, data)
+    out, data, wide = refs[-3:]
+    views = [
+        piece.at[:, :, pl.ds(shift * tile, tile)] for piece, shift in zip(pieces, shifts)
+    ]
+    gather_rows(places, views, slice(None), data)
     beams = weights.shape[1]
     for q in range(2):
-        part = partial[q, :, here] + jnp.dot(
+        part = partial[q, :, first * tile : (first + 1) * tile] + jnp.dot(
             weights[q], data[...], preferred_element_type=jnp.float32
         )
         for j in range(tile // LANES):
@@ -277,17 +279,23 @@
     )(weights, *[piece for _, _, piece in pieces])
 
 
-def beam_late(weights, partial, pieces, tile):
+def beam_late(weights, partial, pieces, first, tile, before):
     _, beams, depth = weights.shape
-    total = pieces[0][2].shape[2]
+    total = partial.shape[2]
     high = 2 * tile // LANES
     pitch = high + 1
-    return pl.pallas_call(
-        functools.partial(late_body, [(g, j) for g, j, _ in pieces], tile, pitch),
-        grid=(total // tile,),
-        in_specs=[VMEM_WHOLE] * (2 + len(pieces)),
-        out_specs=pl.BlockSpec((beams, high, LANES), lambda n: (0, n, 0)),
+    extra = [] if before is None else [before]
+    shifts = [first if piece.shape[2] == total else 0 for _, _, piece in pieces]
+    return pl.pallas_call(
+        functools.partial(
+            late_body, [(g, j) for g, j, _ in pieces], shifts, tile, first, pitch
+        ),
+        grid=(1,),
+        in_specs=[VMEM_WHOLE] * (2 + len(pieces))
+        + [pl.BlockSpec(memory_space=pl.ANY)] * len(extra),
+        out_specs=pl.BlockSpec((beams, high, LANES), lambda n: (0, first, 0)),
         out_shape=jax.ShapeDtypeStruct((beams, 2 * total // LANES, LANES), jnp.bfloat16),
+        input_output_aliases={2 + len(pieces): 0} if extra else {},
         scratch_shapes=[
             pltpu.VMEM((depth, tile), jnp.bfloat16),
             pltpu.VMEM((beams * pitch, LANES), jnp.float32),
@@ -296,7 +304,7 @@
             dimension_semantics=("arbitrary",), vmem_limit_bytes=KERNEL_VMEM
         ),
         name="late",
-    )(weights, partial, *[piece for _, _, piece in pieces])
+    )(weights, partial, *[piece for _, _, piece in pieces], *extra)
 
 
 def swap(array, axis, step, size):
@@ -305,7 +313,7 @@
 
 def fast(stn, freq, voltages, filter_taps, beam_weights, station_map, active_counts):
     slots, polars, chans, _, samples = voltages.shape
-    _, fine = filter_taps.shape
+    taps, fine = filter_taps.shape
     s_me = lax.axis_index("stn")
     f_me = lax.axis_index("freq")
 
@@ -326,6 +334,7 @@
     )
     table = cos_sin(fine)
     planes = freq // 2
+    total = polars * (samples - (taps - 1) * fine)
     held = {}
     for jz in range(planes):
         made = spectra_pair(info, jz, view, filter_taps, table)
@@ -334,17 +343,27 @@
             held[j, p] = piece if j == 0 else swap(piece, "freq", j, freq)
 
     bits = [1 << i for i in range(stn.bit_length() - 1)]
-    have = {}
+    early, late = [], [[], []]
+    tile = total // 2
     for (j, p), piece in held.items():
-        have[j, p] = {0: piece}
-        for bit in bits if j % 2 == 0 else bits[::-1]:
-            have[j, p].update({g ^ bit: swap(a, "stn", bit, stn) for g, a in have[j, p].items()})
-
-    every = [
-        (g, j, piece) for (j, _), group in have.items() for g, piece in group.items()
-    ]
-    partial = beam_early(w_early, [e for e in every if e[1] < freq - 2], 4 * LANES)
-    out = beam_late(w_late, partial, [e for e in every if e[1] >= freq - 2], 20 * LANES)
+        have = {0: piece}
+        halves = {}
+        for i, bit in enumerate(bits if j % 2 == 0 else bits[::-1]):
+            for n, (g, a) in enumerate(list(have.items())):
+                if j >= freq - 2 and i == len(bits) - 1 and n > 0:
+                    parts = [a[:, :, h * tile : (h + 1) * tile] for h in range(2)]
+                    halves[g ^ bit] = [swap(part, "stn", bit, stn) for part in parts]
+                else:
+                    have[g ^ bit] = swap(a, "stn", bit, stn)
+        for h in range(2):
+            late[h] += [(g, j, a) for g, a in have.items() if j >= freq - 2]
+            late[h] += [(g, j, a[h]) for g, a in halves.items()]
+        early += [(g, j, a) for g, a in have.items() if j < freq - 2]
+
+    partial = beam_early(w_early, early, 4 * LANES)
+    out = None
+    for h in range(2):
+        out = beam_late(w_late, partial, late[h], h, tile, out)
     high = out.shape[1] // 2
     return out.reshape(out.shape[0], high, 2, LANES).transpose(0, 2, 1, 3).reshape(
         out.shape[0], 2, 1, high * LANES

time: 153 us -> 165 us (1.078); the launches traced: 151 us -> 165 us
  starting transfers between devices: 42.9 us -> 59.4 us
  waiting for transfers between devices: 84.8 us -> 74.6 us
  local copies, waits for them, and re-layouts: 0.02 us -> 5.97 us
    ppermute x34 -> x36, starting transfers between devices: 42.9 us -> 59.4 us  [swap(): return lax.ppermute(array, axis, [(i, i ^ step) for i in range(size)])]
    ppermute x34 -> x36, waiting for transfers between devices: 84.8 us -> 74.6 us  [swap(): return lax.ppermute(array, axis, [(i, i ^ step) for i in range(size)])]
    unnamed x10, local copies, waits for them, and re-layouts: 0.02 us -> 5.92 us
    pallas_call x1 -> x2, Pallas kernels: 3.7 us -> 5.15 us  [beam_late(): pl.pallas_call(functools.partial(late_body, [(g, j) for g, j, _ in pieces...]
  transfers between devices with their start and end apart: 34 -> 36, of which waited for: 15 -> 14; matrix products, arithmetic and copies ran while one was open for 0% -> 0% of each run, Pallas kernels for 10% -> 13%
where the time goes in v5:
time: 165 us
  waiting for transfers between devices  74.6 us (45%)
  starting transfers between devices  59.4 us (36%)
  Pallas kernels  24.1 us (15%)
  local copies, waits for them, and re-layouts  5.97 us (4%)
    ppermute x36, waiting for transfers between devices, swap(): return lax.ppermute(array, axis, [(i, i ^ step) for i in range(size)])  74.6 us
    ppermute x36, starting transfers between devices, swap(): return lax.ppermute(array, axis, [(i, i ^ step) for i in range(size)])  59.4 us
    pallas_call x4, Pallas kernels, spectra_pair(): pl.pallas_call(functools.partial(spectra_body, (taps, frames_out, per_pai...  11.3 us
    unnamed x10, local copies, waits for them, and re-layouts  5.92 us
    pallas_call x1, Pallas kernels, beam_early(): pl.pallas_call(functools.partial(early_body, [(g, j) for g, j, _ in piece...  5.85 us
    pallas_call x2, Pallas kernels, beam_late(): pl.pallas_call(functools.partial(late_body, [(g, j) for g, j, _ in pieces...  5.15 us
  transfers between devices with their start and end apart: 36, of which 14 were waited for; matrix products, arithmetic and copies ran while one was open for 0% of the time, Pallas kernels for 13%

profile of v5, /device:TPU:0, one launch (start us, length us, event | category | flops | bytes accessed | tf_op | source)
XLA Modules:
  0.0 165.0 jit_solution(16466765269051269932)
XLA Ops:
  0.7 1.0 copy-done.2
  3.2 3.0 %collective-permute-start = (bf16[2,8,16,256]{3,2,1,0:T(8,128)(2,1)S(1)}, bf16[2,8,16,256]{3,2,1,0:T(8,128)(2,1)S(1)}, u32[]{:S(2)}, u32[]{:S(2)}) collective-permute-start(bf16[2,8,16,256]{3,2,1,0:T(8,128)(2,1)S(1)} %get-tuple-element.20), channel_id=1, source_target_pairs={{0,8},{8,0},{16,24},{24,16},{1,9},{9,1},{17,25},{25,17},{2,10},{10... | collective-permute-start | bytes 393224 | tf_op jit(solution)/shard_map/ppermute | solution.py:311
  6.3 2.6 %copy-done = bf16[16,2,8,2,5376]{4,3,2,1,0:T(2,128)(2,1)S(1)} copy-done((bf16[16,2,8,2,5376]{4,3,2,1,0:T(2,128)(2,1)S(1)}, bf16[16,2,8,2,5376]{4,3,2,1,0:T(2,128)(2,1)}, u32[]{:S(2)}) %copy-start) | copy-done | bytes 5505048
  10.5 2.5 %spectra.7 = (bf16[2,16,5120]{2,1,0:T(8,128)(2,1)S(1)}, bf16[2,16,5120]{2,1,0:T(8,128)(2,1)S(1)}) custom-call(s32[2]{0:T(128)S(1)} %pad_add_fusion.info, bf16[16,2,4,168,128]{4,3,2,1,0:T(8,128)(2,1)S(1)} %bitcast.19, f32[12,256]{1,0:T(8,128)S(1)} %copy-done.3, bf16[256,512]{1,0:T(8,128)(2,1)S(1)} %copy-done.1), custom_call_target="tpu_custom_call" | custom-call | tf_op jit(solution)/shard_map/spectra/pallas_call | solution.py:137
  13.0 3.7 %collective-permute-start.26 = (bf16[2,16,5120]{2,1,0:T(8,128)(2,1)S(1)}, bf16[2,16,5120]{2,1,0:T(8,128)(2,1)S(1)}, u32[]{:S(2)}, u32[]{:S(2)}) collective-permute-start(bf16[2,16,5120]{2,1,0:T(8,128)(2,1)S(1)} %get-tuple-element.31), channel_id=1, source_target_pairs={{0,6},{1,7},{2,4},{3,5},{4,2},{5,3},{6,0},{7,1},{8,14},{9,15},{10,... | collective-permute-start | bytes 983048 | tf_op jit(solution)/shard_map/ppermute | solution.py:311
  16.7 2.5 %spectra.6 = (bf16[2,16,5120]{2,1,0:T(8,128)(2,1)S(1)}, bf16[2,16,5120]{2,1,0:T(8,128)(2,1)S(1)}) custom-call(s32[2]{0:T(128)S(1)} %pad_add_fusion.info, bf16[16,2,4,168,128]{4,3,2,1,0:T(8,128)(2,1)S(1)} %bitcast.20, f32[12,256]{1,0:T(8,128)S(1)} %copy-done.3, bf16[256,512]{1,0:T(8,128)(2,1)S(1)} %copy-done.1), custom_call_target="tpu_custom_call" | custom-call | tf_op jit(solution)/shard_map/spectra/pallas_call | solution.py:137
  19.3 2.6 %collective-permute-start.22 = (bf16[2,16,5120]{2,1,0:T(8,128)(2,1)S(1)}, bf16[2,16,5120]{2,1,0:T(8,128)(2,1)S(1)}, u32[]{:S(2)}, u32[]{:S(2)}) collective-permute-start(bf16[2,16,5120]{2,1,0:T(8,128)(2,1)S(1)} %get-tuple-element.30), channel_id=1, source_target_pairs={{0,5},{1,4},{2,7},{3,6},{4,1},{5,0},{6,3},{7,2},{8,13},{9,12},{10,... | collective-permute-start | bytes 983048 | tf_op jit(solution)/shard_map/ppermute | solution.py:311
  21.9 1.5 collective-permute-start.1
  23.4 4.4 %collective-permute-done.1 = bf16[2,8,16,256]{3,2,1,0:T(8,128)(2,1)S(1)} collective-permute-done((bf16[2,8,16,256]{3,2,1,0:T(8,128)(2,1)S(1)}, bf16[2,8,16,256]{3,2,1,0:T(8,128)(2,1)S(1)}, u32[]{:S(2)}, u32[]{:S(2)}) %collective-permute-start.1) | collective-permute-done | bytes 131104 | tf_op jit(solution)/shard_map/ppermute | solution.py:311
  27.8 1.5 collective-permute-start.2
  29.3 2.5 %spectra.5 = (bf16[2,16,5120]{2,1,0:T(8,128)(2,1)S(1)}, bf16[2,16,5120]{2,1,0:T(8,128)(2,1)S(1)}) custom-call(s32[2]{0:T(128)S(1)} %pad_add_fusion.info, bf16[16,2,4,168,128]{4,3,2,1,0:T(8,128)(2,1)S(1)} %bitcast.21, f32[12,256]{1,0:T(8,128)S(1)} %copy-done.3, bf16[256,512]{1,0:T(8,128)(2,1)S(1)} %copy-done.1), custom_call_target="tpu_custom_call" | custom-call | tf_op jit(solution)/shard_map/spectra/pallas_call | solution.py:137
  31.8 3.6 %spectra.4 = (bf16[2,16,5120]{2,1,0:T(8,128)(2,1)S(1)}, bf16[2,16,5120]{2,1,0:T(8,128)(2,1)S(1)}) custom-call(s32[2]{0:T(128)S(1)} %pad_add_fusion.info, bf16[16,2,4,168,128]{4,3,2,1,0:T(8,128)(2,1)} %bitcast.18, f32[12,256]{1,0:T(8,128)} %taps_ref.7, bf16[256,512]{1,0:T(8,128)(2,1)} %constant.14.table), custom_call_target="tpu_custom_call" | custom-call | tf_op jit(solution)/shard_map/spectra/pallas_call | solution.py:137
  35.5 1.2 collective-permute-start.10
  36.7 14.0 %collective-permute-start.14 = (bf16[2,16,5120]{2,1,0:T(8,128)(2,1)S(1)}, bf16[2,16,5120]{2,1,0:T(8,128)(2,1)S(1)}, u32[]{:S(2)}, u32[]{:S(2)}) collective-permute-start(bf16[2,16,5120]{2,1,0:T(8,128)(2,1)S(1)} %get-tuple-element.28), channel_id=1, source_target_pairs={{0,3},{1,2},{2,1},{3,0},{4,7},{5,6},{6,5},{7,4},{8,11},{9,10},{10,... | collective-permute-start | bytes 983048 | tf_op jit(solution)/shard_map/ppermute | solution.py:311
  50.7 2.3 %collective-permute-start.6 = (bf16[2,16,5120]{2,1,0:T(8,128)(2,1)S(1)}, bf16[2,16,5120]{2,1,0:T(8,128)(2,1)S(1)}, u32[]{:S(2)}, u32[]{:S(2)}) collective-permute-start(bf16[2,16,5120]{2,1,0:T(8,128)(2,1)S(1)} %get-tuple-element.26), channel_id=1, source_target_pairs={{0,1},{1,0},{2,3},{3,2},{4,5},{5,4},{6,7},{7,6},{8,9},{9,8},{10,11... | collective-permute-start | bytes 983048 | tf_op jit(solution)/shard_map/ppermute | solution.py:311
  53.0 13.5 %collective-permute-done.18.refs_16_ = bf16[2,16,5120]{2,1,0:T(8,128)(2,1)S(1)} collective-permute-done((bf16[2,16,5120]{2,1,0:T(8,128)(2,1)S(1)}, bf16[2,16,5120]{2,1,0:T(8,128)(2,1)S(1)}, u32[]{:S(2)}, u32[]{:S(2)}) %collective-permute-start.18) | collective-permute-done | bytes 327712 | tf_op jit(solution)/shard_map/ppermute | solution.py:311
  66.5 1.5 collective-permute-start.4
  68.0 3.6 %collective-permute-done.22.refs_20_ = bf16[2,16,5120]{2,1,0:T(8,128)(2,1)S(1)} collective-permute-done((bf16[2,16,5120]{2,1,0:T(8,128)(2,1)S(1)}, bf16[2,16,5120]{2,1,0:T(8,128)(2,1)S(1)}, u32[]{:S(2)}, u32[]{:S(2)}) %collective-permute-start.22) | collective-permute-done | bytes 327712 | tf_op jit(solution)/shard_map/ppermute | solution.py:311
  72.1 1.5 collective-permute-start.28
  73.6 1.5 collective-permute-start.27
  75.7 1.5 collective-permute-start.20
  77.2 5.0 %collective-permute-done.3.refs_1_ = bf16[2,16,5120]{2,1,0:T(8,128)(2,1)S(1)} collective-permute-done((bf16[2,16,5120]{2,1,0:T(8,128)(2,1)S(1)}, bf16[2,16,5120]{2,1,0:T(8,128)(2,1)S(1)}, u32[]{:S(2)}, u32[]{:S(2)}) %collective-permute-start.3) | collective-permute-done | bytes 327712 | tf_op jit(solution)/shard_map/ppermute | solution.py:311
  82.7 1.5 collective-permute-start.24
  84.2 5.0 %collective-permute-done.27.refs_1_ = bf16[2,16,5120]{2,1,0:T(8,128)(2,1)S(1)} collective-permute-done((bf16[2,16,5120]{2,1,0:T(8,128)(2,1)S(1)}, bf16[2,16,5120]{2,1,0:T(8,128)(2,1)S(1)}, u32[]{:S(2)}, u32[]{:S(2)}) %collective-permute-start.27) | collective-permute-done | bytes 327712 | tf_op jit(solution)/shard_map/ppermute | solution.py:311
  89.2 1.5 collective-permute-start.23
  91.2 5.5 %collective-permute-done.20.refs_18_ = bf16[2,16,5120]{2,1,0:T(8,128)(2,1)S(1)} collective-permute-done((bf16[2,16,5120]{2,1,0:T(8,128)(2,1)S(1)}, bf16[2,16,5120]{2,1,0:T(8,128)(2,1)S(1)}, u32[]{:S(2)}, u32[]{:S(2)}) %collective-permute-start.20) | collective-permute-done | bytes 327712 | tf_op jit(solution)/shard_map/ppermute | solution.py:311
  96.8 1.5 collective-permute-start.11
  98.8 4.5 %collective-permute-done.24.refs_22_ = bf16[2,16,5120]{2,1,0:T(8,128)(2,1)S(1)} collective-permute-done((bf16[2,16,5120]{2,1,0:T(8,128)(2,1)S(1)}, bf16[2,16,5120]{2,1,0:T(8,128)(2,1)S(1)}, u32[]{:S(2)}, u32[]{:S(2)}) %collective-permute-start.24) | collective-permute-done | bytes 327712 | tf_op jit(solution)/shard_map/ppermute | solution.py:311
  103.2 1.5 collective-permute-start.15
  105.3 5.5 %collective-permute-done.12.refs_10_ = bf16[2,16,5120]{2,1,0:T(8,128)(2,1)S(1)} collective-permute-done((bf16[2,16,5120]{2,1,0:T(8,128)(2,1)S(1)}, bf16[2,16,5120]{2,1,0:T(8,128)(2,1)S(1)}, u32[]{:S(2)}, u32[]{:S(2)}) %collective-permute-start.12) | collective-permute-done | bytes 327712 | tf_op jit(solution)/shard_map/ppermute | solution.py:311
  110.8 1.5 collective-permute-start.7
  112.8 4.5 %collective-permute-done.16.refs_14_ = bf16[2,16,5120]{2,1,0:T(8,128)(2,1)S(1)} collective-permute-done((bf16[2,16,5120]{2,1,0:T(8,128)(2,1)S(1)}, bf16[2,16,5120]{2,1,0:T(8,128)(2,1)S(1)}, u32[]{:S(2)}, u32[]{:S(2)}) %collective-permute-start.16) | collective-permute-done | bytes 327712 | tf_op jit(solution)/shard_map/ppermute | solution.py:311
  117.3 1.5 collective-permute-start.21
  119.4 4.9 %collective-permute-done.8.refs_6_ = bf16[2,16,5120]{2,1,0:T(8,128)(2,1)S(1)} collective-permute-done((bf16[2,16,5120]{2,1,0:T(8,128)(2,1)S(1)}, bf16[2,16,5120]{2,1,0:T(8,128)(2,1)S(1)}, u32[]{:S(2)}, u32[]{:S(2)}) %collective-permute-start.8) | collective-permute-done | bytes 327712 | tf_op jit(solution)/shard_map/ppermute | solution.py:311
  124.8 1.5 collective-permute-start.13
  126.4 5.5 %collective-permute-done.5.refs_3_ = bf16[2,16,5120]{2,1,0:T(8,128)(2,1)S(1)} collective-permute-done((bf16[2,16,5120]{2,1,0:T(8,128)(2,1)S(1)}, bf16[2,16,5120]{2,1,0:T(8,128)(2,1)S(1)}, u32[]{:S(2)}, u32[]{:S(2)}) %collective-permute-start.5) | collective-permute-done | bytes 327712 | tf_op jit(solution)/shard_map/ppermute | solution.py:311
  131.9 1.5 collective-permute-start.17
  133.4 5.5 %collective-permute-done.21.refs_19_ = bf16[2,16,5120]{2,1,0:T(8,128)(2,1)S(1)} collective-permute-done((bf16[2,16,5120]{2,1,0:T(8,128)(2,1)S(1)}, bf16[2,16,5120]{2,1,0:T(8,128)(2,1)S(1)}, u32[]{:S(2)}, u32[]{:S(2)}) %collective-permute-start.21) | collective-permute-done | bytes 327712 | tf_op jit(solution)/shard_map/ppermute | solution.py:311
  138.9 1.5 collective-permute-start.9
  140.4 1.6 collective-permute-start.34
  142.0 3.9 %collective-permute-done.13.refs_11_ = bf16[2,16,5120]{2,1,0:T(8,128)(2,1)S(1)} collective-permute-done((bf16[2,16,5120]{2,1,0:T(8,128)(2,1)S(1)}, bf16[2,16,5120]{2,1,0:T(8,128)(2,1)S(1)}, u32[]{:S(2)}, u32[]{:S(2)}) %collective-permute-start.13) | collective-permute-done | bytes 327712 | tf_op jit(solution)/shard_map/ppermute | solution.py:311
  145.9 1.5 collective-permute-start.35
  147.4 1.5 collective-permute-start.29
  148.9 3.5 %collective-permute-done.9.refs_7_ = bf16[2,16,5120]{2,1,0:T(8,128)(2,1)S(1)} collective-permute-done((bf16[2,16,5120]{2,1,0:T(8,128)(2,1)S(1)}, bf16[2,16,5120]{2,1,0:T(8,128)(2,1)S(1)}, u32[]{:S(2)}, u32[]{:S(2)}) %collective-permute-start.9) | collective-permute-done | bytes 327712 | tf_op jit(solution)/shard_map/ppermute | solution.py:311
  152.9 1.0 turn.1
  154.0 5.8 %early.1.partial = f32[2,256,5120]{2,1,0:T(8,128)S(1)} custom-call(bf16[2,256,768]{2,1,0:T(8,128)(2,1)S(1)} %get-tuple-element.24.weights, bf16[2,16,5120]{2,1,0:T(8,128)(2,1)S(1)} %get-tuple-element.25.refs_0_, bf16[2,16,5120]{2,1,0:T(8,128)(2,1)S(1)} %collective-permute-done.3.refs_1_, bf16[2,16,5120]{2,1,0:T(8,128)(2,1)S(1)} %collective-permute-done.4.refs_2_, ...), custom_call_target="tpu_custom_call" | custom-call | tf_op jit(solution)/shard_map/early/pallas_call | solution.py:268
  159.8 2.6 %late.2.refs_8_ = bf16[256,80,128]{2,1,0:T(8,128)(2,1)} custom-call(bf16[2,256,256]{2,1,0:T(8,128)(2,1)S(1)} %get-tuple-element.23.weights, f32[2,256,5120]{2,1,0:T(8,128)S(1)} %early.1.partial, bf16[2,16,5120]{2,1,0:T(8,128)(2,1)S(1)} %collective-permute-done.26.refs_0_, bf16[2,16,5120]{2,1,0:T(8,128)(2,1)S(1)} %collective-permute-done.27.refs_1_, ...), custom_call_target="tpu_custom_call" | custom-call | tf_op jit(solution)/shard_map/late/pallas_call | solution.py:289
  162.4 2.6 %late.3 = bf16[256,80,128]{2,1,0:T(8,128)(2,1)} custom-call(bf16[2,256,256]{2,1,0:T(8,128)(2,1)S(1)} %get-tuple-element.23.weights, f32[2,256,5120]{2,1,0:T(8,128)S(1)} %early.1.partial, bf16[2,16,5120]{2,1,0:T(8,128)(2,1)S(1)} %collective-permute-done.26.refs_0_, ...), custom_call_target="tpu_custom_call", output_to_operand_aliasing={{}: (10, {})} | custom-call | tf_op jit(solution)/shard_map/late/pallas_call | solution.py:289
  (46 shorter events, 8.7 us)
Async XLA Ops:
  0.7 1.0 copy-start.2
  1.8 0.7 copy-start.4
  3.2 18.7 %collective-permute-start = (bf16[2,8,16,256]{3,2,1,0:T(8,128)(2,1)S(1)}, bf16[2,8,16,256]{3,2,1,0:T(8,128)(2,1)S(1)}, u32[]{:S(2)}, u32[]{:S(2)}) collective-permute-start(bf16[2,8,16,256]{3,2,1,0:T(8,128)(2,1)S(1)} %get-tuple-element.20), channel_id=1, source_target_pairs={{0,8},{8,0},{16,24},{24,16},{1,9},{9,1},{17,25},{25,17},{2,10},{10... | collective-permute-start | bytes 393224 | tf_op jit(solution)/shard_map/ppermute | solution.py:311
  6.3 2.6 %copy-start = (bf16[16,2,8,2,5376]{4,3,2,1,0:T(2,128)(2,1)S(1)}, bf16[16,2,8,2,5376]{4,3,2,1,0:T(2,128)(2,1)}, u32[]{:S(2)}) copy-start(bf16[16,2,8,2,5376]{4,3,2,1,0:T(2,128)(2,1)} %param.6) | copy-start | bytes 16515076
  8.8 0.9 copy-start.1
  9.8 0.7 copy-start.3
  13.0 23.7 %collective-permute-start.26 = (bf16[2,16,5120]{2,1,0:T(8,128)(2,1)S(1)}, bf16[2,16,5120]{2,1,0:T(8,128)(2,1)S(1)}, u32[]{:S(2)}, u32[]{:S(2)}) collective-permute-start(bf16[2,16,5120]{2,1,0:T(8,128)(2,1)S(1)} %get-tuple-element.31), channel_id=1, source_target_pairs={{0,6},{1,7},{2,4},{3,5},{4,2},{5,3},{6,0},{7,1},{8,14},{9,15},{10,... | collective-permute-start | bytes 983048 | tf_op jit(solution)/shard_map/ppermute | solution.py:311
  16.7 34.0 %collective-permute-start.30 = (bf16[2,16,5120]{2,1,0:T(8,128)(2,1)S(1)}, bf16[2,16,5120]{2,1,0:T(8,128)(2,1)S(1)}, u32[]{:S(2)}, u32[]{:S(2)}) collective-permute-start(bf16[2,16,5120]{2,1,0:T(8,128)(2,1)S(1)} %get-tuple-element.32), channel_id=1, source_target_pairs={{0,7},{1,6},{2,5},{3,4},{4,3},{5,2},{6,1},{7,0},{8,15},{9,14},{10,... | collective-permute-start | bytes 983048 | tf_op jit(solution)/shard_map/ppermute | solution.py:311
  19.3 47.2 %collective-permute-start.18 = (bf16[2,16,5120]{2,1,0:T(8,128)(2,1)S(1)}, bf16[2,16,5120]{2,1,0:T(8,128)(2,1)S(1)}, u32[]{:S(2)}, u32[]{:S(2)}) collective-permute-start(bf16[2,16,5120]{2,1,0:T(8,128)(2,1)S(1)} %get-tuple-element.29), channel_id=1, source_target_pairs={{0,4},{1,5},{2,6},{3,7},{4,0},{5,1},{6,2},{7,3},{8,12},{9,13},{10,... | collective-permute-start | bytes 983048 | tf_op jit(solution)/shard_map/ppermute | solution.py:311
  19.3 52.2 %collective-permute-start.22 = (bf16[2,16,5120]{2,1,0:T(8,128)(2,1)S(1)}, bf16[2,16,5120]{2,1,0:T(8,128)(2,1)S(1)}, u32[]{:S(2)}, u32[]{:S(2)}) collective-permute-start(bf16[2,16,5120]{2,1,0:T(8,128)(2,1)S(1)} %get-tuple-element.30), channel_id=1, source_target_pairs={{0,5},{1,4},{2,7},{3,6},{4,1},{5,0},{6,3},{7,2},{8,13},{9,12},{10,... | collective-permute-start | bytes 983048 | tf_op jit(solution)/shard_map/ppermute | solution.py:311
  21.9 5.9 %collective-permute-start.1 = (bf16[2,8,16,256]{3,2,1,0:T(8,128)(2,1)S(1)}, bf16[2,8,16,256]{3,2,1,0:T(8,128)(2,1)S(1)}, u32[]{:S(2)}, u32[]{:S(2)}) collective-permute-start(bf16[2,8,16,256]{3,2,1,0:T(8,128)(2,1)S(1)} %get-tuple-element.21), channel_id=1, source_target_pairs={{0,16},{8,24},{16,0},{24,8},{1,17},{9,25},{17,1},{25,9},{2,18},{10... | collective-permute-start | bytes 393224 | tf_op jit(solution)/shard_map/ppermute | solution.py:311
  27.8 7.7 %collective-permute-start.2 = (bf16[2,8,16,256]{3,2,1,0:T(8,128)(2,1)S(1)}, bf16[2,8,16,256]{3,2,1,0:T(8,128)(2,1)S(1)}, u32[]{:S(2)}, u32[]{:S(2)}) collective-permute-start(bf16[2,8,16,256]{3,2,1,0:T(8,128)(2,1)S(1)} %get-tuple-element.22), channel_id=1, source_target_pairs={{0,24},{8,16},{16,8},{24,0},{1,25},{9,17},{17,9},{25,1},{2,26},{10... | collective-permute-start | bytes 393224 | tf_op jit(solution)/shard_map/ppermute | solution.py:311
  35.5 36.7 %collective-permute-start.10 = (bf16[2,16,5120]{2,1,0:T(8,128)(2,1)S(1)}, bf16[2,16,5120]{2,1,0:T(8,128)(2,1)S(1)}, u32[]{:S(2)}, u32[]{:S(2)}) collective-permute-start(bf16[2,16,5120]{2,1,0:T(8,128)(2,1)S(1)} %get-tuple-element.27), channel_id=1, source_target_pairs={{0,2},{1,3},{2,0},{3,1},{4,6},{5,7},{6,4},{7,5},{8,10},{9,11},{10,... | collective-permute-start | bytes 983048 | tf_op jit(solution)/shard_map/ppermute | solution.py:311
  36.7 36.9 %collective-permute-start.14 = (bf16[2,16,5120]{2,1,0:T(8,128)(2,1)S(1)}, bf16[2,16,5120]{2,1,0:T(8,128)(2,1)S(1)}, u32[]{:S(2)}, u32[]{:S(2)}) collective-permute-start(bf16[2,16,5120]{2,1,0:T(8,128)(2,1)S(1)} %get-tuple-element.28), channel_id=1, source_target_pairs={{0,3},{1,2},{2,1},{3,0},{4,7},{5,6},{6,5},{7,4},{8,11},{9,10},{10,... | collective-permute-start | bytes 983048 | tf_op jit(solution)/shard_map/ppermute | solution.py:311
  50.7 24.4 %collective-permute-start.6 = (bf16[2,16,5120]{2,1,0:T(8,128)(2,1)S(1)}, bf16[2,16,5120]{2,1,0:T(8,128)(2,1)S(1)}, u32[]{:S(2)}, u32[]{:S(2)}) collective-permute-start(bf16[2,16,5120]{2,1,0:T(8,128)(2,1)S(1)} %get-tuple-element.26), channel_id=1, source_target_pairs={{0,1},{1,0},{2,3},{3,2},{4,5},{5,4},{6,7},{7,6},{8,9},{9,8},{10,11... | collective-permute-start | bytes 983048 | tf_op jit(solution)/shard_map/ppermute | solution.py:311
  66.5 9.2 %collective-permute-start.4 = (bf16[2,16,5120]{2,1,0:T(8,128)(2,1)S(1)}, bf16[2,16,5120]{2,1,0:T(8,128)(2,1)S(1)}, u32[]{:S(2)}, u32[]{:S(2)}) collective-permute-start(bf16[2,16,5120]{2,1,0:T(8,128)(2,1)S(1)} %get-tuple-element.25.refs_0_), channel_id=1, source_target_pairs={{0,16},{8,24},{16,0},{24,8},{1,17},{9,25},{17,1},{25,9},{2,18},{10... | collective-permute-start | bytes 983048 | tf_op jit(solution)/shard_map/ppermute | solution.py:311
  71.6 10.6 %collective-permute-start.3 = (bf16[2,16,5120]{2,1,0:T(8,128)(2,1)S(1)}, bf16[2,16,5120]{2,1,0:T(8,128)(2,1)S(1)}, u32[]{:S(2)}, u32[]{:S(2)}) collective-permute-start(bf16[2,16,5120]{2,1,0:T(8,128)(2,1)S(1)} %get-tuple-element.25.refs_0_), channel_id=1, source_target_pairs={{0,8},{8,0},{16,24},{24,16},{1,9},{9,1},{17,25},{25,17},{2,10},{10... | collective-permute-start | bytes 983048 | tf_op jit(solution)/shard_map/ppermute | solution.py:311
  72.1 10.6 %collective-permute-start.28 = (bf16[2,16,5120]{2,1,0:T(8,128)(2,1)S(1)}, bf16[2,16,5120]{2,1,0:T(8,128)(2,1)S(1)}, u32[]{:S(2)}, u32[]{:S(2)}) collective-permute-start(bf16[2,16,5120]{2,1,0:T(8,128)(2,1)S(1)} %collective-permute-done.26.refs_0_), channel_id=1, source_target_pairs={{0,16},{8,24},{16,0},{24,8},{1,17},{9,25},{17,1},{25,9},{2,18},{10... | collective-permute-start | bytes 983048 | tf_op jit(solution)/shard_map/ppermute | solution.py:311
  73.6 15.5 %collective-permute-start.27 = (bf16[2,16,5120]{2,1,0:T(8,128)(2,1)S(1)}, bf16[2,16,5120]{2,1,0:T(8,128)(2,1)S(1)}, u32[]{:S(2)}, u32[]{:S(2)}) collective-permute-start(bf16[2,16,5120]{2,1,0:T(8,128)(2,1)S(1)} %collective-permute-done.26.refs_0_), channel_id=1, source_target_pairs={{0,8},{8,0},{16,24},{24,16},{1,9},{9,1},{17,25},{25,17},{2,10},{10... | collective-permute-start | bytes 983048 | tf_op jit(solution)/shard_map/ppermute | solution.py:311
  75.1 15.6 %collective-permute-start.31 = (bf16[2,16,5120]{2,1,0:T(8,128)(2,1)S(1)}, bf16[2,16,5120]{2,1,0:T(8,128)(2,1)S(1)}, u32[]{:S(2)}, u32[]{:S(2)}) collective-permute-start(bf16[2,16,5120]{2,1,0:T(8,128)(2,1)S(1)} %collective-permute-done.30.refs_4_), channel_id=1, source_target_pairs={{0,16},{8,24},{16,0},{24,8},{1,17},{9,25},{17,1},{25,9},{2,18},{10... | collective-permute-start | bytes 983048 | tf_op jit(solution)/shard_map/ppermute | solution.py:311
  75.7 21.1 %collective-permute-start.20 = (bf16[2,16,5120]{2,1,0:T(8,128)(2,1)S(1)}, bf16[2,16,5120]{2,1,0:T(8,128)(2,1)S(1)}, u32[]{:S(2)}, u32[]{:S(2)}) collective-permute-start(bf16[2,16,5120]{2,1,0:T(8,128)(2,1)S(1)} %collective-permute-done.18.refs_16_), channel_id=1, source_target_pairs={{0,16},{8,24},{16,0},{24,8},{1,17},{9,25},{17,1},{25,9},{2,18},{10... | collective-permute-start | bytes 983048 | tf_op jit(solution)/shard_map/ppermute | solution.py:311
  82.2 16.1 %collective-permute-start.19 = (bf16[2,16,5120]{2,1,0:T(8,128)(2,1)S(1)}, bf16[2,16,5120]{2,1,0:T(8,128)(2,1)S(1)}, u32[]{:S(2)}, u32[]{:S(2)}) collective-permute-start(bf16[2,16,5120]{2,1,0:T(8,128)(2,1)S(1)} %collective-permute-done.18.refs_16_), channel_id=1, source_target_pairs={{0,8},{8,0},{16,24},{24,16},{1,9},{9,1},{17,25},{25,17},{2,10},{10... | collective-permute-start | bytes 983048 | tf_op jit(solution)/shard_map/ppermute | solution.py:311
  82.7 20.5 %collective-permute-start.24 = (bf16[2,16,5120]{2,1,0:T(8,128)(2,1)S(1)}, bf16[2,16,5120]{2,1,0:T(8,128)(2,1)S(1)}, u32[]{:S(2)}, u32[]{:S(2)}) collective-permute-start(bf16[2,16,5120]{2,1,0:T(8,128)(2,1)S(1)} %collective-permute-done.22.refs_20_), channel_id=1, source_target_pairs={{0,8},{8,0},{16,24},{24,16},{1,9},{9,1},{17,25},{25,17},{2,10},{10... | collective-permute-start | bytes 983048 | tf_op jit(solution)/shard_map/ppermute | solution.py:311
  89.2 15.6 %collective-permute-start.23 = (bf16[2,16,5120]{2,1,0:T(8,128)(2,1)S(1)}, bf16[2,16,5120]{2,1,0:T(8,128)(2,1)S(1)}, u32[]{:S(2)}, u32[]{:S(2)}) collective-permute-start(bf16[2,16,5120]{2,1,0:T(8,128)(2,1)S(1)} %collective-permute-done.22.refs_20_), channel_id=1, source_target_pairs={{0,16},{8,24},{16,0},{24,8},{1,17},{9,25},{17,1},{25,9},{2,18},{10... | collective-permute-start | bytes 983048 | tf_op jit(solution)/shard_map/ppermute | solution.py:311
  90.7 20.1 %collective-permute-start.12 = (bf16[2,16,5120]{2,1,0:T(8,128)(2,1)S(1)}, bf16[2,16,5120]{2,1,0:T(8,128)(2,1)S(1)}, u32[]{:S(2)}, u32[]{:S(2)}) collective-permute-start(bf16[2,16,5120]{2,1,0:T(8,128)(2,1)S(1)} %collective-permute-done.10.refs_8_), channel_id=1, source_target_pairs={{0,16},{8,24},{16,0},{24,8},{1,17},{9,25},{17,1},{25,9},{2,18},{10... | collective-permute-start | bytes 983048 | tf_op jit(solution)/shard_map/ppermute | solution.py:311
  96.8 15.6 %collective-permute-start.11 = (bf16[2,16,5120]{2,1,0:T(8,128)(2,1)S(1)}, bf16[2,16,5120]{2,1,0:T(8,128)(2,1)S(1)}, u32[]{:S(2)}, u32[]{:S(2)}) collective-permute-start(bf16[2,16,5120]{2,1,0:T(8,128)(2,1)S(1)} %collective-permute-done.10.refs_8_), channel_id=1, source_target_pairs={{0,8},{8,0},{16,24},{24,16},{1,9},{9,1},{17,25},{25,17},{2,10},{10... | collective-permute-start | bytes 983048 | tf_op jit(solution)/shard_map/ppermute | solution.py:311
  98.2 19.0 %collective-permute-start.16 = (bf16[2,16,5120]{2,1,0:T(8,128)(2,1)S(1)}, bf16[2,16,5120]{2,1,0:T(8,128)(2,1)S(1)}, u32[]{:S(2)}, u32[]{:S(2)}) collective-permute-start(bf16[2,16,5120]{2,1,0:T(8,128)(2,1)S(1)} %collective-permute-done.14.refs_12_), channel_id=1, source_target_pairs={{0,8},{8,0},{16,24},{24,16},{1,9},{9,1},{17,25},{25,17},{2,10},{10... | collective-permute-start | bytes 983048 | tf_op jit(solution)/shard_map/ppermute | solution.py:311
  103.2 15.6 %collective-permute-start.15 = (bf16[2,16,5120]{2,1,0:T(8,128)(2,1)S(1)}, bf16[2,16,5120]{2,1,0:T(8,128)(2,1)S(1)}, u32[]{:S(2)}, u32[]{:S(2)}) collective-permute-start(bf16[2,16,5120]{2,1,0:T(8,128)(2,1)S(1)} %collective-permute-done.14.refs_12_), channel_id=1, source_target_pairs={{0,16},{8,24},{16,0},{24,8},{1,17},{9,25},{17,1},{25,9},{2,18},{10... | collective-permute-start | bytes 983048 | tf_op jit(solution)/shard_map/ppermute | solution.py:311
  104.8 19.5 %collective-permute-start.8 = (bf16[2,16,5120]{2,1,0:T(8,128)(2,1)S(1)}, bf16[2,16,5120]{2,1,0:T(8,128)(2,1)S(1)}, u32[]{:S(2)}, u32[]{:S(2)}) collective-permute-start(bf16[2,16,5120]{2,1,0:T(8,128)(2,1)S(1)} %collective-permute-done.6.refs_4_), channel_id=1, source_target_pairs={{0,8},{8,0},{16,24},{24,16},{1,9},{9,1},{17,25},{25,17},{2,10},{10... | collective-permute-start | bytes 983048 | tf_op jit(solution)/shard_map/ppermute | solution.py:311
  110.8 14.0 %collective-permute-start.7 = (bf16[2,16,5120]{2,1,0:T(8,128)(2,1)S(1)}, bf16[2,16,5120]{2,1,0:T(8,128)(2,1)S(1)}, u32[]{:S(2)}, u32[]{:S(2)}) collective-permute-start(bf16[2,16,5120]{2,1,0:T(8,128)(2,1)S(1)} %collective-permute-done.6.refs_4_), channel_id=1, source_target_pairs={{0,16},{8,24},{16,0},{24,8},{1,17},{9,25},{17,1},{25,9},{2,18},{10... | collective-permute-start | bytes 983048 | tf_op jit(solution)/shard_map/ppermute | solution.py:311
  112.3 19.5 %collective-permute-start.5 = (bf16[2,16,5120]{2,1,0:T(8,128)(2,1)S(1)}, bf16[2,16,5120]{2,1,0:T(8,128)(2,1)S(1)}, u32[]{:S(2)}, u32[]{:S(2)}) collective-permute-start(bf16[2,16,5120]{2,1,0:T(8,128)(2,1)S(1)} %collective-permute-done.3.refs_1_), channel_id=1, source_target_pairs={{0,16},{8,24},{16,0},{24,8},{1,17},{9,25},{17,1},{25,9},{2,18},{10... | collective-permute-start | bytes 983048 | tf_op jit(solution)/shard_map/ppermute | solution.py:311
  117.3 21.6 %collective-permute-start.21 = (bf16[2,16,5120]{2,1,0:T(8,128)(2,1)S(1)}, bf16[2,16,5120]{2,1,0:T(8,128)(2,1)S(1)}, u32[]{:S(2)}, u32[]{:S(2)}) collective-permute-start(bf16[2,16,5120]{2,1,0:T(8,128)(2,1)S(1)} %collective-permute-done.19.refs_17_), channel_id=1, source_target_pairs={{0,16},{8,24},{16,0},{24,8},{1,17},{9,25},{17,1},{25,9},{2,18},{10... | collective-permute-start | bytes 983048 | tf_op jit(solution)/shard_map/ppermute | solution.py:311
  118.8 41.0 %collective-permute-start.32 = (bf16[2,16,5120]{2,1,0:T(8,128)(2,1)S(1)}, bf16[2,16,5120]{2,1,0:T(8,128)(2,1)S(1)}, u32[]{:S(2)}, u32[]{:S(2)}) collective-permute-start(bf16[2,16,5120]{2,1,0:T(8,128)(2,1)S(1)} %collective-permute-done.30.refs_4_), channel_id=1, source_target_pairs={{0,8},{8,0},{16,24},{24,16},{1,9},{9,1},{17,25},{25,17},{2,10},{10... | collective-permute-start | bytes 983048 | tf_op jit(solution)/shard_map/ppermute | solution.py:311
  124.3 16.1 %collective-permute-start.25 = (bf16[2,16,5120]{2,1,0:T(8,128)(2,1)S(1)}, bf16[2,16,5120]{2,1,0:T(8,128)(2,1)S(1)}, u32[]{:S(2)}, u32[]{:S(2)}) collective-permute-start(bf16[2,16,5120]{2,1,0:T(8,128)(2,1)S(1)} %collective-permute-done.23.refs_21_), channel_id=1, source_target_pairs={{0,8},{8,0},{16,24},{24,16},{1,9},{9,1},{17,25},{25,17},{2,10},{10... | collective-permute-start | bytes 983048 | tf_op jit(solution)/shard_map/ppermute | solution.py:311
  124.8 21.1 %collective-permute-start.13 = (bf16[2,16,5120]{2,1,0:T(8,128)(2,1)S(1)}, bf16[2,16,5120]{2,1,0:T(8,128)(2,1)S(1)}, u32[]{:S(2)}, u32[]{:S(2)}) collective-permute-start(bf16[2,16,5120]{2,1,0:T(8,128)(2,1)S(1)} %collective-permute-done.11.refs_9_), channel_id=1, source_target_pairs={{0,16},{8,24},{16,0},{24,8},{1,17},{9,25},{17,1},{25,9},{2,18},{10... | collective-permute-start | bytes 983048 | tf_op jit(solution)/shard_map/ppermute | solution.py:311
  131.9 15.5 %collective-permute-start.17 = (bf16[2,16,5120]{2,1,0:T(8,128)(2,1)S(1)}, bf16[2,16,5120]{2,1,0:T(8,128)(2,1)S(1)}, u32[]{:S(2)}, u32[]{:S(2)}) collective-permute-start(bf16[2,16,5120]{2,1,0:T(8,128)(2,1)S(1)} %collective-permute-done.15.refs_13_), channel_id=1, source_target_pairs={{0,8},{8,0},{16,24},{24,16},{1,9},{9,1},{17,25},{25,17},{2,10},{10... | collective-permute-start | bytes 983048 | tf_op jit(solution)/shard_map/ppermute | solution.py:311
  138.9 13.5 %collective-permute-start.9 = (bf16[2,16,5120]{2,1,0:T(8,128)(2,1)S(1)}, bf16[2,16,5120]{2,1,0:T(8,128)(2,1)S(1)}, u32[]{:S(2)}, u32[]{:S(2)}) collective-permute-start(bf16[2,16,5120]{2,1,0:T(8,128)(2,1)S(1)} %collective-permute-done.7.refs_5_), channel_id=1, source_target_pairs={{0,8},{8,0},{16,24},{24,16},{1,9},{9,1},{17,25},{25,17},{2,10},{10... | collective-permute-start | bytes 983048 | tf_op jit(solution)/shard_map/ppermute | solution.py:311
  140.4 19.4 %collective-permute-start.34 = (bf16[2,16,2560]{2,1,0:T(8,128)(2,1)S(1)}, bf16[2,16,2560]{2,1,0:T(8,128)(2,1)S(1)}, u32[]{:S(2)}, u32[]{:S(2)}) collective-permute-start(bf16[2,16,2560]{2,1,0:T(8,128)(2,1)S(1)} %get-tuple-element.35), channel_id=1, source_target_pairs={{0,16},{8,24},{16,0},{24,8},{1,17},{9,25},{17,1},{25,9},{2,18},{10... | collective-permute-start | bytes 491528 | tf_op jit(solution)/shard_map/ppermute | solution.py:311
  145.9 13.9 %collective-permute-start.35 = (bf16[2,16,2560]{2,1,0:T(8,128)(2,1)S(1)}, bf16[2,16,2560]{2,1,0:T(8,128)(2,1)S(1)}, u32[]{:S(2)}, u32[]{:S(2)}) collective-permute-start(bf16[2,16,2560]{2,1,0:T(8,128)(2,1)S(1)} %get-tuple-element.33), channel_id=1, source_target_pairs={{0,8},{8,0},{16,24},{24,16},{1,9},{9,1},{17,25},{25,17},{2,10},{10... | collective-permute-start | bytes 491528 | tf_op jit(solution)/shard_map/ppermute | solution.py:311
  147.4 15.0 %collective-permute-start.29 = (bf16[2,16,2560]{2,1,0:T(8,128)(2,1)S(1)}, bf16[2,16,2560]{2,1,0:T(8,128)(2,1)S(1)}, u32[]{:S(2)}, u32[]{:S(2)}) collective-permute-start(bf16[2,16,2560]{2,1,0:T(8,128)(2,1)S(1)} %get-tuple-element.36), channel_id=1, source_target_pairs={{0,16},{8,24},{16,0},{24,8},{1,17},{9,25},{17,1},{25,9},{2,18},{10... | collective-permute-start | bytes 491528 | tf_op jit(solution)/shard_map/ppermute | solution.py:311
  152.4 10.0 %collective-permute-start.33 = (bf16[2,16,2560]{2,1,0:T(8,128)(2,1)S(1)}, bf16[2,16,2560]{2,1,0:T(8,128)(2,1)S(1)}, u32[]{:S(2)}, u32[]{:S(2)}) collective-permute-start(bf16[2,16,2560]{2,1,0:T(8,128)(2,1)S(1)} %get-tuple-element.34), channel_id=1, source_target_pairs={{0,8},{8,0},{16,24},{24,16},{1,9},{9,1},{17,25},{25,17},{2,10},{10... | collective-permute-start | bytes 491528 | tf_op jit(solution)/shard_map/ppermute | solution.py:311
